TPU v7x, 32 devices: a whole 2x2x4 slice. The times are simulated.
32 devices in a mesh: wide: 16 (over z, y, x), band: 2 (over core).
Axes of the slice: x: 2, y: 2, z: 4, core: 2. Of those that a mesh axis runs over, the one named last changes fastest.
Arguments:
- prior_states: bfloat16 [256, 2, 64, 8, 128], P('wide', 'band'), may hold values from -6 to 6
- measured_anomalies: bfloat16 [2, 64, 256, 128], P('band', 'wide'), may hold values from -6 to 6
- departures: bfloat16 [2, 64, 128], P('band', 'wide'), may hold values from -15 to 15
- error_precisions: bfloat16 [2, 64, 128], P('band', 'wide'), may hold values from 0.25 to 4
- datum_totals: int32 [2, 64], P('band', 'wide'), may hold values from 64 to 128, as said below
- datum_patch_owner: int32 [2, 64, 128], P('band', 'wide'), may hold values from 0 to 3
- patch_group_lookup: int32 [2, 64, 4], P('band', 'wide'), may hold values from 0 to 11, as said below
Outputs:
- analysis: bfloat16 [256, 2, 64, 8, 128], P('wide', 'band')
Inputs may be any that keep to these rules, and one draw needn't show every extreme that they name: The observations of a block fill its first datum_totals slots; in every band some block is full (128). `patch_group_lookup`: entry 0 of every list lies below 4 (a block of the band below), entry 1 at 8 or above (a block of the band above), and the other entries are distinct blocks of the tile's own band, from 4 to 7.
All inputs are finite; a program needn't handle non-finite values.
Results may differ from a plain program's by a relative error of at most 0.0062.
Values may be sent and summed in bfloat16 or wider, within the bound.
No kernel may reach another device: no remote copies, remote signals or barrier semaphores. Data moves between devices by JAX's collectives and lax.ppermute only.
A program may use at most 64 MiB of HBM per device.

v0:
```python
import jax
import jax.numpy as jnp
from jax import lax
from jax.sharding import PartitionSpec as P

NS_ITERS = 6


LOC_FAR = 0.5
HIGH = lax.Precision.HIGHEST


def extended(x, sides, width):
    for axis, dim in sides:
        peers, length = (lax.axis_size(axis), x.shape[dim])
        up = [(i, (i + 1) % peers) for i in range(peers - 1)]
        down = [(j, i) for i, j in up]
        last = lax.slice_in_dim(x, length - width, length, axis=dim)
        first = lax.slice_in_dim(x, 0, width, axis=dim)
        before = lax.ppermute(last, axis, up)
        after = lax.ppermute(first, axis, down)
        x = jnp.concatenate([before, x, after], axis=dim)
    return x


def on_device(
    prior_states,
    measured_anomalies,
    departures,
    error_precisions,
    datum_totals,
    datum_patch_owner,
    patch_group_lookup,
):
    sample_states = measured_anomalies.shape[2]
    blocks_here = measured_anomalies.shape[1]
    slots = measured_anomalies.shape[3]
    tiles_here = patch_group_lookup.shape[1]
    slot_index = jnp.arange(slots, dtype=jnp.int32)
    live = jnp.where(slot_index[None, :] < datum_totals[0][:, None], 1.0, 0.0)
    base = error_precisions[0].astype(jnp.float32) * live
    tile_ids = jnp.arange(tiles_here, dtype=jnp.int32)
    near = jnp.where(datum_patch_owner[0][:, None, :] == tile_ids[None, :, None], 1.0, LOC_FAR)
    weight_rows = (base[:, None, :] * near).astype(jnp.bfloat16)
    packed = jnp.concatenate(
        [measured_anomalies[0], departures[0][:, None, :], weight_rows], axis=1
    )
    own_lists = patch_group_lookup[0]
    beside_all = extended(packed[None], (("band", 0),), 1)
    beside_all = beside_all.reshape(3 * blocks_here, sample_states + 1 + tiles_here, slots)
    tile_obs = beside_all[own_lists]
    pert = tile_obs[:, :, :sample_states, :]
    innov = tile_obs[:, :, sample_states, :]
    weights = jnp.stack(
        [tile_obs[index, :, sample_states + 1 + index, :] for index in range(tiles_here)]
    )
    scaled = (pert.astype(jnp.float32) * weights.astype(jnp.float32)[:, :, None, :]).astype(
        jnp.bfloat16
    )
    identity = jnp.eye(sample_states, dtype=jnp.float32)
    precision_matrix = (sample_states - 1) * identity + jnp.einsum(
        "tnkb,tnjb->tkj", scaled, pert, preferred_element_type=jnp.float32
    )
    drive = jnp.einsum("tnkb,tnb->tk", scaled, innov, preferred_element_type=jnp.float32)
    norm_c = jnp.sqrt(jnp.sum(precision_matrix * precision_matrix, axis=(1, 2)))
    current = precision_matrix / norm_c[:, None, None]
    root_inv = jnp.broadcast_to(identity, current.shape)
    for sweep in range(NS_ITERS):
        factor = 1.5 * identity - 0.5 * jnp.einsum(
            "tij,tjk->tik", root_inv, current, precision=HIGH
        )
        current = jnp.einsum("tij,tjk->tik", current, factor, precision=HIGH)
        root_inv = jnp.einsum("tij,tjk->tik", factor, root_inv, precision=HIGH)
    inner = jnp.einsum("tij,tj->ti", root_inv, drive, precision=HIGH)
    gain_vec = jnp.einsum("tij,tj->ti", root_inv, inner, precision=HIGH) / norm_c[:, None]
    spread_scale = jnp.sqrt((sample_states - 1) / norm_c)
    mix = (spread_scale[:, None, None] * root_inv + gain_vec[:, :, None]).astype(jnp.bfloat16)
    gathered_records = lax.all_to_all(prior_states, "wide", split_axis=2, concat_axis=0, tiled=True)
    array_shape = gathered_records.shape
    flat = gathered_records.reshape(sample_states, tiles_here, -1)
    mean_field = jnp.sum(flat, axis=0, dtype=jnp.float32) / sample_states
    spread = (flat.astype(jnp.float32) - mean_field).astype(jnp.bfloat16)
    result = mean_field + jnp.einsum(
        "tjk,jtp->ktp", mix, spread, preferred_element_type=jnp.float32
    )
    return lax.all_to_all(
        result.astype(jnp.bfloat16).reshape(array_shape),
        "wide",
        split_axis=0,
        concat_axis=2,
        tiled=True,
    )


def solution(mesh):
    in_specs = (
        P("wide", "band", None, None, None),
        P("band", "wide", None, None),
        P("band", "wide", None),
        P("band", "wide", None),
        P("band", "wide"),
        P("band", "wide", None),
        P("band", "wide", None),
    )
    out_specs = P("wide", "band", None, None, None)
    return jax.shard_map(
        on_device, mesh=mesh, in_specs=in_specs, out_specs=out_specs, check_vma=False
    )
```

profile of v0, /device:TPU:0, one launch (start us, length us, event | category | flops | bytes accessed | tf_op | source)
XLA Modules:
  0.0 136.8 jit_solution(10624637453279660126)
XLA Ops:
  0.0 0.7 copy.48
  0.7 0.8 convert_multiply_fusion
  1.4 0.7 multiply_convert_fusion.7
  2.1 1.0 maximum_bitcast_fusion
  3.1 1.3 collective-permute-start.1
  4.4 3.8 %collective-permute-start = (bf16[1,4,261,128]{3,2,1,0:T(8,128)(2,1)S(1)}, bf16[1,4,261,128]{3,2,1,0:T(8,128)(2,1)}, u32[]{:S(2)}, u32[]{:S(2)}) collective-permute-start(bf16[1,4,261,128]{3,2,1,0:T(8,128)(2,1)S(1)} %maximum_bitcast_fusion), channel_id=1, source_target_pairs={{0,1},{2,3},{4,5},{6,7},{8,9},{10,11},{12,13},{14,15},{16,17},{18,... | collective-permute-start | bytes 801800 | tf_op jit(solution)/shard_map/ppermute | solution.py:20
  8.1 3.5 %copy.46 = bf16[16,1,64,8,128]{4,3,1,0,2:T(8,128)(2,1)} copy(bf16[16,1,64,8,128]{4,3,2,1,0:T(8,128)(2,1)} %param.7) | data formatting | bytes 4194304 | tf_op args[0]
  11.7 0.0 copy-start.4
  11.7 8.5 %all-to-all-start = ((bf16[16,1,64,8,128]{4,3,1,0,2:T(8,128)(2,1)}), bf16[16,1,64,8,128]{4,3,1,0,2:T(8,128)(2,1)S(1)}, u32[]{:S(2)}, u32[]{:S(2)}) async-start(bf16[16,1,64,8,128]{4,3,1,0,2:T(8,128)(2,1)} %copy.46), calls=%async_computation | async-start | bytes 4194304 | tf_op jit(solution)/shard_map/all_to_all | solution.py:78
  20.2 0.0 copy-done.4
  20.2 0.1 reshape.143
  20.3 0.7 fusion.20
  21.0 0.7 fusion.22
  21.7 0.0 collective-permute-done.1
  21.7 0.0 copy-start.2
  21.7 0.7 copy-done.2
  22.4 0.0 collective-permute-done
  22.4 1.1 pad_maximum_fusion
  23.5 0.0 copy-start.3
  23.6 1.7 %gather_fusion = bf16[16,261,128]{2,1,0:T(8,128)(2,1)} fusion(bf16[12,261,128]{2,1,0:T(8,128)(2,1)S(1)} %bitcast.100, s32[1024]{0:T(1024)S(1)} %pad_clamp_fusion), kind=kCustom, calls=%fused_computation | custom fusion | bytes 2138176 | tf_op jit(solution)/shard_map/gather | solution.py:51
  25.2 0.8 fusion.28
  26.0 0.0 copy-done.3
  26.0 0.0 copy-start.1
  26.0 2.2 %multiply_reduce_fusion = (f32[4]{0:T(128)S(1)}, f32[4,256,256]{2,1,0:T(8,128)S(1)}) fusion(bf16[4,4,261,128]{3,2,1,0:T(8,128)(2,1)} %bitcast.102, f32[4,4,128]{2,1,0:T(4,128)S(1)} %maximum_convert_fusion, f32[256,256]{1,0:T(8,128)S(1)} %copy-done.3), kind=kOutput, calls=%fused_computation.23 | convolution fusion | flops 270794752 | bytes 3416080 | tf_op jit(solution)/shard_map/tnkb,tnjb->tkj/dot_general | solution.py:61
  28.2 0.0 copy-done.1
  28.2 1.1 fusion.9
  29.4 1.2 fusion.23
  30.6 1.1 fusion.16
  31.7 1.2 fusion.8
  32.9 1.1 fusion.30
  34.1 1.1 fusion.29
  35.2 0.0 copy-start
  35.2 1.2 fusion.7
  36.4 0.0 copy-done
  36.4 0.4 fusion.1
  36.8 1.2 fusion.32
  38.0 1.1 fusion.31
  39.2 1.4 fusion.6
  40.5 1.1 fusion.34
  41.7 1.1 fusion.33
  42.8 1.2 fusion.5
  44.0 1.1 fusion.35
  45.2 1.1 fusion.36
  46.3 1.2 fusion.4
  47.5 1.1 fusion.37
  48.7 1.0 fusion.26
  49.7 1.0 fusion.24
  50.7 0.1 bitcast_divide_fusion
  50.7 11.6 %all-to-all-done = bf16[16,1,64,8,128]{4,3,1,0,2:T(8,128)(2,1)S(1)} async-done(((bf16[16,1,64,8,128]{4,3,1,0,2:T(8,128)(2,1)}), bf16[16,1,64,8,128]{4,3,1,0,2:T(8,128)(2,1)S(1)}, u32[]{:S(2)}, u32[]{:S(2)}) %all-to-all-start) | async-done | bytes 2097184 | tf_op jit(solution)/shard_map/all_to_all | solution.py:78
  62.3 0.4 convert_reduce_fusion
  62.8 2.5 %copy_bitcast_fusion = f32[16,16,1,4,8,128]{5,4,1,0,3,2:T(8,128)} fusion(bf16[16,1,16,4,8,128]{5,4,0,3,2,1:T(8,128)(2,1)S(1)} %bitcast.97), kind=kLoop, calls=%fused_computation.1 | loop fusion | flops 1048576 | bytes 6291456 | tf_op jit(solution)/shard_map/convert_element_type | solution.py:81
  65.3 4.9 %reshape.138 = f32[256,4,1024]{2,0,1:T(8,128)} reshape(f32[16,16,1,4,8,128]{5,4,1,0,3,2:T(8,128)} %copy_bitcast_fusion) | data formatting | bytes 8388608 | tf_op jit(solution)/shard_map/convert_element_type | solution.py:81
  70.2 3.7 %add_convert_fusion = bf16[4,1024,256]{2,1,0:T(8,128)(2,1)S(1)} fusion(f32[256,4,1024]{2,0,1:T(8,128)} %reshape.138, f32[4,1024]{1,0:T(4,128)S(1)} %bitcast.106, f32[4,256,256]{2,1,0:T(8,128)S(1)} %fusion.37, f32[4,256]{1,0:T(4,128)S(1)} %bitcast_divide_fusion, f32[4]{0:T(128)S(1)} %get-tuple-element.9), kind=kOutput, calls=%fused_computation.2 | convolution fusion | flops 541851648 | bytes 7360528 | tf_op jit(solution)/shard_map/tjk,jtp->ktp/dot_general | solution.py:83
  73.9 3.1 %copy.50 = bf16[256,1,4,8,128]{4,3,2,1,0:T(8,128)(2,1)} copy(bf16[256,1,4,8,128]{0,4,3,2,1:T(8,128)(2,1)S(1)} %bitcast.98) | data formatting | bytes 4194304 | tf_op jit(solution)/shard_map/reshape | solution.py:87
  76.9 58.0 %all_to_all.27 = bf16[256,1,4,8,128]{4,3,2,1,0:T(8,128)(2,1)S(1)} all-to-all(bf16[256,1,4,8,128]{4,3,2,1,0:T(8,128)(2,1)} %copy.50), channel_id=1, replica_groups=mesh['wide'=16,'band'=2] {'wide'}, dimensions={0} | all-to-all | bytes 4194304 | tf_op jit(solution)/shard_map/all_to_all | solution.py:86
  135.0 1.9 %copy.51 = bf16[16,1,16,4,8,128]{5,4,3,2,0,1:T(8,128)(2,1)} copy(bf16[16,1,16,4,8,128]{5,4,3,0,2,1:T(8,128)(2,1)S(1)} %bitcast.99) | data formatting | bytes 4194304 | tf_op jit(solution)/shard_map/all_to_all | solution.py:86
  (12 shorter events, 0.1 us)
Async XLA Ops:
  3.1 18.6 %collective-permute-start.1 = (bf16[1,4,261,128]{3,2,1,0:T(8,128)(2,1)S(1)}, bf16[1,4,261,128]{3,2,1,0:T(8,128)(2,1)S(1)}, u32[]{:S(2)}, u32[]{:S(2)}) collective-permute-start(bf16[1,4,261,128]{3,2,1,0:T(8,128)(2,1)S(1)} %maximum_bitcast_fusion), channel_id=1, source_target_pairs={{1,0},{3,2},{5,4},{7,6},{9,8},{11,10},{13,12},{15,14},{17,16},{19,... | collective-permute-start | bytes 801800 | tf_op jit(solution)/shard_map/ppermute | solution.py:21
  4.4 18.0 %collective-permute-start = (bf16[1,4,261,128]{3,2,1,0:T(8,128)(2,1)S(1)}, bf16[1,4,261,128]{3,2,1,0:T(8,128)(2,1)}, u32[]{:S(2)}, u32[]{:S(2)}) collective-permute-start(bf16[1,4,261,128]{3,2,1,0:T(8,128)(2,1)S(1)} %maximum_bitcast_fusion), channel_id=1, source_target_pairs={{0,1},{2,3},{4,5},{6,7},{8,9},{10,11},{12,13},{14,15},{16,17},{18,... | collective-permute-start | bytes 801800 | tf_op jit(solution)/shard_map/ppermute | solution.py:20
  11.7 8.5 %copy-start.4 = (s32[1,4,4]{2,1,0:T(4,128)S(1)}, s32[1,4,4]{2,1,0:T(4,128)}, u32[]{:S(2)}) copy-start(s32[1,4,4]{2,1,0:T(4,128)} %param.13) | copy-start | bytes 196
  11.7 50.6 %all-to-all-start = ((bf16[16,1,64,8,128]{4,3,1,0,2:T(8,128)(2,1)}), bf16[16,1,64,8,128]{4,3,1,0,2:T(8,128)(2,1)S(1)}, u32[]{:S(2)}, u32[]{:S(2)}) async-start(bf16[16,1,64,8,128]{4,3,1,0,2:T(8,128)(2,1)} %copy.46), calls=%async_computation | async-start | bytes 4194304 | tf_op jit(solution)/shard_map/all_to_all | solution.py:78
  21.7 0.7 copy-start.2
  23.5 2.5 %copy-start.3 = (f32[256,256]{1,0:T(8,128)S(1)}, f32[256,256]{1,0:T(8,128)}, u32[]{:S(2)}) copy-start(f32[256,256]{1,0:T(8,128)} %fusion.22) | copy-start | bytes 786436
  26.0 2.2 %copy-start.1 = (f32[256,256]{1,0:T(8,128)S(1)}, f32[256,256]{1,0:T(8,128)}, u32[]{:S(2)}) copy-start(f32[256,256]{1,0:T(8,128)} %fusion.20) | copy-start | bytes 786436
  35.2 1.2 copy-start
where the time goes:
time: 137 us
  blocking collectives  58 us (42%)
  matrix products  28.1 us (21%)
  local copies, waits for them, and re-layouts  17.3 us (13%)
  starting transfers between devices  13.5 us (10%)
  waiting for transfers between devices  11.6 us (8%)
  other arithmetic  8.02 us (6%)
    all_to_all x1, blocking collectives, on_device(): lax.all_to_all(result.astype(jnp.bfloat16).reshape(array_shape), 'wide',...  58 us
    all_to_all x1, waiting for transfers between devices, on_device(): lax.all_to_all(prior_states, 'wide', split_axis=2, concat_axis=0, tiled=T...  11.6 us
    all_to_all x1, starting transfers between devices, on_device(): lax.all_to_all(prior_states, 'wide', split_axis=2, concat_axis=0, tiled=T...  8.47 us
    dot_general x6, matrix products, on_device(): jnp.einsum('tij,tjk->tik', root_inv, current, precision=HIGH)  7.25 us
    dot_general x6, matrix products, on_device(): root_inv = jnp.einsum('tij,tjk->tik', factor, root_inv, precision=HIGH)  6.83 us
    dot_general x5, matrix products, on_device(): current = jnp.einsum('tij,tjk->tik', current, factor, precision=HIGH)  5.81 us
    convert_element_type x1, local copies, waits for them, and re-layouts, on_device(): mean_field = jnp.sum(flat, axis=0, dtype=jnp.float32) / sample_states  4.92 us
    unnamed x14, local copies, waits for them, and re-layouts  4.27 us
  transfers between devices with their start and end apart: 3, of which 1 were waited for; matrix products, arithmetic and copies ran while one was open for 24% of the time, Pallas kernels for 0%

commit v1 on v0

v1 whole, which is shorter than its diff:
```python
import functools

import jax
import jax.numpy as jnp
from jax import lax
from jax.experimental import pallas as pl
from jax.experimental.pallas import tpu as pltpu
from jax.sharding import PartitionSpec as P


NS_ITERS = 6
LOC_FAR = 0.5
DIRECT_MAX = 16


def split(x):
    high = x.astype(jnp.bfloat16)
    return high, (x - high.astype(jnp.float32)).astype(jnp.bfloat16)


def dot3(a, b):
    (ah, al), (bh, bl) = a, b
    dot = functools.partial(jnp.dot, preferred_element_type=jnp.float32)
    return dot(ah, bh) + (dot(ah, bl) + dot(al, bh))


def mix_kernel(groups, lists, spot, own, below, above, own_aux, below_aux, above_aux, mix, pert_buf):
    tiles, members, _ = mix.shape
    slots = own.shape[2]
    entries = lists.shape[1]
    blocks = own.shape[0]
    rows = members // groups
    me = spot[0]
    contract_last = (((1,), (1,)), ((), ()))
    row = lax.broadcasted_iota(jnp.int32, (members, members), 0)
    col = lax.broadcasted_iota(jnp.int32, (members, members), 1)
    eye = jnp.where(row == col, 1.0, 0.0).astype(jnp.float32)
    state = []
    for t in range(tiles):
        weights, innovs = [], []
        for n in range(entries):
            name = lists[t, n]
            if n == 0:
                src, aux, block = below, below_aux, name
            elif n == 1:
                src, aux, block = above, above_aux, name - 2 * blocks
            else:
                src, aux, block = own, own_aux, name - blocks
            for u in range(groups):
                start = 0 if groups == 1 else pl.multiple_of((me ^ u) * rows, rows)
                pert_buf[t, u * rows:(u + 1) * rows, n * slots:(n + 1) * slots] = src[
                    block, pl.ds(start, rows), :
                ]
            weights.append(aux[block, t:t + 1, :])
            innovs.append(aux[block, tiles:tiles + 1, :])
        pert = pert_buf[t]
        weight = jnp.concatenate(weights, axis=1)
        innov = jnp.concatenate(innovs, axis=1)
        scaled = (pert.astype(jnp.float32) * weight).astype(jnp.bfloat16)
        precision = (members - 1) * eye + lax.dot_general(
            pert, scaled, contract_last, preferred_element_type=jnp.float32
        )
        drive = lax.dot_general(
            jnp.broadcast_to(innov, (8, innov.shape[1])).astype(jnp.bfloat16),
            scaled,
            contract_last,
            preferred_element_type=jnp.float32,
        )
        square = jnp.sum(precision * precision, axis=0, keepdims=True)
        norm = jnp.sqrt(jnp.sum(square, axis=1, keepdims=True))
        state.append((precision / norm, drive, norm))
    currents = [s[0] for s in state]
    roots = [None] * tiles
    for sweep in range(NS_ITERS):
        for t in range(tiles):
            current = split(currents[t])
            if sweep == 0:
                factor = 1.5 * eye - 0.5 * currents[t]
            else:
                factor = 1.5 * eye - 0.5 * dot3(current, split(roots[t]))
            both = split(factor)
            if sweep < NS_ITERS - 1:
                currents[t] = dot3(both, current)
            roots[t] = factor if sweep == 0 else dot3(split(roots[t]), both)
    for t in range(tiles):
        _, drive, norm = state[t]
        root = split(roots[t])
        inner = dot3(split(drive), root)
        gain = dot3(split(inner), root) / norm
        scale = jnp.sqrt((members - 1) / norm)
        mix[t] = (scale * roots[t] + gain[0:1, :]).astype(jnp.bfloat16)


def analysis_kernel(pieces, mix, *refs):
    arrived, sent = refs[:pieces], refs[pieces:2 * pieces]
    spread_buf, out_buf = refs[2 * pieces:]
    tiles, members, _ = mix.shape
    rows = members // pieces
    depth, points = arrived[0].shape[2:]
    for t in range(tiles):
        mean = jnp.zeros((depth, points), jnp.float32)
        for u in range(pieces):
            mean += jnp.sum(arrived[u][:, t].astype(jnp.float32), axis=0)
        mean = mean / members
        for u in range(pieces):
            spread = arrived[u][:, t].astype(jnp.float32) - mean
            spread_buf[u * rows * depth:(u + 1) * rows * depth, :] = spread.reshape(
                rows * depth, points
            )
        step = 2 if depth % 2 == 0 else 1
        for level in range(0, depth, step):
            field = jnp.concatenate(
                [
                    spread_buf[pl.ds(level + k, members, stride=depth), :].astype(jnp.bfloat16)
                    for k in range(step)
                ],
                axis=1,
            )
            result = jnp.dot(mix[t], field, preferred_element_type=jnp.float32)
            for k in range(step):
                out_buf[pl.ds(level + k, members, stride=depth), :] = (
                    result[:, k * points:(k + 1) * points] + mean[level + k:level + k + 1, :]
                )
        for u in range(pieces):
            sent[u][:, t] = (
                out_buf[u * rows * depth:(u + 1) * rows * depth, :]
                .reshape(rows, depth, points)
                .astype(jnp.bfloat16)
            )


def neighbours(x, axis):
    peers = lax.axis_size(axis)
    if peers == 1:
        return x, x
    if peers == 2:
        other = lax.ppermute(x, axis, [(0, 1), (1, 0)])
        return other, other
    up = [(i, i + 1) for i in range(peers - 1)]
    return lax.ppermute(x, axis, up), lax.ppermute(x, axis, [(j, i) for i, j in up])


def send_order(wide):
    far = list(range(wide // 2, wide))
    half = len(far) // 2
    mixed = [s for pair in zip(far[half:], far[:half]) for s in pair]
    return mixed + list(range(1, wide // 2))


def on_device(
    prior_states,
    measured_anomalies,
    departures,
    error_precisions,
    datum_totals,
    datum_patch_owner,
    patch_group_lookup,
):
    wide = lax.axis_size("wide")
    bands = lax.axis_size("band")
    me = lax.axis_index("wide").astype(jnp.int32)
    direct = wide <= DIRECT_MAX
    mine, _, _, depth, points = prior_states.shape
    blocks, members, slots = measured_anomalies.shape[1:]
    tiles = patch_group_lookup.shape[1]
    fields = prior_states.reshape(mine, wide, tiles, depth, points)

    if direct:
        arrived = {0: lax.dynamic_index_in_dim(fields, me, 1, keepdims=False)}
        for s in send_order(wide):
            part = lax.dynamic_index_in_dim(fields, me ^ s, 1, keepdims=False)
            arrived[s] = lax.ppermute(part, "wide", [(i, i ^ s) for i in range(wide)])
        arrived = [arrived[s] for s in range(wide)]
    else:
        arrived = [
            lax.all_to_all(fields, "wide", split_axis=1, concat_axis=0, tiled=True).reshape(
                members, tiles, depth, points
            )
        ]
    pieces = len(arrived)

    slot_index = jnp.arange(slots, dtype=jnp.int32)
    live = jnp.where(slot_index[None, :] < datum_totals[0][:, None], 1.0, 0.0)
    base = error_precisions[0].astype(jnp.float32) * live
    tile_ids = jnp.arange(tiles, dtype=jnp.int32)
    near = jnp.where(datum_patch_owner[0][:, None, :] == tile_ids[None, :, None], 1.0, LOC_FAR)
    pad = -(tiles + 1) % 8
    aux = jnp.concatenate(
        [
            base[:, None, :] * near,
            departures[0][:, None, :].astype(jnp.float32),
            jnp.zeros((blocks, pad, slots), jnp.float32),
        ],
        axis=1,
    )
    below, above = neighbours(measured_anomalies[0], "band")
    below_aux, above_aux = neighbours(aux, "band")
    band = lax.axis_index("band")
    below_aux = jnp.where(band > 0, below_aux, 0.0)
    above_aux = jnp.where(band < bands - 1, above_aux, 0.0)

    vmem = pl.BlockSpec(memory_space=pltpu.VMEM)
    smem = pl.BlockSpec(memory_space=pltpu.SMEM)
    mix = pl.pallas_call(
        functools.partial(mix_kernel, pieces),
        out_shape=jax.ShapeDtypeStruct((tiles, members, members), jnp.bfloat16),
        in_specs=[smem, smem] + [vmem] * 6,
        out_specs=vmem,
        scratch_shapes=[
            pltpu.VMEM((tiles, members, patch_group_lookup.shape[2] * slots), jnp.bfloat16)
        ],
        name="mix",
    )(
        patch_group_lookup[0],
        me.reshape(1),
        measured_anomalies[0],
        below,
        above,
        aux,
        below_aux,
        above_aux,
    )
    rows = members // pieces
    sent = pl.pallas_call(
        functools.partial(analysis_kernel, pieces),
        out_shape=[jax.ShapeDtypeStruct((rows, tiles, depth, points), jnp.bfloat16)] * pieces,
        in_specs=[vmem] * (1 + pieces),
        out_specs=[vmem] * pieces,
        scratch_shapes=[pltpu.VMEM((members * depth, points), jnp.float32)] * 2,
        name="analysis",
    )(mix, *arrived)

    if not direct:
        back = lax.all_to_all(
            sent[0].reshape(wide, mine, tiles, depth, points),
            "wide",
            split_axis=0,
            concat_axis=2,
            tiled=True,
        )
        return back.reshape(prior_states.shape)
    result = jnp.zeros(fields.shape, jnp.bfloat16)
    result = lax.dynamic_update_index_in_dim(result, sent[0], me, 1)
    back = {}
    for s in send_order(wide):
        back[s] = lax.ppermute(sent[s], "wide", [(i, i ^ s) for i in range(wide)])
    for s in send_order(wide):
        result = lax.dynamic_update_index_in_dim(result, back[s], me ^ s, 1)
    return result.reshape(prior_states.shape)


def solution(mesh):
    in_specs = (
        P("wide", "band", None, None, None),
        P("band", "wide", None, None),
        P("band", "wide", None),
        P("band", "wide", None),
        P("band", "wide"),
        P("band", "wide", None),
        P("band", "wide", None),
    )
    out_specs = P("wide", "band", None, None, None)
    return jax.shard_map(
        on_device, mesh=mesh, in_specs=in_specs, out_specs=out_specs, check_vma=False
    )
```

time: 137 us -> 141 us (1.029)
  starting transfers between devices: 13.5 us -> 84.8 us
  blocking collectives: 58 us -> 0 us
  matrix products: 28.1 us -> 0 us
  waiting for transfers between devices: 11.6 us -> 30.1 us
  Pallas kernels: 0 us -> 17.7 us
  local copies, waits for them, and re-layouts: 17.3 us -> 6.55 us
  other arithmetic: 8.02 us -> 0.76 us
    ppermute x2 -> x32, starting transfers between devices: 5.04 us -> 84.8 us  [the longest x15 45.2 us: on_device(): back[s] = lax.ppermute(sent[s], 'wide', [(i, i ^ s) for i in range(wide)])]
    all_to_all x1 -> x0, blocking collectives: 58 us -> none  [on_device(): lax.all_to_all(result.astype(jnp.bfloat16).reshape(array_shape), 'wide',...]
    ppermute x2 -> x32, waiting for transfers between devices: 0.01 us -> 30.1 us  [the longest x15 16.9 us: on_device(): arrived[s] = lax.ppermute(part, 'wide', [(i, i ^ s) for i in range(wide)])]
    dot_general x22 -> x0, matrix products: 28.1 us -> none  [the longest x6 7.25 us: on_device(): jnp.einsum('tij,tjk->tik', root_inv, current, precision=HIGH)]
    pallas_call x0 -> x2, Pallas kernels: none -> 17.7 us  [the longest x1 12.2 us: on_device(): pl.pallas_call(functools.partial(mix_kernel, pieces), out_shape=jax.Shape...]
    all_to_all x1 -> x0, waiting for transfers between devices: 11.6 us -> none  [on_device(): lax.all_to_all(prior_states, 'wide', split_axis=2, concat_axis=0, tiled=T...]
    all_to_all x1 -> x0, starting transfers between devices: 8.47 us -> none  [on_device(): lax.all_to_all(prior_states, 'wide', split_axis=2, concat_axis=0, tiled=T...]
    convert_element_type x1 -> x0, local copies, waits for them, and re-layouts: 4.92 us -> none  [on_device(): mean_field = jnp.sum(flat, axis=0, dtype=jnp.float32) / sample_states]
  transfers between devices with their start and end apart: 3 -> 32, of which waited for: 1 -> 10; matrix products, arithmetic and copies ran while one was open for 24% -> 1% of each run, Pallas kernels for 0% -> 9%
where the time goes in v1:
time: 141 us; the launch traced here: 140 us
  starting transfers between devices  84.8 us (60%)
  waiting for transfers between devices  30.1 us (21%)
  Pallas kernels  17.7 us (13%)
  local copies, waits for them, and re-layouts  6.55 us (5%)
    ppermute x15, starting transfers between devices, on_device(): back[s] = lax.ppermute(sent[s], 'wide', [(i, i ^ s) for i in range(wide)])  45.2 us
    ppermute x15, starting transfers between devices, on_device(): arrived[s] = lax.ppermute(part, 'wide', [(i, i ^ s) for i in range(wide)])  39.5 us
    ppermute x15, waiting for transfers between devices, on_device(): arrived[s] = lax.ppermute(part, 'wide', [(i, i ^ s) for i in range(wide)])  16.9 us
    ppermute x15, waiting for transfers between devices, on_device(): back[s] = lax.ppermute(sent[s], 'wide', [(i, i ^ s) for i in range(wide)])  13.2 us
    pallas_call x1, Pallas kernels, on_device(): pl.pallas_call(functools.partial(mix_kernel, pieces), out_shape=jax.Shape...  12.2 us
    pallas_call x1, Pallas kernels, on_device(): pl.pallas_call(functools.partial(analysis_kernel, pieces), out_shape=[jax...  5.46 us
    squeeze x1, local copies, waits for them, and re-layouts, on_device(): part = lax.dynamic_index_in_dim(fields, me ^ s, 1, keepdims=False)  2.82 us
  transfers between devices with their start and end apart: 32, of which 10 were waited for; matrix products, arithmetic and copies ran while one was open for 1% of the time, Pallas kernels for 9%

profile of v1, /device:TPU:0, one launch (start us, length us, event | category | flops | bytes accessed | tf_op | source)
XLA Modules:
  0.0 140.5 jit_solution(14925015183731265569)
XLA Ops:
  0.0 2.8 %dynamic-slice_bitcast_fusion = (bf16[16,4,8,128]{3,2,1,0:T(8,128)(2,1)S(1)}, bf16[16,4,8,128]{3,2,1,0:T(8,128)(2,1)S(1)}, bf16[16,4,8,128]{3,2,1,0:T(8,128)(2,1...) fusion(bf16[16,16,4,8,128]{4,3,2,1,0:T(8,128)(2,1)} %bitcast.12, ...), kind=kLoop, calls=%fused_computation.16 | loop fusion | bytes 4194368 | tf_op jit(solution)/shard_map/jit(dynamic_index_in_dim)/squeeze | solution.py:171
  2.8 5.0 %collective-permute-start.10 = (bf16[16,4,8,128]{3,2,1,0:T(8,128)(2,1)S(1)}, bf16[16,4,8,128]{3,2,1,0:T(8,128)(2,1)S(1)}, u32[]{:S(2)}, u32[]{:S(2)}) collective-permute-start(bf16[16,4,8,128]{3,2,1,0:T(8,128)(2,1)S(1)} %get-tuple-element.43), channel_id=1, source_target_pairs={{0,18},{2,16},{4,22},{6,20},{8,26},{10,24},{12,30},{14,28},{16,2},... | collective-permute-start | bytes 393224 | tf_op jit(solution)/shard_map/ppermute | solution.py:172
  7.8 1.3 collective-permute-start.11
  9.1 0.1 convert_multiply_fusion
  9.2 0.1 pad.2.clone
  9.3 0.1 maximum_maximum_fusion.own_aux
  9.4 0.0 collective-permute-start.1
  9.4 2.6 %collective-permute-start.12 = (bf16[16,4,8,128]{3,2,1,0:T(8,128)(2,1)S(1)}, bf16[16,4,8,128]{3,2,1,0:T(8,128)(2,1)S(1)}, u32[]{:S(2)}, u32[]{:S(2)}) collective-permute-start(bf16[16,4,8,128]{3,2,1,0:T(8,128)(2,1)S(1)} %get-tuple-element.41), channel_id=1, source_target_pairs={{0,22},{2,20},{4,18},{6,16},{8,30},{10,28},{12,26},{14,24},{16,6},... | collective-permute-start | bytes 393224 | tf_op jit(solution)/shard_map/ppermute | solution.py:172
  12.0 1.3 collective-permute-start.13
  13.3 3.4 %collective-permute-start.14 = (bf16[16,4,8,128]{3,2,1,0:T(8,128)(2,1)S(1)}, bf16[16,4,8,128]{3,2,1,0:T(8,128)(2,1)S(1)}, u32[]{:S(2)}, u32[]{:S(2)}) collective-permute-start(bf16[16,4,8,128]{3,2,1,0:T(8,128)(2,1)S(1)} %get-tuple-element.39), channel_id=1, source_target_pairs={{0,26},{2,24},{4,30},{6,28},{8,18},{10,16},{12,22},{14,20},{16,10}... | collective-permute-start | bytes 393224 | tf_op jit(solution)/shard_map/ppermute | solution.py:172
  16.7 9.5 %collective-permute-done.10.refs_9_ = bf16[16,4,8,128]{3,2,1,0:T(8,128)(2,1)S(1)} collective-permute-done((bf16[16,4,8,128]{3,2,1,0:T(8,128)(2,1)S(1)}, bf16[16,4,8,128]{3,2,1,0:T(8,128)(2,1)S(1)}, u32[]{:S(2)}, u32[]{:S(2)}) %collective-permute-start.10) | collective-permute-done | bytes 131104 | tf_op jit(solution)/shard_map/ppermute | solution.py:172
  26.2 3.7 %collective-permute-start.15 = (bf16[16,4,8,128]{3,2,1,0:T(8,128)(2,1)S(1)}, bf16[16,4,8,128]{3,2,1,0:T(8,128)(2,1)S(1)}, u32[]{:S(2)}, u32[]{:S(2)}) collective-permute-start(bf16[16,4,8,128]{3,2,1,0:T(8,128)(2,1)S(1)} %get-tuple-element.38), channel_id=1, source_target_pairs={{0,28},{2,30},{4,24},{6,26},{8,20},{10,22},{12,16},{14,18},{16,12}... | collective-permute-start | bytes 393224 | tf_op jit(solution)/shard_map/ppermute | solution.py:172
  29.9 0.4 collective-permute-done.11.refs_10_
  30.3 0.0 collective-permute-start
  30.3 5.6 %collective-permute-done.12.refs_11_ = bf16[16,4,8,128]{3,2,1,0:T(8,128)(2,1)S(1)} collective-permute-done((bf16[16,4,8,128]{3,2,1,0:T(8,128)(2,1)S(1)}, bf16[16,4,8,128]{3,2,1,0:T(8,128)(2,1)S(1)}, u32[]{:S(2)}, u32[]{:S(2)}) %collective-permute-start.12) | collective-permute-done | bytes 131104 | tf_op jit(solution)/shard_map/ppermute | solution.py:172
  35.9 3.4 %collective-permute-start.16 = (bf16[16,4,8,128]{3,2,1,0:T(8,128)(2,1)S(1)}, bf16[16,4,8,128]{3,2,1,0:T(8,128)(2,1)S(1)}, u32[]{:S(2)}, u32[]{:S(2)}) collective-permute-start(bf16[16,4,8,128]{3,2,1,0:T(8,128)(2,1)S(1)} %get-tuple-element.37), channel_id=1, source_target_pairs={{0,30},{2,28},{4,26},{6,24},{8,22},{10,20},{12,18},{14,16},{16,14}... | collective-permute-start | bytes 393224 | tf_op jit(solution)/shard_map/ppermute | solution.py:172
  39.3 0.0 collective-permute-done.14.refs_13_
  39.3 2.4 %collective-permute-start.3 = (bf16[16,4,8,128]{3,2,1,0:T(8,128)(2,1)S(1)}, bf16[16,4,8,128]{3,2,1,0:T(8,128)(2,1)S(1)}, u32[]{:S(2)}, u32[]{:S(2)}) collective-permute-start(bf16[16,4,8,128]{3,2,1,0:T(8,128)(2,1)S(1)} %get-tuple-element.50), channel_id=1, source_target_pairs={{0,4},{2,6},{4,0},{6,2},{8,12},{10,14},{12,8},{14,10},{16,20},{18,... | collective-permute-start | bytes 393224 | tf_op jit(solution)/shard_map/ppermute | solution.py:172
  41.7 0.0 collective-permute-done.15.refs_14_
  41.7 1.5 %collective-permute-start.4 = (bf16[16,4,8,128]{3,2,1,0:T(8,128)(2,1)S(1)}, bf16[16,4,8,128]{3,2,1,0:T(8,128)(2,1)S(1)}, u32[]{:S(2)}, u32[]{:S(2)}) collective-permute-start(bf16[16,4,8,128]{3,2,1,0:T(8,128)(2,1)S(1)} %get-tuple-element.49), channel_id=1, source_target_pairs={{0,6},{2,4},{4,2},{6,0},{8,14},{10,12},{12,10},{14,8},{16,22},{18,... | collective-permute-start | bytes 393224 | tf_op jit(solution)/shard_map/ppermute | solution.py:172
  43.2 1.5 %collective-permute-done.16.refs_15_ = bf16[16,4,8,128]{3,2,1,0:T(8,128)(2,1)S(1)} collective-permute-done((bf16[16,4,8,128]{3,2,1,0:T(8,128)(2,1)S(1)}, bf16[16,4,8,128]{3,2,1,0:T(8,128)(2,1)S(1)}, u32[]{:S(2)}, u32[]{:S(2)}) %collective-permute-start.16) | collective-permute-done | bytes 131104 | tf_op jit(solution)/shard_map/ppermute | solution.py:172
  44.7 5.0 %collective-permute-start.5 = (bf16[16,4,8,128]{3,2,1,0:T(8,128)(2,1)S(1)}, bf16[16,4,8,128]{3,2,1,0:T(8,128)(2,1)S(1)}, u32[]{:S(2)}, u32[]{:S(2)}) collective-permute-start(bf16[16,4,8,128]{3,2,1,0:T(8,128)(2,1)S(1)} %get-tuple-element.48), channel_id=1, source_target_pairs={{0,8},{2,10},{4,12},{6,14},{8,0},{10,2},{12,4},{14,6},{16,24},{18,... | collective-permute-start | bytes 393224 | tf_op jit(solution)/shard_map/ppermute | solution.py:172
  49.6 0.0 collective-permute-done.2.refs_1_
  49.6 0.9 collective-permute-start.6
  50.5 0.0 collective-permute-done.3.refs_2_
  50.6 3.9 %collective-permute-start.7 = (bf16[16,4,8,128]{3,2,1,0:T(8,128)(2,1)S(1)}, bf16[16,4,8,128]{3,2,1,0:T(8,128)(2,1)S(1)}, u32[]{:S(2)}, u32[]{:S(2)}) collective-permute-start(bf16[16,4,8,128]{3,2,1,0:T(8,128)(2,1)S(1)} %get-tuple-element.46), channel_id=1, source_target_pairs={{0,12},{2,14},{4,8},{6,10},{8,4},{10,6},{12,0},{14,2},{16,28},{18,... | collective-permute-start | bytes 393224 | tf_op jit(solution)/shard_map/ppermute | solution.py:172
  54.4 0.0 collective-permute-done.4.refs_3_
  54.5 0.6 collective-permute-start.8
  55.0 4.7 %collective-permute-start.9 = (bf16[16,4,8,128]{3,2,1,0:T(8,128)(2,1)S(1)}, bf16[16,4,8,128]{3,2,1,0:T(8,128)(2,1)S(1)}, u32[]{:S(2)}, u32[]{:S(2)}) collective-permute-start(bf16[16,4,8,128]{3,2,1,0:T(8,128)(2,1)S(1)} %get-tuple-element.44), channel_id=1, source_target_pairs={{0,16},{2,18},{4,20},{6,22},{8,24},{10,26},{12,28},{14,30},{16,0},... | collective-permute-start | bytes 393224 | tf_op jit(solution)/shard_map/ppermute | solution.py:172
  59.7 0.6 broadcast_select_fusion
  60.3 12.2 %mix.1 = bf16[4,256,256]{2,1,0:T(8,128)(2,1)} custom-call(s32[4,4]{1,0:T(4,128)} %bitcast.129, s32[1]{0:T(128)} %bitcast.1.spot, bf16[4,256,128]{2,1,0:T(8,128)(2,1)} %bitcast.126, bf16[4,256,128]{2,1,0:T(8,128)(2,1)} %copy-done.1, bf16[4,256,128]{2,1,0:T(8,128)(2,1)} %copy-done.1, f32[4,8,128]{2,1,0:T(8,128)} %copy-done.19, ...), custom_call_target="tpu_custom_call" | custom-call | tf_op jit(solution)/shard_map/mix/pallas_call | solution.py:204
  72.5 0.0 collective-permute-done.7.refs_6_
  72.7 0.5 copy-done.13
  73.2 0.0 copy-done.14
  73.2 0.1 copy-done.15
  73.3 0.1 copy-done.16
  73.3 0.0 copy-done.17
  73.3 5.5 %analysis.1 = (bf16[16,4,8,128]{3,2,1,0:T(8,128)(2,1)}, bf16[16,4,8,128]{3,2,1,0:T(8,128)(2,1)}, bf16[16,4,8,128]{3,2,1,0:T(8,128)(2,1)}, bf16[16,4,8,128]{3,2,1...) custom-call(bf16[4,256,256]{2,1,0:T(8,128)(2,1)} %mix.1, ...), custom_call_target="tpu_custom_call" | custom-call | tf_op jit(solution)/shard_map/analysis/pallas_call | solution.py:224
  78.9 0.7 collective-permute-start.17
  79.6 0.3 collective-permute-start.18
  79.9 4.9 %collective-permute-start.19 = (bf16[16,4,8,128]{3,2,1,0:T(8,128)(2,1)}, bf16[16,4,8,128]{3,2,1,0:T(8,128)(2,1)S(1)}, u32[]{:S(2)}, u32[]{:S(2)}) collective-permute-start(bf16[16,4,8,128]{3,2,1,0:T(8,128)(2,1)} %get-tuple-element.24), channel_id=1, source_target_pairs={{0,26},{2,24},{4,30},{6,28},{8,18},{10,16},{12,22},{14,20},{16,10}... | collective-permute-start | bytes 393224 | tf_op jit(solution)/shard_map/ppermute | solution.py:246
  84.8 0.9 collective-permute-start.20
  85.7 1.2 collective-permute-start.21
  86.9 0.4 broadcast_in_dim.79
  87.4 0.0 collective-permute-done.17
  87.4 13.6 %collective-permute-start.22 = (bf16[16,4,8,128]{3,2,1,0:T(8,128)(2,1)S(1)}, bf16[16,4,8,128]{3,2,1,0:T(8,128)(2,1)S(1)}, u32[]{:S(2)}, u32[]{:S(2)}) collective-permute-start(bf16[16,4,8,128]{3,2,1,0:T(8,128)(2,1)S(1)} %copy-done.33), channel_id=1, source_target_pairs={{0,20},{2,22},{4,16},{6,18},{8,28},{10,30},{12,24},{14,26},{16,4},... | collective-permute-start | bytes 393224 | tf_op jit(solution)/shard_map/ppermute | solution.py:246
  101.0 0.2 collective-permute-done.18
  101.2 3.5 %collective-permute-start.23 = (bf16[16,4,8,128]{3,2,1,0:T(8,128)(2,1)S(1)}, bf16[16,4,8,128]{3,2,1,0:T(8,128)(2,1)S(1)}, u32[]{:S(2)}, u32[]{:S(2)}) collective-permute-start(bf16[16,4,8,128]{3,2,1,0:T(8,128)(2,1)S(1)} %copy-done.32), channel_id=1, source_target_pairs={{0,30},{2,28},{4,26},{6,24},{8,22},{10,20},{12,18},{14,16},{16,14}... | collective-permute-start | bytes 393224 | tf_op jit(solution)/shard_map/ppermute | solution.py:246
  104.8 8.5 %collective-permute-start.24 = (bf16[16,4,8,128]{3,2,1,0:T(8,128)(2,1)S(1)}, bf16[16,4,8,128]{3,2,1,0:T(8,128)(2,1)S(1)}, u32[]{:S(2)}, u32[]{:S(2)}) collective-permute-start(bf16[16,4,8,128]{3,2,1,0:T(8,128)(2,1)S(1)} %copy-done.31), channel_id=1, source_target_pairs={{0,22},{2,20},{4,18},{6,16},{8,30},{10,28},{12,26},{14,24},{16,6},... | collective-permute-start | bytes 393224 | tf_op jit(solution)/shard_map/ppermute | solution.py:246
  113.3 0.7 collective-permute-start.25
  114.0 4.5 %collective-permute-start.26 = (bf16[16,4,8,128]{3,2,1,0:T(8,128)(2,1)S(1)}, bf16[16,4,8,128]{3,2,1,0:T(8,128)(2,1)S(1)}, u32[]{:S(2)}, u32[]{:S(2)}) collective-permute-start(bf16[16,4,8,128]{3,2,1,0:T(8,128)(2,1)S(1)} %copy-done.29), channel_id=1, source_target_pairs={{0,4},{2,6},{4,0},{6,2},{8,12},{10,14},{12,8},{14,10},{16,20},{18,... | collective-permute-start | bytes 393224 | tf_op jit(solution)/shard_map/ppermute | solution.py:246
  118.5 3.9 %collective-permute-done.22 = bf16[16,4,8,128]{3,2,1,0:T(8,128)(2,1)S(1)} collective-permute-done((bf16[16,4,8,128]{3,2,1,0:T(8,128)(2,1)S(1)}, bf16[16,4,8,128]{3,2,1,0:T(8,128)(2,1)S(1)}, u32[]{:S(2)}, u32[]{:S(2)}) %collective-permute-start.22) | collective-permute-done | bytes 131104 | tf_op jit(solution)/shard_map/ppermute | solution.py:246
  122.4 0.5 collective-permute-start.27
  123.0 0.5 copy.24
  123.5 0.3 copy-done.27
  123.8 3.0 %collective-permute-start.28 = (bf16[16,4,8,128]{3,2,1,0:T(8,128)(2,1)S(1)}, bf16[16,4,8,128]{3,2,1,0:T(8,128)(2,1)S(1)}, u32[]{:S(2)}, u32[]{:S(2)}) collective-permute-start(bf16[16,4,8,128]{3,2,1,0:T(8,128)(2,1)S(1)} %copy-done.27), channel_id=1, source_target_pairs={{0,8},{2,10},{4,12},{6,14},{8,0},{10,2},{12,4},{14,6},{16,24},{18,... | collective-permute-start | bytes 393224 | tf_op jit(solution)/shard_map/ppermute | solution.py:246
  126.8 1.0 collective-permute-done.24
  127.9 1.5 %collective-permute-start.30 = (bf16[16,4,8,128]{3,2,1,0:T(8,128)(2,1)S(1)}, bf16[16,4,8,128]{3,2,1,0:T(8,128)(2,1)S(1)}, u32[]{:S(2)}, u32[]{:S(2)}) collective-permute-start(bf16[16,4,8,128]{3,2,1,0:T(8,128)(2,1)S(1)} %copy-done.25), channel_id=1, source_target_pairs={{0,12},{2,14},{4,8},{6,10},{8,4},{10,6},{12,0},{14,2},{16,28},{18,... | collective-permute-start | bytes 393224 | tf_op jit(solution)/shard_map/ppermute | solution.py:246
  129.4 1.6 %collective-permute-start.31 = (bf16[16,4,8,128]{3,2,1,0:T(8,128)(2,1)S(1)}, bf16[16,4,8,128]{3,2,1,0:T(8,128)(2,1)S(1)}, u32[]{:S(2)}, u32[]{:S(2)}) collective-permute-start(bf16[16,4,8,128]{3,2,1,0:T(8,128)(2,1)S(1)} %copy-done.24), channel_id=1, source_target_pairs={{0,14},{2,12},{4,10},{6,8},{8,6},{10,4},{12,2},{14,0},{16,30},{18,... | collective-permute-start | bytes 393224 | tf_op jit(solution)/shard_map/ppermute | solution.py:246
  131.1 4.0 %collective-permute-done.29 = bf16[16,4,8,128]{3,2,1,0:T(8,128)(2,1)S(1)} collective-permute-done((bf16[16,4,8,128]{3,2,1,0:T(8,128)(2,1)S(1)}, bf16[16,4,8,128]{3,2,1,0:T(8,128)(2,1)S(1)}, u32[]{:S(2)}, u32[]{:S(2)}) %collective-permute-start.29) | collective-permute-done | bytes 131104 | tf_op jit(solution)/shard_map/ppermute | solution.py:246
  135.1 2.1 %collective-permute-done.30 = bf16[16,4,8,128]{3,2,1,0:T(8,128)(2,1)S(1)} collective-permute-done((bf16[16,4,8,128]{3,2,1,0:T(8,128)(2,1)S(1)}, bf16[16,4,8,128]{3,2,1,0:T(8,128)(2,1)S(1)}, u32[]{:S(2)}, u32[]{:S(2)}) %collective-permute-start.30) | collective-permute-done | bytes 131104 | tf_op jit(solution)/shard_map/ppermute | solution.py:246
  137.3 1.8 %collective-permute-done.31 = bf16[16,4,8,128]{3,2,1,0:T(8,128)(2,1)S(1)} collective-permute-done((bf16[16,4,8,128]{3,2,1,0:T(8,128)(2,1)S(1)}, bf16[16,4,8,128]{3,2,1,0:T(8,128)(2,1)S(1)}, u32[]{:S(2)}, u32[]{:S(2)}) %collective-permute-start.31) | collective-permute-done | bytes 131104 | tf_op jit(solution)/shard_map/ppermute | solution.py:246
  139.1 0.0 copy-start
  139.1 1.3 copy-done
  (96 shorter events, 0.5 us)
Async XLA Ops:
  0.0 9.1 %copy-start.21 = (bf16[1,4,128]{2,1,0:T(4,128)(2,1)S(1)}, bf16[1,4,128]{2,1,0:T(4,128)(2,1)}, u32[]{:S(2)}) copy-start(bf16[1,4,128]{2,1,0:T(4,128)(2,1)} %param.9) | copy-start | bytes 3076
  0.0 9.1 %copy-start.22 = (bf16[1,4,128]{2,1,0:T(4,128)(2,1)S(1)}, bf16[1,4,128]{2,1,0:T(4,128)(2,1)}, u32[]{:S(2)}) copy-start(bf16[1,4,128]{2,1,0:T(4,128)(2,1)} %param.10) | copy-start | bytes 3076
  0.0 9.1 %copy-start.23 = (s32[1,4]{1,0:T(1,128)S(1)}, s32[1,4]{1,0:T(1,128)}, u32[]{:S(2)}) copy-start(s32[1,4]{1,0:T(1,128)} %param.11) | copy-start | bytes 52
  0.0 9.2 %copy-start.20 = (s32[1,4,128]{2,1,0:T(4,128)S(1)}, s32[1,4,128]{2,1,0:T(4,128)}, u32[]{:S(2)}) copy-start(s32[1,4,128]{2,1,0:T(4,128)} %param.12) | copy-start | bytes 6148
  0.0 30.3 %copy-start.2 = (bf16[1,4,256,128]{3,2,1,0:T(8,128)(2,1)S(1)}, bf16[1,4,256,128]{3,2,1,0:T(8,128)(2,1)}, u32[]{:S(2)}) copy-start(bf16[1,4,256,128]{3,2,1,0:T(8,128)(2,1)} %param.8) | copy-start | bytes 786436
  2.8 23.4 %collective-permute-start.10 = (bf16[16,4,8,128]{3,2,1,0:T(8,128)(2,1)S(1)}, bf16[16,4,8,128]{3,2,1,0:T(8,128)(2,1)S(1)}, u32[]{:S(2)}, u32[]{:S(2)}) collective-permute-start(bf16[16,4,8,128]{3,2,1,0:T(8,128)(2,1)S(1)} %get-tuple-element.43), channel_id=1, source_target_pairs={{0,18},{2,16},{4,22},{6,20},{8,26},{10,24},{12,30},{14,28},{16,2},... | collective-permute-start | bytes 393224 | tf_op jit(solution)/shard_map/ppermute | solution.py:172
  7.8 22.5 %collective-permute-start.11 = (bf16[16,4,8,128]{3,2,1,0:T(8,128)(2,1)S(1)}, bf16[16,4,8,128]{3,2,1,0:T(8,128)(2,1)S(1)}, u32[]{:S(2)}, u32[]{:S(2)}) collective-permute-start(bf16[16,4,8,128]{3,2,1,0:T(8,128)(2,1)S(1)} %get-tuple-element.42), channel_id=1, source_target_pairs={{0,20},{2,22},{4,16},{6,18},{8,28},{10,30},{12,24},{14,26},{16,4},... | collective-permute-start | bytes 393224 | tf_op jit(solution)/shard_map/ppermute | solution.py:172
  9.4 50.9 %copy-start.19 = (f32[4,8,128]{2,1,0:T(8,128)}, f32[4,8,128]{2,1,0:T(8,128)S(1)}, u32[]{:S(2)}) copy-start(f32[4,8,128]{2,1,0:T(8,128)S(1)} %maximum_maximum_fusion.own_aux) | copy-start | bytes 49156
  9.4 3.9 %collective-permute-start.1 = (f32[4,8,128]{2,1,0:T(8,128)S(1)}, f32[4,8,128]{2,1,0:T(8,128)S(1)}, u32[]{:S(2)}, u32[]{:S(2)}) collective-permute-start(f32[4,8,128]{2,1,0:T(8,128)S(1)} %maximum_maximum_fusion.own_aux), channel_id=1, source_target_pairs={{0,1},{1,0},{2,3},{3,2},{4,5},{5,4},{6,7},{7,6},{8,9},{9,8},{10,11... | collective-permute-start | bytes 49160 | tf_op jit(solution)/shard_map/ppermute | solution.py:137
  9.4 26.5 %collective-permute-start.12 = (bf16[16,4,8,128]{3,2,1,0:T(8,128)(2,1)S(1)}, bf16[16,4,8,128]{3,2,1,0:T(8,128)(2,1)S(1)}, u32[]{:S(2)}, u32[]{:S(2)}) collective-permute-start(bf16[16,4,8,128]{3,2,1,0:T(8,128)(2,1)S(1)} %get-tuple-element.41), channel_id=1, source_target_pairs={{0,22},{2,20},{4,18},{6,16},{8,30},{10,28},{12,26},{14,24},{16,6},... | collective-permute-start | bytes 393224 | tf_op jit(solution)/shard_map/ppermute | solution.py:172
  12.0 27.3 %collective-permute-start.13 = (bf16[16,4,8,128]{3,2,1,0:T(8,128)(2,1)S(1)}, bf16[16,4,8,128]{3,2,1,0:T(8,128)(2,1)S(1)}, u32[]{:S(2)}, u32[]{:S(2)}) collective-permute-start(bf16[16,4,8,128]{3,2,1,0:T(8,128)(2,1)S(1)} %get-tuple-element.40), channel_id=1, source_target_pairs={{0,24},{2,26},{4,28},{6,30},{8,16},{10,18},{12,20},{14,22},{16,8},... | collective-permute-start | bytes 393224 | tf_op jit(solution)/shard_map/ppermute | solution.py:172
  13.3 26.0 %collective-permute-start.14 = (bf16[16,4,8,128]{3,2,1,0:T(8,128)(2,1)S(1)}, bf16[16,4,8,128]{3,2,1,0:T(8,128)(2,1)S(1)}, u32[]{:S(2)}, u32[]{:S(2)}) collective-permute-start(bf16[16,4,8,128]{3,2,1,0:T(8,128)(2,1)S(1)} %get-tuple-element.39), channel_id=1, source_target_pairs={{0,26},{2,24},{4,30},{6,28},{8,18},{10,16},{12,22},{14,20},{16,10}... | collective-permute-start | bytes 393224 | tf_op jit(solution)/shard_map/ppermute | solution.py:172
  26.2 46.4 %copy-start.3 = (bf16[16,4,8,128]{3,2,1,0:T(8,128)(2,1)}, bf16[16,4,8,128]{3,2,1,0:T(8,128)(2,1)S(1)}, u32[]{:S(2)}) copy-start(bf16[16,4,8,128]{3,2,1,0:T(8,128)(2,1)S(1)} %collective-permute-done.10.refs_9_) | copy-start | bytes 393220
  26.2 15.5 %collective-permute-start.15 = (bf16[16,4,8,128]{3,2,1,0:T(8,128)(2,1)S(1)}, bf16[16,4,8,128]{3,2,1,0:T(8,128)(2,1)S(1)}, u32[]{:S(2)}, u32[]{:S(2)}) collective-permute-start(bf16[16,4,8,128]{3,2,1,0:T(8,128)(2,1)S(1)} %get-tuple-element.38), channel_id=1, source_target_pairs={{0,28},{2,30},{4,24},{6,26},{8,20},{10,22},{12,16},{14,18},{16,12}... | collective-permute-start | bytes 393224 | tf_op jit(solution)/shard_map/ppermute | solution.py:172
  30.3 42.3 %copy-start.4 = (bf16[16,4,8,128]{3,2,1,0:T(8,128)(2,1)}, bf16[16,4,8,128]{3,2,1,0:T(8,128)(2,1)S(1)}, u32[]{:S(2)}) copy-start(bf16[16,4,8,128]{3,2,1,0:T(8,128)(2,1)S(1)} %collective-permute-done.11.refs_10_) | copy-start | bytes 393220
  30.3 24.7 %collective-permute-start = (bf16[4,256,128]{2,1,0:T(8,128)(2,1)S(1)}, bf16[4,256,128]{2,1,0:T(8,128)(2,1)S(1)}, u32[]{:S(2)}, u32[]{:S(2)}) collective-permute-start(bf16[4,256,128]{2,1,0:T(8,128)(2,1)S(1)} %bitcast.127), channel_id=1, source_target_pairs={{0,1},{1,0},{2,3},{3,2},{4,5},{5,4},{6,7},{7,6},{8,9},{9,8},{10,11... | collective-permute-start | bytes 786440 | tf_op jit(solution)/shard_map/ppermute | solution.py:137
  35.9 36.7 %copy-start.5 = (bf16[16,4,8,128]{3,2,1,0:T(8,128)(2,1)}, bf16[16,4,8,128]{3,2,1,0:T(8,128)(2,1)S(1)}, u32[]{:S(2)}) copy-start(bf16[16,4,8,128]{3,2,1,0:T(8,128)(2,1)S(1)} %collective-permute-done.12.refs_11_) | copy-start | bytes 393220
  35.9 8.8 %collective-permute-start.16 = (bf16[16,4,8,128]{3,2,1,0:T(8,128)(2,1)S(1)}, bf16[16,4,8,128]{3,2,1,0:T(8,128)(2,1)S(1)}, u32[]{:S(2)}, u32[]{:S(2)}) collective-permute-start(bf16[16,4,8,128]{3,2,1,0:T(8,128)(2,1)S(1)} %get-tuple-element.37), channel_id=1, source_target_pairs={{0,30},{2,28},{4,26},{6,24},{8,22},{10,20},{12,18},{14,16},{16,14}... | collective-permute-start | bytes 393224 | tf_op jit(solution)/shard_map/ppermute | solution.py:172
  39.3 33.3 %copy-start.6 = (bf16[16,4,8,128]{3,2,1,0:T(8,128)(2,1)}, bf16[16,4,8,128]{3,2,1,0:T(8,128)(2,1)S(1)}, u32[]{:S(2)}) copy-start(bf16[16,4,8,128]{3,2,1,0:T(8,128)(2,1)S(1)} %collective-permute-done.13.refs_12_) | copy-start | bytes 393220
  39.3 10.3 %collective-permute-start.2 = (bf16[16,4,8,128]{3,2,1,0:T(8,128)(2,1)S(1)}, bf16[16,4,8,128]{3,2,1,0:T(8,128)(2,1)S(1)}, u32[]{:S(2)}, u32[]{:S(2)}) collective-permute-start(bf16[16,4,8,128]{3,2,1,0:T(8,128)(2,1)S(1)} %get-tuple-element.51), channel_id=1, source_target_pairs={{0,2},{2,0},{4,6},{6,4},{8,10},{10,8},{12,14},{14,12},{16,18},{18,... | collective-permute-start | bytes 393224 | tf_op jit(solution)/shard_map/ppermute | solution.py:172
  39.3 33.3 %copy-start.7 = (bf16[16,4,8,128]{3,2,1,0:T(8,128)(2,1)}, bf16[16,4,8,128]{3,2,1,0:T(8,128)(2,1)S(1)}, u32[]{:S(2)}) copy-start(bf16[16,4,8,128]{3,2,1,0:T(8,128)(2,1)S(1)} %collective-permute-done.14.refs_13_) | copy-start | bytes 393220
  39.3 11.2 %collective-permute-start.3 = (bf16[16,4,8,128]{3,2,1,0:T(8,128)(2,1)S(1)}, bf16[16,4,8,128]{3,2,1,0:T(8,128)(2,1)S(1)}, u32[]{:S(2)}, u32[]{:S(2)}) collective-permute-start(bf16[16,4,8,128]{3,2,1,0:T(8,128)(2,1)S(1)} %get-tuple-element.50), channel_id=1, source_target_pairs={{0,4},{2,6},{4,0},{6,2},{8,12},{10,14},{12,8},{14,10},{16,20},{18,... | collective-permute-start | bytes 393224 | tf_op jit(solution)/shard_map/ppermute | solution.py:172
  41.7 30.9 %copy-start.8 = (bf16[16,4,8,128]{3,2,1,0:T(8,128)(2,1)}, bf16[16,4,8,128]{3,2,1,0:T(8,128)(2,1)S(1)}, u32[]{:S(2)}) copy-start(bf16[16,4,8,128]{3,2,1,0:T(8,128)(2,1)S(1)} %collective-permute-done.15.refs_14_) | copy-start | bytes 393220
  41.7 12.7 %collective-permute-start.4 = (bf16[16,4,8,128]{3,2,1,0:T(8,128)(2,1)S(1)}, bf16[16,4,8,128]{3,2,1,0:T(8,128)(2,1)S(1)}, u32[]{:S(2)}, u32[]{:S(2)}) collective-permute-start(bf16[16,4,8,128]{3,2,1,0:T(8,128)(2,1)S(1)} %get-tuple-element.49), channel_id=1, source_target_pairs={{0,6},{2,4},{4,2},{6,0},{8,14},{10,12},{12,10},{14,8},{16,22},{18,... | collective-permute-start | bytes 393224 | tf_op jit(solution)/shard_map/ppermute | solution.py:172
  44.7 28.0 %copy-start.9 = (bf16[16,4,8,128]{3,2,1,0:T(8,128)(2,1)}, bf16[16,4,8,128]{3,2,1,0:T(8,128)(2,1)S(1)}, u32[]{:S(2)}) copy-start(bf16[16,4,8,128]{3,2,1,0:T(8,128)(2,1)S(1)} %collective-permute-done.16.refs_15_) | copy-start | bytes 393220
  44.7 27.8 %collective-permute-start.5 = (bf16[16,4,8,128]{3,2,1,0:T(8,128)(2,1)S(1)}, bf16[16,4,8,128]{3,2,1,0:T(8,128)(2,1)S(1)}, u32[]{:S(2)}, u32[]{:S(2)}) collective-permute-start(bf16[16,4,8,128]{3,2,1,0:T(8,128)(2,1)S(1)} %get-tuple-element.48), channel_id=1, source_target_pairs={{0,8},{2,10},{4,12},{6,14},{8,0},{10,2},{12,4},{14,6},{16,24},{18,... | collective-permute-start | bytes 393224 | tf_op jit(solution)/shard_map/ppermute | solution.py:172
  49.6 23.0 %copy-start.10 = (bf16[16,4,8,128]{3,2,1,0:T(8,128)(2,1)}, bf16[16,4,8,128]{3,2,1,0:T(8,128)(2,1)S(1)}, u32[]{:S(2)}) copy-start(bf16[16,4,8,128]{3,2,1,0:T(8,128)(2,1)S(1)} %collective-permute-done.2.refs_1_) | copy-start | bytes 393220
  49.6 22.9 %collective-permute-start.6 = (bf16[16,4,8,128]{3,2,1,0:T(8,128)(2,1)S(1)}, bf16[16,4,8,128]{3,2,1,0:T(8,128)(2,1)S(1)}, u32[]{:S(2)}, u32[]{:S(2)}) collective-permute-start(bf16[16,4,8,128]{3,2,1,0:T(8,128)(2,1)S(1)} %get-tuple-element.47), channel_id=1, source_target_pairs={{0,10},{2,8},{4,14},{6,12},{8,2},{10,0},{12,6},{14,4},{16,26},{18,... | collective-permute-start | bytes 393224 | tf_op jit(solution)/shard_map/ppermute | solution.py:172
  50.6 22.1 %copy-start.11 = (bf16[16,4,8,128]{3,2,1,0:T(8,128)(2,1)}, bf16[16,4,8,128]{3,2,1,0:T(8,128)(2,1)S(1)}, u32[]{:S(2)}) copy-start(bf16[16,4,8,128]{3,2,1,0:T(8,128)(2,1)S(1)} %collective-permute-done.3.refs_2_) | copy-start | bytes 393220
  50.6 22.0 %collective-permute-start.7 = (bf16[16,4,8,128]{3,2,1,0:T(8,128)(2,1)S(1)}, bf16[16,4,8,128]{3,2,1,0:T(8,128)(2,1)S(1)}, u32[]{:S(2)}, u32[]{:S(2)}) collective-permute-start(bf16[16,4,8,128]{3,2,1,0:T(8,128)(2,1)S(1)} %get-tuple-element.46), channel_id=1, source_target_pairs={{0,12},{2,14},{4,8},{6,10},{8,4},{10,6},{12,0},{14,2},{16,28},{18,... | collective-permute-start | bytes 393224 | tf_op jit(solution)/shard_map/ppermute | solution.py:172
  54.5 18.2 %copy-start.12 = (bf16[16,4,8,128]{3,2,1,0:T(8,128)(2,1)}, bf16[16,4,8,128]{3,2,1,0:T(8,128)(2,1)S(1)}, u32[]{:S(2)}) copy-start(bf16[16,4,8,128]{3,2,1,0:T(8,128)(2,1)S(1)} %collective-permute-done.4.refs_3_) | copy-start | bytes 393220
  54.5 18.1 %collective-permute-start.8 = (bf16[16,4,8,128]{3,2,1,0:T(8,128)(2,1)S(1)}, bf16[16,4,8,128]{3,2,1,0:T(8,128)(2,1)S(1)}, u32[]{:S(2)}, u32[]{:S(2)}) collective-permute-start(bf16[16,4,8,128]{3,2,1,0:T(8,128)(2,1)S(1)} %get-tuple-element.45), channel_id=1, source_target_pairs={{0,14},{2,12},{4,10},{6,8},{8,6},{10,4},{12,2},{14,0},{16,30},{18,... | collective-permute-start | bytes 393224 | tf_op jit(solution)/shard_map/ppermute | solution.py:172
  55.0 5.3 %copy-start.1 = (bf16[4,256,128]{2,1,0:T(8,128)(2,1)}, bf16[4,256,128]{2,1,0:T(8,128)(2,1)S(1)}, u32[]{:S(2)}) copy-start(bf16[4,256,128]{2,1,0:T(8,128)(2,1)S(1)} %collective-permute-done.below.above) | copy-start | bytes 786436
  55.0 17.5 %collective-permute-start.9 = (bf16[16,4,8,128]{3,2,1,0:T(8,128)(2,1)S(1)}, bf16[16,4,8,128]{3,2,1,0:T(8,128)(2,1)S(1)}, u32[]{:S(2)}, u32[]{:S(2)}) collective-permute-start(bf16[16,4,8,128]{3,2,1,0:T(8,128)(2,1)S(1)} %get-tuple-element.44), channel_id=1, source_target_pairs={{0,16},{2,18},{4,20},{6,22},{8,24},{10,26},{12,28},{14,30},{16,0},... | collective-permute-start | bytes 393224 | tf_op jit(solution)/shard_map/ppermute | solution.py:172
  72.5 0.7 copy-start.15
  72.6 0.8 copy-start.16
  72.6 0.8 copy-start.17
  78.8 8.5 %copy-start.18 = (bf16[16,4,8,128]{3,2,1,0:T(8,128)(2,1)S(1)}, bf16[16,4,8,128]{3,2,1,0:T(8,128)(2,1)}, u32[]{:S(2)}) copy-start(bf16[16,4,8,128]{3,2,1,0:T(8,128)(2,1)} %get-tuple-element.21) | copy-start | bytes 393220
  78.8 8.6 %copy-start.33 = (bf16[16,4,8,128]{3,2,1,0:T(8,128)(2,1)S(1)}, bf16[16,4,8,128]{3,2,1,0:T(8,128)(2,1)}, u32[]{:S(2)}) copy-start(bf16[16,4,8,128]{3,2,1,0:T(8,128)(2,1)} %get-tuple-element.27) | copy-start | bytes 393220
  78.8 22.4 %copy-start.32 = (bf16[16,4,8,128]{3,2,1,0:T(8,128)(2,1)S(1)}, bf16[16,4,8,128]{3,2,1,0:T(8,128)(2,1)}, u32[]{:S(2)}) copy-start(bf16[16,4,8,128]{3,2,1,0:T(8,128)(2,1)} %get-tuple-element.28) | copy-start | bytes 393220
  78.8 25.9 %copy-start.31 = (bf16[16,4,8,128]{3,2,1,0:T(8,128)(2,1)S(1)}, bf16[16,4,8,128]{3,2,1,0:T(8,128)(2,1)}, u32[]{:S(2)}) copy-start(bf16[16,4,8,128]{3,2,1,0:T(8,128)(2,1)} %get-tuple-element.29) | copy-start | bytes 393220
  78.9 34.4 %copy-start.30 = (bf16[16,4,8,128]{3,2,1,0:T(8,128)(2,1)S(1)}, bf16[16,4,8,128]{3,2,1,0:T(8,128)(2,1)}, u32[]{:S(2)}) copy-start(bf16[16,4,8,128]{3,2,1,0:T(8,128)(2,1)} %get-tuple-element.30) | copy-start | bytes 393220
  78.9 35.1 %copy-start.29 = (bf16[16,4,8,128]{3,2,1,0:T(8,128)(2,1)S(1)}, bf16[16,4,8,128]{3,2,1,0:T(8,128)(2,1)}, u32[]{:S(2)}) copy-start(bf16[16,4,8,128]{3,2,1,0:T(8,128)(2,1)} %get-tuple-element.31) | copy-start | bytes 393220
  78.9 43.6 %copy-start.28 = (bf16[16,4,8,128]{3,2,1,0:T(8,128)(2,1)S(1)}, bf16[16,4,8,128]{3,2,1,0:T(8,128)(2,1)}, u32[]{:S(2)}) copy-start(bf16[16,4,8,128]{3,2,1,0:T(8,128)(2,1)} %get-tuple-element.32) | copy-start | bytes 393220
  78.9 8.5 %collective-permute-start.17 = (bf16[16,4,8,128]{3,2,1,0:T(8,128)(2,1)}, bf16[16,4,8,128]{3,2,1,0:T(8,128)(2,1)S(1)}, u32[]{:S(2)}, u32[]{:S(2)}) collective-permute-start(bf16[16,4,8,128]{3,2,1,0:T(8,128)(2,1)} %get-tuple-element.22), channel_id=1, source_target_pairs={{0,24},{2,26},{4,28},{6,30},{8,16},{10,18},{12,20},{14,22},{16,8},... | collective-permute-start | bytes 393224 | tf_op jit(solution)/shard_map/ppermute | solution.py:246
  79.6 21.6 %collective-permute-start.18 = (bf16[16,4,8,128]{3,2,1,0:T(8,128)(2,1)}, bf16[16,4,8,128]{3,2,1,0:T(8,128)(2,1)S(1)}, u32[]{:S(2)}, u32[]{:S(2)}) collective-permute-start(bf16[16,4,8,128]{3,2,1,0:T(8,128)(2,1)} %get-tuple-element.23), channel_id=1, source_target_pairs={{0,16},{2,18},{4,20},{6,22},{8,24},{10,26},{12,28},{14,30},{16,0},... | collective-permute-start | bytes 393224 | tf_op jit(solution)/shard_map/ppermute | solution.py:246
  79.9 24.8 %collective-permute-start.19 = (bf16[16,4,8,128]{3,2,1,0:T(8,128)(2,1)}, bf16[16,4,8,128]{3,2,1,0:T(8,128)(2,1)S(1)}, u32[]{:S(2)}, u32[]{:S(2)}) collective-permute-start(bf16[16,4,8,128]{3,2,1,0:T(8,128)(2,1)} %get-tuple-element.24), channel_id=1, source_target_pairs={{0,26},{2,24},{4,30},{6,28},{8,18},{10,16},{12,22},{14,20},{16,10}... | collective-permute-start | bytes 393224 | tf_op jit(solution)/shard_map/ppermute | solution.py:246
  84.8 28.4 %collective-permute-start.20 = (bf16[16,4,8,128]{3,2,1,0:T(8,128)(2,1)}, bf16[16,4,8,128]{3,2,1,0:T(8,128)(2,1)S(1)}, u32[]{:S(2)}, u32[]{:S(2)}) collective-permute-start(bf16[16,4,8,128]{3,2,1,0:T(8,128)(2,1)} %get-tuple-element.25), channel_id=1, source_target_pairs={{0,18},{2,16},{4,22},{6,20},{8,26},{10,24},{12,30},{14,28},{16,2},... | collective-permute-start | bytes 393224 | tf_op jit(solution)/shard_map/ppermute | solution.py:246
  85.7 28.3 %collective-permute-start.21 = (bf16[16,4,8,128]{3,2,1,0:T(8,128)(2,1)}, bf16[16,4,8,128]{3,2,1,0:T(8,128)(2,1)S(1)}, u32[]{:S(2)}, u32[]{:S(2)}) collective-permute-start(bf16[16,4,8,128]{3,2,1,0:T(8,128)(2,1)} %get-tuple-element.26), channel_id=1, source_target_pairs={{0,28},{2,30},{4,24},{6,26},{8,20},{10,22},{12,16},{14,18},{16,12}... | collective-permute-start | bytes 393224 | tf_op jit(solution)/shard_map/ppermute | solution.py:246
  87.4 35.0 %collective-permute-start.22 = (bf16[16,4,8,128]{3,2,1,0:T(8,128)(2,1)S(1)}, bf16[16,4,8,128]{3,2,1,0:T(8,128)(2,1)S(1)}, u32[]{:S(2)}, u32[]{:S(2)}) collective-permute-start(bf16[16,4,8,128]{3,2,1,0:T(8,128)(2,1)S(1)} %copy-done.33), channel_id=1, source_target_pairs={{0,20},{2,22},{4,16},{6,18},{8,28},{10,30},{12,24},{14,26},{16,4},... | collective-permute-start | bytes 393224 | tf_op jit(solution)/shard_map/ppermute | solution.py:246
  101.2 22.3 %collective-permute-start.23 = (bf16[16,4,8,128]{3,2,1,0:T(8,128)(2,1)S(1)}, bf16[16,4,8,128]{3,2,1,0:T(8,128)(2,1)S(1)}, u32[]{:S(2)}, u32[]{:S(2)}) collective-permute-start(bf16[16,4,8,128]{3,2,1,0:T(8,128)(2,1)S(1)} %copy-done.32), channel_id=1, source_target_pairs={{0,30},{2,28},{4,26},{6,24},{8,22},{10,20},{12,18},{14,16},{16,14}... | collective-permute-start | bytes 393224 | tf_op jit(solution)/shard_map/ppermute | solution.py:246
  104.8 23.1 %collective-permute-start.24 = (bf16[16,4,8,128]{3,2,1,0:T(8,128)(2,1)S(1)}, bf16[16,4,8,128]{3,2,1,0:T(8,128)(2,1)S(1)}, u32[]{:S(2)}, u32[]{:S(2)}) collective-permute-start(bf16[16,4,8,128]{3,2,1,0:T(8,128)(2,1)S(1)} %copy-done.31), channel_id=1, source_target_pairs={{0,22},{2,20},{4,18},{6,16},{8,30},{10,28},{12,26},{14,24},{16,6},... | collective-permute-start | bytes 393224 | tf_op jit(solution)/shard_map/ppermute | solution.py:246
  113.3 14.6 %collective-permute-start.25 = (bf16[16,4,8,128]{3,2,1,0:T(8,128)(2,1)S(1)}, bf16[16,4,8,128]{3,2,1,0:T(8,128)(2,1)S(1)}, u32[]{:S(2)}, u32[]{:S(2)}) collective-permute-start(bf16[16,4,8,128]{3,2,1,0:T(8,128)(2,1)S(1)} %copy-done.30), channel_id=1, source_target_pairs={{0,2},{2,0},{4,6},{6,4},{8,10},{10,8},{12,14},{14,12},{16,18},{18,... | collective-permute-start | bytes 393224 | tf_op jit(solution)/shard_map/ppermute | solution.py:246
  114.0 15.4 %collective-permute-start.26 = (bf16[16,4,8,128]{3,2,1,0:T(8,128)(2,1)S(1)}, bf16[16,4,8,128]{3,2,1,0:T(8,128)(2,1)S(1)}, u32[]{:S(2)}, u32[]{:S(2)}) collective-permute-start(bf16[16,4,8,128]{3,2,1,0:T(8,128)(2,1)S(1)} %copy-done.29), channel_id=1, source_target_pairs={{0,4},{2,6},{4,0},{6,2},{8,12},{10,14},{12,8},{14,10},{16,20},{18,... | collective-permute-start | bytes 393224 | tf_op jit(solution)/shard_map/ppermute | solution.py:246
  122.4 8.6 %collective-permute-start.27 = (bf16[16,4,8,128]{3,2,1,0:T(8,128)(2,1)S(1)}, bf16[16,4,8,128]{3,2,1,0:T(8,128)(2,1)S(1)}, u32[]{:S(2)}, u32[]{:S(2)}) collective-permute-start(bf16[16,4,8,128]{3,2,1,0:T(8,128)(2,1)S(1)} %copy-done.28), channel_id=1, source_target_pairs={{0,6},{2,4},{4,2},{6,0},{8,14},{10,12},{12,10},{14,8},{16,22},{18,... | collective-permute-start | bytes 393224 | tf_op jit(solution)/shard_map/ppermute | solution.py:246
  122.9 0.9 copy-start.27
  122.9 4.9 %copy-start.26 = (bf16[16,4,8,128]{3,2,1,0:T(8,128)(2,1)S(1)}, bf16[16,4,8,128]{3,2,1,0:T(8,128)(2,1)}, u32[]{:S(2)}) copy-start(bf16[16,4,8,128]{3,2,1,0:T(8,128)(2,1)} %get-tuple-element.34) | copy-start | bytes 393220
  122.9 4.9 %copy-start.25 = (bf16[16,4,8,128]{3,2,1,0:T(8,128)(2,1)S(1)}, bf16[16,4,8,128]{3,2,1,0:T(8,128)(2,1)}, u32[]{:S(2)}) copy-start(bf16[16,4,8,128]{3,2,1,0:T(8,128)(2,1)} %get-tuple-element.35) | copy-start | bytes 393220
  122.9 6.4 %copy-start.24 = (bf16[16,4,8,128]{3,2,1,0:T(8,128)(2,1)S(1)}, bf16[16,4,8,128]{3,2,1,0:T(8,128)(2,1)}, u32[]{:S(2)}) copy-start(bf16[16,4,8,128]{3,2,1,0:T(8,128)(2,1)} %get-tuple-element.36) | copy-start | bytes 393220
  123.8 7.2 %collective-permute-start.28 = (bf16[16,4,8,128]{3,2,1,0:T(8,128)(2,1)S(1)}, bf16[16,4,8,128]{3,2,1,0:T(8,128)(2,1)S(1)}, u32[]{:S(2)}, u32[]{:S(2)}) collective-permute-start(bf16[16,4,8,128]{3,2,1,0:T(8,128)(2,1)S(1)} %copy-done.27), channel_id=1, source_target_pairs={{0,8},{2,10},{4,12},{6,14},{8,0},{10,2},{12,4},{14,6},{16,24},{18,... | collective-permute-start | bytes 393224 | tf_op jit(solution)/shard_map/ppermute | solution.py:246
  127.8 7.3 %collective-permute-start.29 = (bf16[16,4,8,128]{3,2,1,0:T(8,128)(2,1)S(1)}, bf16[16,4,8,128]{3,2,1,0:T(8,128)(2,1)S(1)}, u32[]{:S(2)}, u32[]{:S(2)}) collective-permute-start(bf16[16,4,8,128]{3,2,1,0:T(8,128)(2,1)S(1)} %copy-done.26), channel_id=1, source_target_pairs={{0,10},{2,8},{4,14},{6,12},{8,2},{10,0},{12,6},{14,4},{16,26},{18,... | collective-permute-start | bytes 393224 | tf_op jit(solution)/shard_map/ppermute | solution.py:246
  127.9 9.4 %collective-permute-start.30 = (bf16[16,4,8,128]{3,2,1,0:T(8,128)(2,1)S(1)}, bf16[16,4,8,128]{3,2,1,0:T(8,128)(2,1)S(1)}, u32[]{:S(2)}, u32[]{:S(2)}) collective-permute-start(bf16[16,4,8,128]{3,2,1,0:T(8,128)(2,1)S(1)} %copy-done.25), channel_id=1, source_target_pairs={{0,12},{2,14},{4,8},{6,10},{8,4},{10,6},{12,0},{14,2},{16,28},{18,... | collective-permute-start | bytes 393224 | tf_op jit(solution)/shard_map/ppermute | solution.py:246
  129.4 9.7 %collective-permute-start.31 = (bf16[16,4,8,128]{3,2,1,0:T(8,128)(2,1)S(1)}, bf16[16,4,8,128]{3,2,1,0:T(8,128)(2,1)S(1)}, u32[]{:S(2)}, u32[]{:S(2)}) collective-permute-start(bf16[16,4,8,128]{3,2,1,0:T(8,128)(2,1)S(1)} %copy-done.24), channel_id=1, source_target_pairs={{0,14},{2,12},{4,10},{6,8},{8,6},{10,4},{12,2},{14,0},{16,30},{18,... | collective-permute-start | bytes 393224 | tf_op jit(solution)/shard_map/ppermute | solution.py:246
  139.1 1.3 copy-start
  (2 other events, 1.3 us)

commit v2 on v1

v2 whole, which is shorter than its diff:
```python
import functools

import jax
import jax.numpy as jnp
from jax import lax
from jax.experimental import pallas as pl
from jax.experimental.pallas import tpu as pltpu
from jax.sharding import PartitionSpec as P


NS_ITERS = 6
LOC_FAR = 0.5
DIRECT_MAX = 16

LATE = 2
MIB = 1 << 20


def split(x):
    high = x.astype(jnp.bfloat16)
    return high, (x - high.astype(jnp.float32)).astype(jnp.bfloat16)


def dot3(a, b):
    (ah, al), (bh, bl) = a, b
    dot = functools.partial(jnp.dot, preferred_element_type=jnp.float32)
    return dot(ah, bh) + (dot(ah, bl) + dot(al, bh))


def mix_kernel(order, lists, spot, own, below, above, own_aux, below_aux, above_aux, mix, rest, pert_buf):
    tiles, members, _ = mix.shape
    slots = own.shape[2]
    entries = lists.shape[1]
    blocks = own.shape[0]
    rows = members // len(order)
    me = spot[0]
    contract_last = (((1,), (1,)), ((), ()))
    row = lax.broadcasted_iota(jnp.int32, (members, members), 0)
    col = lax.broadcasted_iota(jnp.int32, (members, members), 1)
    eye = jnp.where(row == col, 1.0, 0.0).astype(jnp.float32)
    state = []
    for t in range(tiles):
        weights, innovs = [], []
        for n in range(entries):
            name = lists[t, n]
            if n == 0:
                src, aux, block = below, below_aux, name
            elif n == 1:
                src, aux, block = above, above_aux, name - 2 * blocks
            else:
                src, aux, block = own, own_aux, name - blocks
            for q, u in enumerate(order):
                start = 0 if len(order) == 1 else pl.multiple_of((me ^ u) * rows, rows)
                pert_buf[t, q * rows:(q + 1) * rows, n * slots:(n + 1) * slots] = src[
                    block, pl.ds(start, rows), :
                ]
            weights.append(aux[block, t:t + 1, :])
            innovs.append(aux[block, tiles:tiles + 1, :])
        pert = pert_buf[t]
        weight = jnp.concatenate(weights, axis=1)
        innov = jnp.concatenate(innovs, axis=1)
        scaled = (pert.astype(jnp.float32) * weight).astype(jnp.bfloat16)
        precision = (members - 1) * eye + lax.dot_general(
            pert, scaled, contract_last, preferred_element_type=jnp.float32
        )
        drive = lax.dot_general(
            jnp.broadcast_to(innov, (8, innov.shape[1])).astype(jnp.bfloat16),
            scaled,
            contract_last,
            preferred_element_type=jnp.float32,
        )
        square = jnp.sum(precision * precision, axis=0, keepdims=True)
        norm = jnp.sqrt(jnp.sum(square, axis=1, keepdims=True))
        state.append((precision / norm, drive, norm))
    currents = [s[0] for s in state]
    roots = [None] * tiles
    for sweep in range(NS_ITERS):
        for t in range(tiles):
            current = split(currents[t])
            if sweep == 0:
                factor = 1.5 * eye - 0.5 * currents[t]
            else:
                factor = 1.5 * eye - 0.5 * dot3(current, split(roots[t]))
            both = split(factor)
            if sweep < NS_ITERS - 1:
                currents[t] = dot3(both, current)
            roots[t] = factor if sweep == 0 else dot3(split(roots[t]), both)
    for t in range(tiles):
        _, drive, norm = state[t]
        root = split(roots[t])
        inner = dot3(split(drive), root)
        gain = dot3(split(inner), root) / norm
        scale = jnp.sqrt((members - 1) / norm)
        final = (scale * roots[t] + gain[0:1, :]).astype(jnp.bfloat16)
        mix[t] = final
        left = 1.0 - jnp.sum(final.astype(jnp.float32), axis=1, keepdims=True)
        rest[t] = jnp.broadcast_to(left, rest.shape[1:])


def turn_in(piece, t, buf):
    rows, _, depth, points = piece.shape
    field = piece[:, t].astype(jnp.float32)
    buf[...] = field.reshape(rows * depth, points)
    turned = jnp.concatenate(
        [buf[pl.ds(level, rows, stride=depth), :] for level in range(depth)], axis=1
    )
    return turned.astype(jnp.bfloat16), jnp.sum(field, axis=0)


def gather_kernel(*refs):
    pieces, (fields, total, bufs) = refs[:-3], refs[-3:]
    rows = pieces[0].shape[0]
    for t in range(fields.shape[0]):
        acc = jnp.zeros(total.shape[1:], jnp.float32)
        for q, piece in enumerate(pieces):
            turned, part = turn_in(piece, t, bufs.at[(t * len(pieces) + q) % bufs.shape[0]])
            fields[t, q * rows:(q + 1) * rows, :] = turned
            acc += part
        total[t] = acc


def combine(t, mix, rest, field, mean, sent, first):
    _, depth, rows, points = sent[0].shape
    count = len(sent) * rows
    result = jnp.dot(
        mix[t, first:first + count, :], field, preferred_element_type=jnp.float32
    )
    for level in range(depth):
        part = result[:, level * points:(level + 1) * points]
        part = part + rest[t, first:first + count, :] * mean[level:level + 1, :]
        part = part.astype(jnp.bfloat16)
        for v, out in enumerate(sent):
            out[t, level] = part[v * rows:(v + 1) * rows, :]


def first_kernel(late, first, mix, rest, fields, total, *refs):
    pieces, sent = refs[:late], refs[late:-3]
    late_fields, mean_out, bufs = refs[-3:]
    tiles, members, _ = mix.shape
    rows = pieces[0].shape[0]
    for t in range(tiles):
        acc = total[t]
        turned = [fields[t]]
        for q, piece in enumerate(pieces):
            part, add = turn_in(piece, t, bufs.at[t * late + q])
            late_fields[t, q * rows:(q + 1) * rows, :] = part
            turned.append(part)
            acc += add
        mean = acc / members
        mean_out[t] = mean
        combine(t, mix, rest, jnp.concatenate(turned, axis=0), mean, sent, first)


def second_kernel(mix, rest, fields, late_fields, mean, *sent):
    for t in range(mix.shape[0]):
        field = jnp.concatenate([fields[t], late_fields[t]], axis=0)
        combine(t, mix, rest, field, mean[t], sent, 0)


def place_kernel(order, aliased, spot, *refs):
    pieces = refs[:len(order)]
    result, turned, buf, sems = refs[len(order) + aliased:]
    tiles, depth, rows, points = pieces[0].shape
    copies = []
    for q, (u, piece) in enumerate(zip(order, pieces)):
        for t in range(tiles):
            view = buf.at[(q * tiles + t) % buf.shape[0]]
            for level in range(depth):
                view[pl.ds(level, rows, stride=depth), :] = piece[t, level].astype(jnp.float32)
            turned[q, :, t] = view[...].reshape(rows, depth, points).astype(jnp.bfloat16)
        copy = pltpu.make_async_copy(turned.at[q], result.at[:, spot[0] ^ u], sems.at[q])
        copy.start()
        copies.append(copy)
    for copy in copies:
        copy.wait()


def neighbours(x, axis):
    peers = lax.axis_size(axis)
    if peers == 1:
        return x, x
    if peers == 2:
        other = lax.ppermute(x, axis, [(0, 1), (1, 0)])
        return other, other
    up = [(i, i + 1) for i in range(peers - 1)]
    return lax.ppermute(x, axis, up), lax.ppermute(x, axis, [(j, i) for i, j in up])


def send_order(wide):
    far = list(range(wide // 2, wide))
    half = len(far) // 2
    return [s for pair in zip(far[half:], far[:half]) for s in pair], list(range(1, wide // 2))


def on_device(
    prior_states,
    measured_anomalies,
    departures,
    error_precisions,
    datum_totals,
    datum_patch_owner,
    patch_group_lookup,
):
    wide = lax.axis_size("wide")
    bands = lax.axis_size("band")
    me = lax.axis_index("wide").astype(jnp.int32)
    direct = wide <= DIRECT_MAX
    mine, _, _, depth, points = prior_states.shape
    blocks, members, slots = measured_anomalies.shape[1:]
    tiles, entries = patch_group_lookup.shape[1:]
    fields = prior_states.reshape(mine, wide, tiles, depth, points)
    vmem = pl.BlockSpec(memory_space=pltpu.VMEM)
    smem = pl.BlockSpec(memory_space=pltpu.SMEM)

    def call(kernel, out_shape, in_specs, scratch, limit, **more):
        out_specs = more.pop("out_specs", jax.tree.map(lambda _: vmem, out_shape))
        return pl.pallas_call(
            kernel,
            out_shape=out_shape,
            in_specs=in_specs,
            out_specs=out_specs,
            scratch_shapes=scratch,
            compiler_params=pltpu.CompilerParams(vmem_limit_bytes=limit * MIB),
            **more,
        )

    def swap(x, s):
        return lax.ppermute(x, "wide", [(i, i ^ s) for i in range(wide)])

    if direct:
        far, near_by = send_order(wide)
        arrived = {}
        left = fields
        for group in (far[:2], far[2:], near_by + [0]):
            parts = [lax.dynamic_index_in_dim(left, me ^ s, 1, keepdims=False) for s in group]
            left, *parts = lax.optimization_barrier((left, *parts))
            for s, part in zip(group, parts):
                if s == 0:
                    arrived[0] = part
                    continue
                arrived[s] = swap(part, s)
        late = far[-1:-2 * LATE:-2]
        early = [0] + near_by + [s for s in far if s not in late]
        order = early + late
    else:
        order = [0]

    slot_index = jnp.arange(slots, dtype=jnp.int32)
    live = jnp.where(slot_index[None, :] < datum_totals[0][:, None], 1.0, 0.0)
    base = error_precisions[0].astype(jnp.float32) * live
    tile_ids = jnp.arange(tiles, dtype=jnp.int32)
    near = jnp.where(datum_patch_owner[0][:, None, :] == tile_ids[None, :, None], 1.0, LOC_FAR)
    pad = -(tiles + 1) % 8
    aux = jnp.concatenate(
        [
            base[:, None, :] * near,
            departures[0][:, None, :].astype(jnp.float32),
            jnp.zeros((blocks, pad, slots), jnp.float32),
        ],
        axis=1,
    )
    below, above = neighbours(measured_anomalies[0], "band")
    below_aux, above_aux = neighbours(aux, "band")
    band = lax.axis_index("band")
    below_aux = jnp.where(band > 0, below_aux, 0.0)
    above_aux = jnp.where(band < bands - 1, above_aux, 0.0)

    mix, rest = call(
        functools.partial(mix_kernel, order),
        [
            jax.ShapeDtypeStruct((tiles, members, members), jnp.bfloat16),
            jax.ShapeDtypeStruct((tiles, members, points), jnp.float32),
        ],
        [smem, smem] + [vmem] * 6,
        [pltpu.VMEM((tiles, members, entries * slots), jnp.bfloat16)],
        24,
    )(
        patch_group_lookup[0],
        me.reshape(1),
        measured_anomalies[0],
        below,
        above,
        aux,
        below_aux,
        above_aux,
    )

    if not direct:
        whole = lax.all_to_all(fields, "wide", split_axis=1, concat_axis=0, tiled=True)
        flat = whole.reshape(members, tiles, depth * points)
        mean = jnp.sum(flat, axis=0, dtype=jnp.float32) / members
        spread = (flat.astype(jnp.float32) - mean).astype(jnp.bfloat16)
        result = mean + jnp.einsum("tkj,jtp->ktp", mix, spread, preferred_element_type=jnp.float32)
        back = lax.all_to_all(
            result.astype(jnp.bfloat16).reshape(wide, mine, tiles, depth, points),
            "wide",
            split_axis=0,
            concat_axis=2,
            tiled=True,
        )
        return back.reshape(prior_states.shape)

    width = depth * points
    count = len(early) * mine
    gathered, total = call(
        gather_kernel,
        [
            jax.ShapeDtypeStruct((tiles, count, width), jnp.bfloat16),
            jax.ShapeDtypeStruct((tiles, depth, points), jnp.float32),
        ],
        [vmem] * len(early),
        [pltpu.VMEM((8, mine * depth, points), jnp.float32)],
        12,
    )(*[arrived[s] for s in early])
    piece = jax.ShapeDtypeStruct((tiles, depth, mine, points), jnp.bfloat16)
    close = len(near_by) + 1
    *sent_far, late_fields, mean = call(
        functools.partial(first_kernel, len(late), close * mine),
        [piece] * (len(order) - close)
        + [
            jax.ShapeDtypeStruct((tiles, len(late) * mine, width), jnp.bfloat16),
            jax.ShapeDtypeStruct((tiles, depth, points), jnp.float32),
        ],
        [vmem] * (4 + len(late)),
        [pltpu.VMEM((tiles * len(late), mine * depth, points), jnp.float32)],
        12,
    )(mix, rest, gathered, total, *[arrived[s] for s in late])
    sent_near = call(
        second_kernel, [piece] * close, [vmem] * 5, [], 12
    )(mix, rest, gathered, late_fields, mean)
    sent = dict(zip(order, list(sent_near) + sent_far))
    back = {0: sent[0]}
    for s in far + near_by:
        back[s] = swap(sent[s], s)

    result = jax.ShapeDtypeStruct((mine, wide, tiles, depth, points), jnp.bfloat16)
    hbm = pl.BlockSpec(memory_space=pl.ANY)

    def place(group, *rest):
        return call(
            functools.partial(place_kernel, group, len(rest)),
            result,
            [smem] + [vmem] * len(group) + [hbm] * len(rest),
            [
                pltpu.VMEM((len(group), mine, tiles, depth, points), jnp.bfloat16),
                pltpu.VMEM((4, mine * depth, points), jnp.float32),
                pltpu.SemaphoreType.DMA((len(group),)),
            ],
            12,
            out_specs=hbm,
            input_output_aliases={1 + len(group): 0} if rest else {},
        )(me.reshape(1), *[back[s] for s in group], *rest)

    most = place(early)
    return place(late, most).reshape(prior_states.shape)


def solution(mesh):
    in_specs = (
        P("wide", "band", None, None, None),
        P("band", "wide", None, None),
        P("band", "wide", None),
        P("band", "wide", None),
        P("band", "wide"),
        P("band", "wide", None),
        P("band", "wide", None),
    )
    out_specs = P("wide", "band", None, None, None)
    return jax.shard_map(
        on_device, mesh=mesh, in_specs=in_specs, out_specs=out_specs, check_vma=False
    )
```

time: 141 us -> 139 us (0.986)
  waiting for transfers between devices: 30.1 us -> 50.4 us
  starting transfers between devices: 84.8 us -> 65.7 us
  Pallas kernels: 17.7 us -> 15.1 us
  local copies, waits for them, and re-layouts: 6.55 us -> 4.73 us
  other arithmetic: 0.76 us -> 2.35 us
    ppermute x30, waiting for transfers between devices: 30.1 us -> 50.4 us  [swap(): return lax.ppermute(x, 'wide', [(i, i ^ s) for i in range(wide)])]
    ppermute x30, starting transfers between devices: 84.8 us -> 65.2 us  [swap(): return lax.ppermute(x, 'wide', [(i, i ^ s) for i in range(wide)])]
    pallas_call x2 -> x6, Pallas kernels: 17.7 us -> 15.1 us  [the longest x1 11 us: on_device(): call(functools.partial(mix_kernel, order), [jax.ShapeDtypeStruct((tiles,...]
    unnamed x68 -> x6, local copies, waits for them, and re-layouts: 2.4 us -> 0.01 us
    squeeze x1 -> x3, local copies, waits for them, and re-layouts: 2.82 us -> 4.64 us  [on_device(): lax.dynamic_index_in_dim(left, me ^ s, 1, keepdims=False)]
  transfers between devices with their start and end apart: 32 -> 32, of which waited for: 10 -> 8; matrix products, arithmetic and copies ran while one was open for 1% -> 3% of each run, Pallas kernels for 9% -> 10%
where the time goes in v2:
time: 139 us; the launch traced here: 138 us
  starting transfers between devices  65.7 us (47%)
  waiting for transfers between devices  50.4 us (36%)
  Pallas kernels  15.1 us (11%)
  local copies, waits for them, and re-layouts  4.73 us (3%)
  other arithmetic  2.35 us (2%)
    ppermute x30, starting transfers between devices, swap(): return lax.ppermute(x, 'wide', [(i, i ^ s) for i in range(wide)])  65.2 us
    ppermute x30, waiting for transfers between devices, swap(): return lax.ppermute(x, 'wide', [(i, i ^ s) for i in range(wide)])  50.4 us
    pallas_call x1, Pallas kernels, on_device(): call(functools.partial(mix_kernel, order), [jax.ShapeDtypeStruct((tiles,...  11 us
    squeeze x3, local copies, waits for them, and re-layouts, on_device(): lax.dynamic_index_in_dim(left, me ^ s, 1, keepdims=False)  4.64 us
  transfers between devices with their start and end apart: 32, of which 8 were waited for; matrix products, arithmetic and copies ran while one was open for 3% of the time, Pallas kernels for 10%

profile of v2, /device:TPU:0, one launch (start us, length us, event | category | flops | bytes accessed | tf_op | source)
XLA Modules:
  0.0 138.4 jit_solution(11395864029249375144)
XLA Ops:
  0.0 0.8 convert_element_type.29
  0.8 0.1 pad.2.clone
  0.9 0.8 convert_multiply_fusion
  1.7 0.7 select_multiply_fusion
  2.4 0.1 maximum_maximum_fusion.own_aux
  2.4 0.5 collective-permute-start.1
  2.9 1.7 %dynamic-slice_bitcast_fusion.14 = (bf16[16,4,8,128]{3,2,1,0:T(8,128)(2,1)}, bf16[16,4,8,128]{3,2,1,0:T(8,128)(2,1)S(1)}) fusion(bf16[16,16,4,8,128]{4,3,2,1,0:T(8,128)(2,1)} %bitcast.52, s32[]{:T(128)S(6)} %select_n.82, s32[]{:T(128)S(6)} %select_n.81), kind=kLoop, calls=%fused_computation.14 | loop fusion | bytes 524296 | tf_op jit(solution)/shard_map/jit(dynamic_index_in_dim)/squeeze | solution.py:235
  4.6 4.6 %collective-permute-start.9 = (bf16[16,4,8,128]{3,2,1,0:T(8,128)(2,1)S(1)}, bf16[16,4,8,128]{3,2,1,0:T(8,128)(2,1)S(1)}, u32[]{:S(2)}, u32[]{:S(2)}) collective-permute-start(bf16[16,4,8,128]{3,2,1,0:T(8,128)(2,1)S(1)} %get-tuple-element.57), channel_id=1, source_target_pairs={{0,24},{2,26},{4,28},{6,30},{8,16},{10,18},{12,20},{14,22},{16,8},... | collective-permute-start | bytes 393224 | tf_op jit(solution)/shard_map/ppermute | solution.py:228
  9.2 0.0 collective-permute-start.10
  9.3 2.1 %dynamic-slice_bitcast_fusion.8 = (bf16[16,4,8,128]{3,2,1,0:T(8,128)(2,1)}, bf16[16,4,8,128]{3,2,1,0:T(8,128)(2,1)}, bf16[16,4,8,128]{3,2,1,0:T(8,128)(2,1)}, bf...) fusion(s32[]{:T(128)S(6)} %select_n.88, s32[]{:T(128)S(6)} %select_n.87, ...), kind=kLoop, calls=%fused_computation.8 | loop fusion | bytes 1572888 | tf_op jit(solution)/shard_map/jit(dynamic_index_in_dim)/squeeze | solution.py:235
  11.4 2.8 %collective-permute-start.11 = (bf16[16,4,8,128]{3,2,1,0:T(8,128)(2,1)}, bf16[16,4,8,128]{3,2,1,0:T(8,128)(2,1)S(1)}, u32[]{:S(2)}, u32[]{:S(2)}) collective-permute-start(bf16[16,4,8,128]{3,2,1,0:T(8,128)(2,1)} %get-tuple-element.59), channel_id=1, source_target_pairs={{0,26},{2,24},{4,30},{6,28},{8,18},{10,16},{12,22},{14,20},{16,10}... | collective-permute-start | bytes 393224 | tf_op jit(solution)/shard_map/ppermute | solution.py:228
  14.2 1.1 collective-permute-start.12
  15.3 0.0 collective-permute-done.1
  15.3 3.8 %collective-permute-start.13 = (bf16[16,4,8,128]{3,2,1,0:T(8,128)(2,1)}, bf16[16,4,8,128]{3,2,1,0:T(8,128)(2,1)S(1)}, u32[]{:S(2)}, u32[]{:S(2)}) collective-permute-start(bf16[16,4,8,128]{3,2,1,0:T(8,128)(2,1)} %get-tuple-element.61), channel_id=1, source_target_pairs={{0,28},{2,30},{4,24},{6,26},{8,20},{10,22},{12,16},{14,18},{16,12}... | collective-permute-start | bytes 393224 | tf_op jit(solution)/shard_map/ppermute | solution.py:228
  19.1 0.0 collective-permute-done.9.refs_8_
  19.1 1.1 collective-permute-start.14
  20.2 0.8 dynamic-slice_bitcast_fusion
  21.0 11.7 %collective-permute-done.10.refs_9_ = bf16[16,4,8,128]{3,2,1,0:T(8,128)(2,1)S(1)} collective-permute-done((bf16[16,4,8,128]{3,2,1,0:T(8,128)(2,1)}, bf16[16,4,8,128]{3,2,1,0:T(8,128)(2,1)S(1)}, u32[]{:S(2)}, u32[]{:S(2)}) %collective-permute-start.10) | collective-permute-done | bytes 131104 | tf_op jit(solution)/shard_map/ppermute | solution.py:228
  32.7 1.5 %collective-permute-start.2 = (bf16[16,4,8,128]{3,2,1,0:T(8,128)(2,1)S(1)}, bf16[16,4,8,128]{3,2,1,0:T(8,128)(2,1)S(1)}, u32[]{:S(2)}, u32[]{:S(2)}) collective-permute-start(bf16[16,4,8,128]{3,2,1,0:T(8,128)(2,1)S(1)} %get-tuple-element.50), channel_id=1, source_target_pairs={{0,2},{2,0},{4,6},{6,4},{8,10},{10,8},{12,14},{14,12},{16,18},{18,... | collective-permute-start | bytes 393224 | tf_op jit(solution)/shard_map/ppermute | solution.py:228
  34.2 1.5 %collective-permute-start.3 = (bf16[16,4,8,128]{3,2,1,0:T(8,128)(2,1)}, bf16[16,4,8,128]{3,2,1,0:T(8,128)(2,1)S(1)}, u32[]{:S(2)}, u32[]{:S(2)}) collective-permute-start(bf16[16,4,8,128]{3,2,1,0:T(8,128)(2,1)} %get-tuple-element.51), channel_id=1, source_target_pairs={{0,4},{2,6},{4,0},{6,2},{8,12},{10,14},{12,8},{14,10},{16,20},{18,... | collective-permute-start | bytes 393224 | tf_op jit(solution)/shard_map/ppermute | solution.py:228
  35.7 3.5 %collective-permute-done.12.refs_11_ = bf16[16,4,8,128]{3,2,1,0:T(8,128)(2,1)S(1)} collective-permute-done((bf16[16,4,8,128]{3,2,1,0:T(8,128)(2,1)}, bf16[16,4,8,128]{3,2,1,0:T(8,128)(2,1)S(1)}, u32[]{:S(2)}, u32[]{:S(2)}) %collective-permute-start.12) | collective-permute-done | bytes 131104 | tf_op jit(solution)/shard_map/ppermute | solution.py:228
  39.2 1.5 %collective-permute-start.4 = (bf16[16,4,8,128]{3,2,1,0:T(8,128)(2,1)}, bf16[16,4,8,128]{3,2,1,0:T(8,128)(2,1)S(1)}, u32[]{:S(2)}, u32[]{:S(2)}) collective-permute-start(bf16[16,4,8,128]{3,2,1,0:T(8,128)(2,1)} %get-tuple-element.52), channel_id=1, source_target_pairs={{0,6},{2,4},{4,2},{6,0},{8,14},{10,12},{12,10},{14,8},{16,22},{18,... | collective-permute-start | bytes 393224 | tf_op jit(solution)/shard_map/ppermute | solution.py:228
  40.7 0.0 collective-permute-done.13.refs_12_
  40.7 2.8 %collective-permute-start.5 = (bf16[16,4,8,128]{3,2,1,0:T(8,128)(2,1)}, bf16[16,4,8,128]{3,2,1,0:T(8,128)(2,1)S(1)}, u32[]{:S(2)}, u32[]{:S(2)}) collective-permute-start(bf16[16,4,8,128]{3,2,1,0:T(8,128)(2,1)} %get-tuple-element.53), channel_id=1, source_target_pairs={{0,8},{2,10},{4,12},{6,14},{8,0},{10,2},{12,4},{14,6},{16,24},{18,... | collective-permute-start | bytes 393224 | tf_op jit(solution)/shard_map/ppermute | solution.py:228
  43.5 3.4 %collective-permute-start.6 = (bf16[16,4,8,128]{3,2,1,0:T(8,128)(2,1)}, bf16[16,4,8,128]{3,2,1,0:T(8,128)(2,1)S(1)}, u32[]{:S(2)}, u32[]{:S(2)}) collective-permute-start(bf16[16,4,8,128]{3,2,1,0:T(8,128)(2,1)} %get-tuple-element.54), channel_id=1, source_target_pairs={{0,10},{2,8},{4,14},{6,12},{8,2},{10,0},{12,6},{14,4},{16,26},{18,... | collective-permute-start | bytes 393224 | tf_op jit(solution)/shard_map/ppermute | solution.py:228
  46.9 0.0 collective-permute-start
  47.0 5.1 %collective-permute-start.15 = (bf16[16,4,8,128]{3,2,1,0:T(8,128)(2,1)}, bf16[16,4,8,128]{3,2,1,0:T(8,128)(2,1)S(1)}, u32[]{:S(2)}, u32[]{:S(2)}) collective-permute-start(bf16[16,4,8,128]{3,2,1,0:T(8,128)(2,1)} %get-tuple-element.65), channel_id=1, source_target_pairs={{0,22},{2,20},{4,18},{6,16},{8,30},{10,28},{12,26},{14,24},{16,6},... | collective-permute-start | bytes 393224 | tf_op jit(solution)/shard_map/ppermute | solution.py:228
  52.0 0.0 collective-permute-start.16
  52.0 0.0 collective-permute-done.5.refs_4_
  52.0 2.8 %collective-permute-start.7 = (bf16[16,4,8,128]{3,2,1,0:T(8,128)(2,1)}, bf16[16,4,8,128]{3,2,1,0:T(8,128)(2,1)S(1)}, u32[]{:S(2)}, u32[]{:S(2)}) collective-permute-start(bf16[16,4,8,128]{3,2,1,0:T(8,128)(2,1)} %get-tuple-element.55), channel_id=1, source_target_pairs={{0,12},{2,14},{4,8},{6,10},{8,4},{10,6},{12,0},{14,2},{16,28},{18,... | collective-permute-start | bytes 393224 | tf_op jit(solution)/shard_map/ppermute | solution.py:228
  54.8 0.6 collective-permute-start.8
  55.4 10.0 %collective-permute-done.7.refs_6_ = bf16[16,4,8,128]{3,2,1,0:T(8,128)(2,1)S(1)} collective-permute-done((bf16[16,4,8,128]{3,2,1,0:T(8,128)(2,1)}, bf16[16,4,8,128]{3,2,1,0:T(8,128)(2,1)S(1)}, u32[]{:S(2)}, u32[]{:S(2)}) %collective-permute-start.7) | collective-permute-done | bytes 131104 | tf_op jit(solution)/shard_map/ppermute | solution.py:228
  65.4 0.5 collective-permute-done.8.refs_7_
  66.0 0.8 shard_map.74
  66.8 11.0 %shard_map.73 = (bf16[4,256,256]{2,1,0:T(8,128)(2,1)S(1)}, f32[4,256,128]{2,1,0:T(8,128)S(1)}) custom-call(s32[4,4]{1,0:T(4,128)S(1)} %bitcast.51, s32[1]{0:T(128)} %bitcast.spot, bf16[4,256,128]{2,1,0:T(8,128)(2,1)S(1)} %bitcast.50, bf16[4,256,128]{2,1,0:T(8,128)(2,1)S(1)} %collective-permute-done.below.above, ...), custom_call_target="tpu_custom_call" | custom-call | tf_op jit(solution)/shard_map/pallas_call | solution.py:268
  77.8 0.5 shard_map.75
  78.3 0.5 shard_map.76
  78.8 2.5 %collective-permute-start.19 = (bf16[4,8,16,128]{3,2,1,0:T(8,128)(2,1)S(1)}, bf16[4,8,16,128]{3,2,1,0:T(8,128)(2,1)S(1)}, u32[]{:S(2)}, u32[]{:S(2)}) collective-permute-start(bf16[4,8,16,128]{3,2,1,0:T(8,128)(2,1)S(1)} %get-tuple-element.72), channel_id=1, source_target_pairs={{0,2},{2,0},{4,6},{6,4},{8,10},{10,8},{12,14},{14,12},{16,18},{18,... | collective-permute-start | bytes 393224 | tf_op jit(solution)/shard_map/ppermute | solution.py:228
  81.3 1.5 %collective-permute-start.21 = (bf16[4,8,16,128]{3,2,1,0:T(8,128)(2,1)S(1)}, bf16[4,8,16,128]{3,2,1,0:T(8,128)(2,1)S(1)}, u32[]{:S(2)}, u32[]{:S(2)}) collective-permute-start(bf16[4,8,16,128]{3,2,1,0:T(8,128)(2,1)S(1)} %get-tuple-element.74), channel_id=1, source_target_pairs={{0,6},{2,4},{4,2},{6,0},{8,14},{10,12},{12,10},{14,8},{16,22},{18,... | collective-permute-start | bytes 393224 | tf_op jit(solution)/shard_map/ppermute | solution.py:228
  82.8 0.1 collective-permute-start.22
  82.9 3.3 %collective-permute-start.23 = (bf16[4,8,16,128]{3,2,1,0:T(8,128)(2,1)S(1)}, bf16[4,8,16,128]{3,2,1,0:T(8,128)(2,1)S(1)}, u32[]{:S(2)}, u32[]{:S(2)}) collective-permute-start(bf16[4,8,16,128]{3,2,1,0:T(8,128)(2,1)S(1)} %get-tuple-element.76), channel_id=1, source_target_pairs={{0,10},{2,8},{4,14},{6,12},{8,2},{10,0},{12,6},{14,4},{16,26},{18,... | collective-permute-start | bytes 393224 | tf_op jit(solution)/shard_map/ppermute | solution.py:228
  86.2 0.0 collective-permute-done.19.refs_1_
  86.2 0.2 collective-permute-start.24
  86.4 3.0 %collective-permute-done.20.refs_2_ = bf16[4,8,16,128]{3,2,1,0:T(8,128)(2,1)S(1)} collective-permute-done((bf16[4,8,16,128]{3,2,1,0:T(8,128)(2,1)S(1)}, bf16[4,8,16,128]{3,2,1,0:T(8,128)(2,1)S(1)}, u32[]{:S(2)}, u32[]{:S(2)}) %collective-permute-start.20) | collective-permute-done | bytes 131104 | tf_op jit(solution)/shard_map/ppermute | solution.py:228
  89.3 1.6 %collective-permute-start.25 = (bf16[4,8,16,128]{3,2,1,0:T(8,128)(2,1)S(1)}, bf16[4,8,16,128]{3,2,1,0:T(8,128)(2,1)S(1)}, u32[]{:S(2)}, u32[]{:S(2)}) collective-permute-start(bf16[4,8,16,128]{3,2,1,0:T(8,128)(2,1)S(1)} %get-tuple-element.78), channel_id=1, source_target_pairs={{0,14},{2,12},{4,10},{6,8},{8,6},{10,4},{12,2},{14,0},{16,30},{18,... | collective-permute-start | bytes 393224 | tf_op jit(solution)/shard_map/ppermute | solution.py:228
  90.9 2.9 %collective-permute-start.26 = (bf16[4,8,16,128]{3,2,1,0:T(8,128)(2,1)S(1)}, bf16[4,8,16,128]{3,2,1,0:T(8,128)(2,1)S(1)}, u32[]{:S(2)}, u32[]{:S(2)}) collective-permute-start(bf16[4,8,16,128]{3,2,1,0:T(8,128)(2,1)S(1)} %get-tuple-element.79), channel_id=1, source_target_pairs={{0,24},{2,26},{4,28},{6,30},{8,16},{10,18},{12,20},{14,22},{16,8},... | collective-permute-start | bytes 393224 | tf_op jit(solution)/shard_map/ppermute | solution.py:228
  93.8 0.0 collective-permute-done.23.refs_5_
  93.8 3.4 %collective-permute-start.28 = (bf16[4,8,16,128]{3,2,1,0:T(8,128)(2,1)S(1)}, bf16[4,8,16,128]{3,2,1,0:T(8,128)(2,1)S(1)}, u32[]{:S(2)}, u32[]{:S(2)}) collective-permute-start(bf16[4,8,16,128]{3,2,1,0:T(8,128)(2,1)S(1)} %get-tuple-element.81), channel_id=1, source_target_pairs={{0,26},{2,24},{4,30},{6,28},{8,18},{10,16},{12,22},{14,20},{16,10}... | collective-permute-start | bytes 393224 | tf_op jit(solution)/shard_map/ppermute | solution.py:228
  97.3 0.0 collective-permute-done.24.refs_6_
  97.3 1.7 %collective-permute-start.29 = (bf16[4,8,16,128]{3,2,1,0:T(8,128)(2,1)S(1)}, bf16[4,8,16,128]{3,2,1,0:T(8,128)(2,1)S(1)}, u32[]{:S(2)}, u32[]{:S(2)}) collective-permute-start(bf16[4,8,16,128]{3,2,1,0:T(8,128)(2,1)S(1)} %get-tuple-element.82), channel_id=1, source_target_pairs={{0,18},{2,16},{4,22},{6,20},{8,26},{10,24},{12,30},{14,28},{16,2},... | collective-permute-start | bytes 393224 | tf_op jit(solution)/shard_map/ppermute | solution.py:228
  98.9 0.0 collective-permute-done.25.refs_7_
  99.0 7.0 %collective-permute-start.30 = (bf16[4,8,16,128]{3,2,1,0:T(8,128)(2,1)S(1)}, bf16[4,8,16,128]{3,2,1,0:T(8,128)(2,1)S(1)}, u32[]{:S(2)}, u32[]{:S(2)}) collective-permute-start(bf16[4,8,16,128]{3,2,1,0:T(8,128)(2,1)S(1)} %get-tuple-element.83), channel_id=1, source_target_pairs={{0,28},{2,30},{4,24},{6,26},{8,20},{10,22},{12,16},{14,18},{16,12}... | collective-permute-start | bytes 393224 | tf_op jit(solution)/shard_map/ppermute | solution.py:228
  106.0 0.0 collective-permute-done.26.refs_8_
  106.0 0.0 collective-permute-start.31
  106.0 10.3 %collective-permute-done.27.refs_9_ = bf16[4,8,16,128]{3,2,1,0:T(8,128)(2,1)S(1)} collective-permute-done((bf16[4,8,16,128]{3,2,1,0:T(8,128)(2,1)S(1)}, bf16[4,8,16,128]{3,2,1,0:T(8,128)(2,1)S(1)}, u32[]{:S(2)}, u32[]{:S(2)}) %collective-permute-start.27) | collective-permute-done | bytes 131104 | tf_op jit(solution)/shard_map/ppermute | solution.py:228
  116.3 1.4 collective-permute-start.17
  117.7 0.0 collective-permute-done.28.refs_10_
  117.7 7.0 %collective-permute-start.18 = (bf16[4,8,16,128]{3,2,1,0:T(8,128)(2,1)S(1)}, bf16[4,8,16,128]{3,2,1,0:T(8,128)(2,1)S(1)}, u32[]{:S(2)}, u32[]{:S(2)}) collective-permute-start(bf16[4,8,16,128]{3,2,1,0:T(8,128)(2,1)S(1)} %get-tuple-element.68), channel_id=1, source_target_pairs={{0,20},{2,22},{4,16},{6,18},{8,28},{10,30},{12,24},{14,26},{16,4},... | collective-permute-start | bytes 393224 | tf_op jit(solution)/shard_map/ppermute | solution.py:228
  124.7 1.1 collective-permute-done.29.refs_11_
  125.8 0.0 collective-permute-done.30.refs_12_
  125.8 1.6 %shard_map.77.refs_2_ = bf16[16,16,4,8,128]{4,3,2,1,0:T(8,128)(2,1)} custom-call(s32[1]{0:T(128)} %bitcast.spot, bf16[4,8,16,128]{3,2,1,0:T(8,128)(2,1)S(1)} %get-tuple-element.71.refs_0_, bf16[4,8,16,128]{3,2,1,0:T(8,128)(2,1)S(1)} %collective-permute-done.19.refs_1_, bf16[4,8,16,128]{3,2,1,0:T(8,128)(2,1)S(1)} %collective-permute-done.20.refs_2_, ...), custom_call_target="tpu_custom_call" | custom-call | tf_op jit(solution)/shard_map/pallas_call | solution.py:340
  127.5 10.1 %collective-permute-done.17.refs_0_ = bf16[4,8,16,128]{3,2,1,0:T(8,128)(2,1)S(1)} collective-permute-done((bf16[4,8,16,128]{3,2,1,0:T(8,128)(2,1)S(1)}, bf16[4,8,16,128]{3,2,1,0:T(8,128)(2,1)S(1)}, u32[]{:S(2)}, u32[]{:S(2)}) %collective-permute-start.17) | collective-permute-done | bytes 131104 | tf_op jit(solution)/shard_map/ppermute | solution.py:228
  137.6 0.0 collective-permute-done.18.refs_1_
  137.6 0.8 shard_map.78
  (22 shorter events, 0.1 us)
Async XLA Ops:
  0.0 20.2 %copy-start.2 = (bf16[16,1,64,8,128]{4,3,2,1,0:T(8,128)(2,1)S(1)}, bf16[16,1,64,8,128]{4,3,2,1,0:T(8,128)(2,1)}, u32[]{:S(2)}) copy-start(bf16[16,1,64,8,128]{4,3,2,1,0:T(8,128)(2,1)} %param.7) | copy-start | bytes 6291460
  2.4 12.9 %collective-permute-start.1 = (f32[4,8,128]{2,1,0:T(8,128)S(1)}, f32[4,8,128]{2,1,0:T(8,128)S(1)}, u32[]{:S(2)}, u32[]{:S(2)}) collective-permute-start(f32[4,8,128]{2,1,0:T(8,128)S(1)} %maximum_maximum_fusion.own_aux), channel_id=1, source_target_pairs={{0,1},{1,0},{2,3},{3,2},{4,5},{5,4},{6,7},{7,6},{8,9},{9,8},{10,11... | collective-permute-start | bytes 49160 | tf_op jit(solution)/shard_map/ppermute | solution.py:183
  2.9 44.0 %copy-start = (bf16[1,4,256,128]{3,2,1,0:T(8,128)(2,1)S(1)}, bf16[1,4,256,128]{3,2,1,0:T(8,128)(2,1)}, u32[]{:S(2)}) copy-start(bf16[1,4,256,128]{3,2,1,0:T(8,128)(2,1)} %param.8) | copy-start | bytes 786436
  4.6 14.5 %collective-permute-start.9 = (bf16[16,4,8,128]{3,2,1,0:T(8,128)(2,1)S(1)}, bf16[16,4,8,128]{3,2,1,0:T(8,128)(2,1)S(1)}, u32[]{:S(2)}, u32[]{:S(2)}) collective-permute-start(bf16[16,4,8,128]{3,2,1,0:T(8,128)(2,1)S(1)} %get-tuple-element.57), channel_id=1, source_target_pairs={{0,24},{2,26},{4,28},{6,30},{8,16},{10,18},{12,20},{14,22},{16,8},... | collective-permute-start | bytes 393224 | tf_op jit(solution)/shard_map/ppermute | solution.py:228
  9.2 23.4 %collective-permute-start.10 = (bf16[16,4,8,128]{3,2,1,0:T(8,128)(2,1)}, bf16[16,4,8,128]{3,2,1,0:T(8,128)(2,1)S(1)}, u32[]{:S(2)}, u32[]{:S(2)}) collective-permute-start(bf16[16,4,8,128]{3,2,1,0:T(8,128)(2,1)} %get-tuple-element.58), channel_id=1, source_target_pairs={{0,16},{2,18},{4,20},{6,22},{8,24},{10,26},{12,28},{14,30},{16,0},... | collective-permute-start | bytes 393224 | tf_op jit(solution)/shard_map/ppermute | solution.py:228
  11.4 55.4 %copy-start.1 = (s32[1,4,4]{2,1,0:T(4,128)S(1)}, s32[1,4,4]{2,1,0:T(4,128)}, u32[]{:S(2)}) copy-start(s32[1,4,4]{2,1,0:T(4,128)} %param.13) | copy-start | bytes 196
  11.4 22.8 %collective-permute-start.11 = (bf16[16,4,8,128]{3,2,1,0:T(8,128)(2,1)}, bf16[16,4,8,128]{3,2,1,0:T(8,128)(2,1)S(1)}, u32[]{:S(2)}, u32[]{:S(2)}) collective-permute-start(bf16[16,4,8,128]{3,2,1,0:T(8,128)(2,1)} %get-tuple-element.59), channel_id=1, source_target_pairs={{0,26},{2,24},{4,30},{6,28},{8,18},{10,16},{12,22},{14,20},{16,10}... | collective-permute-start | bytes 393224 | tf_op jit(solution)/shard_map/ppermute | solution.py:228
  14.2 25.0 %collective-permute-start.12 = (bf16[16,4,8,128]{3,2,1,0:T(8,128)(2,1)}, bf16[16,4,8,128]{3,2,1,0:T(8,128)(2,1)S(1)}, u32[]{:S(2)}, u32[]{:S(2)}) collective-permute-start(bf16[16,4,8,128]{3,2,1,0:T(8,128)(2,1)} %get-tuple-element.60), channel_id=1, source_target_pairs={{0,18},{2,16},{4,22},{6,20},{8,26},{10,24},{12,30},{14,28},{16,2},... | collective-permute-start | bytes 393224 | tf_op jit(solution)/shard_map/ppermute | solution.py:228
  15.3 25.4 %collective-permute-start.13 = (bf16[16,4,8,128]{3,2,1,0:T(8,128)(2,1)}, bf16[16,4,8,128]{3,2,1,0:T(8,128)(2,1)S(1)}, u32[]{:S(2)}, u32[]{:S(2)}) collective-permute-start(bf16[16,4,8,128]{3,2,1,0:T(8,128)(2,1)} %get-tuple-element.61), channel_id=1, source_target_pairs={{0,28},{2,30},{4,24},{6,26},{8,20},{10,22},{12,16},{14,18},{16,12}... | collective-permute-start | bytes 393224 | tf_op jit(solution)/shard_map/ppermute | solution.py:228
  19.1 24.5 %collective-permute-start.14 = (bf16[16,4,8,128]{3,2,1,0:T(8,128)(2,1)}, bf16[16,4,8,128]{3,2,1,0:T(8,128)(2,1)S(1)}, u32[]{:S(2)}, u32[]{:S(2)}) collective-permute-start(bf16[16,4,8,128]{3,2,1,0:T(8,128)(2,1)} %get-tuple-element.62), channel_id=1, source_target_pairs={{0,30},{2,28},{4,26},{6,24},{8,22},{10,20},{12,18},{14,16},{16,14}... | collective-permute-start | bytes 393224 | tf_op jit(solution)/shard_map/ppermute | solution.py:228
  32.7 14.2 %collective-permute-start.2 = (bf16[16,4,8,128]{3,2,1,0:T(8,128)(2,1)S(1)}, bf16[16,4,8,128]{3,2,1,0:T(8,128)(2,1)S(1)}, u32[]{:S(2)}, u32[]{:S(2)}) collective-permute-start(bf16[16,4,8,128]{3,2,1,0:T(8,128)(2,1)S(1)} %get-tuple-element.50), channel_id=1, source_target_pairs={{0,2},{2,0},{4,6},{6,4},{8,10},{10,8},{12,14},{14,12},{16,18},{18,... | collective-permute-start | bytes 393224 | tf_op jit(solution)/shard_map/ppermute | solution.py:228
  34.2 12.8 %collective-permute-start.3 = (bf16[16,4,8,128]{3,2,1,0:T(8,128)(2,1)}, bf16[16,4,8,128]{3,2,1,0:T(8,128)(2,1)S(1)}, u32[]{:S(2)}, u32[]{:S(2)}) collective-permute-start(bf16[16,4,8,128]{3,2,1,0:T(8,128)(2,1)} %get-tuple-element.51), channel_id=1, source_target_pairs={{0,4},{2,6},{4,0},{6,2},{8,12},{10,14},{12,8},{14,10},{16,20},{18,... | collective-permute-start | bytes 393224 | tf_op jit(solution)/shard_map/ppermute | solution.py:228
  39.2 12.8 %collective-permute-start.4 = (bf16[16,4,8,128]{3,2,1,0:T(8,128)(2,1)}, bf16[16,4,8,128]{3,2,1,0:T(8,128)(2,1)S(1)}, u32[]{:S(2)}, u32[]{:S(2)}) collective-permute-start(bf16[16,4,8,128]{3,2,1,0:T(8,128)(2,1)} %get-tuple-element.52), channel_id=1, source_target_pairs={{0,6},{2,4},{4,2},{6,0},{8,14},{10,12},{12,10},{14,8},{16,22},{18,... | collective-permute-start | bytes 393224 | tf_op jit(solution)/shard_map/ppermute | solution.py:228
  40.7 11.3 %collective-permute-start.5 = (bf16[16,4,8,128]{3,2,1,0:T(8,128)(2,1)}, bf16[16,4,8,128]{3,2,1,0:T(8,128)(2,1)S(1)}, u32[]{:S(2)}, u32[]{:S(2)}) collective-permute-start(bf16[16,4,8,128]{3,2,1,0:T(8,128)(2,1)} %get-tuple-element.53), channel_id=1, source_target_pairs={{0,8},{2,10},{4,12},{6,14},{8,0},{10,2},{12,4},{14,6},{16,24},{18,... | collective-permute-start | bytes 393224 | tf_op jit(solution)/shard_map/ppermute | solution.py:228
  43.5 11.3 %collective-permute-start.6 = (bf16[16,4,8,128]{3,2,1,0:T(8,128)(2,1)}, bf16[16,4,8,128]{3,2,1,0:T(8,128)(2,1)S(1)}, u32[]{:S(2)}, u32[]{:S(2)}) collective-permute-start(bf16[16,4,8,128]{3,2,1,0:T(8,128)(2,1)} %get-tuple-element.54), channel_id=1, source_target_pairs={{0,10},{2,8},{4,14},{6,12},{8,2},{10,0},{12,6},{14,4},{16,26},{18,... | collective-permute-start | bytes 393224 | tf_op jit(solution)/shard_map/ppermute | solution.py:228
  46.9 19.8 %collective-permute-start = (bf16[4,256,128]{2,1,0:T(8,128)(2,1)S(1)}, bf16[4,256,128]{2,1,0:T(8,128)(2,1)S(1)}, u32[]{:S(2)}, u32[]{:S(2)}) collective-permute-start(bf16[4,256,128]{2,1,0:T(8,128)(2,1)S(1)} %bitcast.49), channel_id=1, source_target_pairs={{0,1},{1,0},{2,3},{3,2},{4,5},{5,4},{6,7},{7,6},{8,9},{9,8},{10,11... | collective-permute-start | bytes 786440 | tf_op jit(solution)/shard_map/ppermute | solution.py:183
  47.0 30.8 %collective-permute-start.15 = (bf16[16,4,8,128]{3,2,1,0:T(8,128)(2,1)}, bf16[16,4,8,128]{3,2,1,0:T(8,128)(2,1)S(1)}, u32[]{:S(2)}, u32[]{:S(2)}) collective-permute-start(bf16[16,4,8,128]{3,2,1,0:T(8,128)(2,1)} %get-tuple-element.65), channel_id=1, source_target_pairs={{0,22},{2,20},{4,18},{6,16},{8,30},{10,28},{12,26},{14,24},{16,6},... | collective-permute-start | bytes 393224 | tf_op jit(solution)/shard_map/ppermute | solution.py:228
  52.0 25.7 %collective-permute-start.16 = (bf16[16,4,8,128]{3,2,1,0:T(8,128)(2,1)}, bf16[16,4,8,128]{3,2,1,0:T(8,128)(2,1)S(1)}, u32[]{:S(2)}, u32[]{:S(2)}) collective-permute-start(bf16[16,4,8,128]{3,2,1,0:T(8,128)(2,1)} %get-tuple-element.66), channel_id=1, source_target_pairs={{0,20},{2,22},{4,16},{6,18},{8,28},{10,30},{12,24},{14,26},{16,4},... | collective-permute-start | bytes 393224 | tf_op jit(solution)/shard_map/ppermute | solution.py:228
  52.0 13.4 %collective-permute-start.7 = (bf16[16,4,8,128]{3,2,1,0:T(8,128)(2,1)}, bf16[16,4,8,128]{3,2,1,0:T(8,128)(2,1)S(1)}, u32[]{:S(2)}, u32[]{:S(2)}) collective-permute-start(bf16[16,4,8,128]{3,2,1,0:T(8,128)(2,1)} %get-tuple-element.55), channel_id=1, source_target_pairs={{0,12},{2,14},{4,8},{6,10},{8,4},{10,6},{12,0},{14,2},{16,28},{18,... | collective-permute-start | bytes 393224 | tf_op jit(solution)/shard_map/ppermute | solution.py:228
  54.8 11.1 %collective-permute-start.8 = (bf16[16,4,8,128]{3,2,1,0:T(8,128)(2,1)S(1)}, bf16[16,4,8,128]{3,2,1,0:T(8,128)(2,1)S(1)}, u32[]{:S(2)}, u32[]{:S(2)}) collective-permute-start(bf16[16,4,8,128]{3,2,1,0:T(8,128)(2,1)S(1)} %get-tuple-element.56), channel_id=1, source_target_pairs={{0,14},{2,12},{4,10},{6,8},{8,6},{10,4},{12,2},{14,0},{16,30},{18,... | collective-permute-start | bytes 393224 | tf_op jit(solution)/shard_map/ppermute | solution.py:228
  78.8 7.4 %collective-permute-start.19 = (bf16[4,8,16,128]{3,2,1,0:T(8,128)(2,1)S(1)}, bf16[4,8,16,128]{3,2,1,0:T(8,128)(2,1)S(1)}, u32[]{:S(2)}, u32[]{:S(2)}) collective-permute-start(bf16[4,8,16,128]{3,2,1,0:T(8,128)(2,1)S(1)} %get-tuple-element.72), channel_id=1, source_target_pairs={{0,2},{2,0},{4,6},{6,4},{8,10},{10,8},{12,14},{14,12},{16,18},{18,... | collective-permute-start | bytes 393224 | tf_op jit(solution)/shard_map/ppermute | solution.py:228
  81.3 8.1 %collective-permute-start.20 = (bf16[4,8,16,128]{3,2,1,0:T(8,128)(2,1)S(1)}, bf16[4,8,16,128]{3,2,1,0:T(8,128)(2,1)S(1)}, u32[]{:S(2)}, u32[]{:S(2)}) collective-permute-start(bf16[4,8,16,128]{3,2,1,0:T(8,128)(2,1)S(1)} %get-tuple-element.73), channel_id=1, source_target_pairs={{0,4},{2,6},{4,0},{6,2},{8,12},{10,14},{12,8},{14,10},{16,20},{18,... | collective-permute-start | bytes 393224 | tf_op jit(solution)/shard_map/ppermute | solution.py:228
  81.3 9.7 %collective-permute-start.21 = (bf16[4,8,16,128]{3,2,1,0:T(8,128)(2,1)S(1)}, bf16[4,8,16,128]{3,2,1,0:T(8,128)(2,1)S(1)}, u32[]{:S(2)}, u32[]{:S(2)}) collective-permute-start(bf16[4,8,16,128]{3,2,1,0:T(8,128)(2,1)S(1)} %get-tuple-element.74), channel_id=1, source_target_pairs={{0,6},{2,4},{4,2},{6,0},{8,14},{10,12},{12,10},{14,8},{16,22},{18,... | collective-permute-start | bytes 393224 | tf_op jit(solution)/shard_map/ppermute | solution.py:228
  82.8 11.0 %collective-permute-start.22 = (bf16[4,8,16,128]{3,2,1,0:T(8,128)(2,1)S(1)}, bf16[4,8,16,128]{3,2,1,0:T(8,128)(2,1)S(1)}, u32[]{:S(2)}, u32[]{:S(2)}) collective-permute-start(bf16[4,8,16,128]{3,2,1,0:T(8,128)(2,1)S(1)} %get-tuple-element.75), channel_id=1, source_target_pairs={{0,8},{2,10},{4,12},{6,14},{8,0},{10,2},{12,4},{14,6},{16,24},{18,... | collective-permute-start | bytes 393224 | tf_op jit(solution)/shard_map/ppermute | solution.py:228
  82.9 10.9 %collective-permute-start.23 = (bf16[4,8,16,128]{3,2,1,0:T(8,128)(2,1)S(1)}, bf16[4,8,16,128]{3,2,1,0:T(8,128)(2,1)S(1)}, u32[]{:S(2)}, u32[]{:S(2)}) collective-permute-start(bf16[4,8,16,128]{3,2,1,0:T(8,128)(2,1)S(1)} %get-tuple-element.76), channel_id=1, source_target_pairs={{0,10},{2,8},{4,14},{6,12},{8,2},{10,0},{12,6},{14,4},{16,26},{18,... | collective-permute-start | bytes 393224 | tf_op jit(solution)/shard_map/ppermute | solution.py:228
  86.2 11.0 %collective-permute-start.24 = (bf16[4,8,16,128]{3,2,1,0:T(8,128)(2,1)S(1)}, bf16[4,8,16,128]{3,2,1,0:T(8,128)(2,1)S(1)}, u32[]{:S(2)}, u32[]{:S(2)}) collective-permute-start(bf16[4,8,16,128]{3,2,1,0:T(8,128)(2,1)S(1)} %get-tuple-element.77), channel_id=1, source_target_pairs={{0,12},{2,14},{4,8},{6,10},{8,4},{10,6},{12,0},{14,2},{16,28},{18,... | collective-permute-start | bytes 393224 | tf_op jit(solution)/shard_map/ppermute | solution.py:228
  89.3 9.6 %collective-permute-start.25 = (bf16[4,8,16,128]{3,2,1,0:T(8,128)(2,1)S(1)}, bf16[4,8,16,128]{3,2,1,0:T(8,128)(2,1)S(1)}, u32[]{:S(2)}, u32[]{:S(2)}) collective-permute-start(bf16[4,8,16,128]{3,2,1,0:T(8,128)(2,1)S(1)} %get-tuple-element.78), channel_id=1, source_target_pairs={{0,14},{2,12},{4,10},{6,8},{8,6},{10,4},{12,2},{14,0},{16,30},{18,... | collective-permute-start | bytes 393224 | tf_op jit(solution)/shard_map/ppermute | solution.py:228
  90.9 15.1 %collective-permute-start.26 = (bf16[4,8,16,128]{3,2,1,0:T(8,128)(2,1)S(1)}, bf16[4,8,16,128]{3,2,1,0:T(8,128)(2,1)S(1)}, u32[]{:S(2)}, u32[]{:S(2)}) collective-permute-start(bf16[4,8,16,128]{3,2,1,0:T(8,128)(2,1)S(1)} %get-tuple-element.79), channel_id=1, source_target_pairs={{0,24},{2,26},{4,28},{6,30},{8,16},{10,18},{12,20},{14,22},{16,8},... | collective-permute-start | bytes 393224 | tf_op jit(solution)/shard_map/ppermute | solution.py:228
  93.8 22.5 %collective-permute-start.27 = (bf16[4,8,16,128]{3,2,1,0:T(8,128)(2,1)S(1)}, bf16[4,8,16,128]{3,2,1,0:T(8,128)(2,1)S(1)}, u32[]{:S(2)}, u32[]{:S(2)}) collective-permute-start(bf16[4,8,16,128]{3,2,1,0:T(8,128)(2,1)S(1)} %get-tuple-element.80), channel_id=1, source_target_pairs={{0,16},{2,18},{4,20},{6,22},{8,24},{10,26},{12,28},{14,30},{16,0},... | collective-permute-start | bytes 393224 | tf_op jit(solution)/shard_map/ppermute | solution.py:228
  93.8 23.9 %collective-permute-start.28 = (bf16[4,8,16,128]{3,2,1,0:T(8,128)(2,1)S(1)}, bf16[4,8,16,128]{3,2,1,0:T(8,128)(2,1)S(1)}, u32[]{:S(2)}, u32[]{:S(2)}) collective-permute-start(bf16[4,8,16,128]{3,2,1,0:T(8,128)(2,1)S(1)} %get-tuple-element.81), channel_id=1, source_target_pairs={{0,26},{2,24},{4,30},{6,28},{8,18},{10,16},{12,22},{14,20},{16,10}... | collective-permute-start | bytes 393224 | tf_op jit(solution)/shard_map/ppermute | solution.py:228
  97.3 28.6 %collective-permute-start.29 = (bf16[4,8,16,128]{3,2,1,0:T(8,128)(2,1)S(1)}, bf16[4,8,16,128]{3,2,1,0:T(8,128)(2,1)S(1)}, u32[]{:S(2)}, u32[]{:S(2)}) collective-permute-start(bf16[4,8,16,128]{3,2,1,0:T(8,128)(2,1)S(1)} %get-tuple-element.82), channel_id=1, source_target_pairs={{0,18},{2,16},{4,22},{6,20},{8,26},{10,24},{12,30},{14,28},{16,2},... | collective-permute-start | bytes 393224 | tf_op jit(solution)/shard_map/ppermute | solution.py:228
  99.0 26.9 %collective-permute-start.30 = (bf16[4,8,16,128]{3,2,1,0:T(8,128)(2,1)S(1)}, bf16[4,8,16,128]{3,2,1,0:T(8,128)(2,1)S(1)}, u32[]{:S(2)}, u32[]{:S(2)}) collective-permute-start(bf16[4,8,16,128]{3,2,1,0:T(8,128)(2,1)S(1)} %get-tuple-element.83), channel_id=1, source_target_pairs={{0,28},{2,30},{4,24},{6,26},{8,20},{10,22},{12,16},{14,18},{16,12}... | collective-permute-start | bytes 393224 | tf_op jit(solution)/shard_map/ppermute | solution.py:228
  106.0 19.8 %collective-permute-start.31 = (bf16[4,8,16,128]{3,2,1,0:T(8,128)(2,1)S(1)}, bf16[4,8,16,128]{3,2,1,0:T(8,128)(2,1)S(1)}, u32[]{:S(2)}, u32[]{:S(2)}) collective-permute-start(bf16[4,8,16,128]{3,2,1,0:T(8,128)(2,1)S(1)} %get-tuple-element.84), channel_id=1, source_target_pairs={{0,30},{2,28},{4,26},{6,24},{8,22},{10,20},{12,18},{14,16},{16,14}... | collective-permute-start | bytes 393224 | tf_op jit(solution)/shard_map/ppermute | solution.py:228
  116.3 21.2 %collective-permute-start.17 = (bf16[4,8,16,128]{3,2,1,0:T(8,128)(2,1)S(1)}, bf16[4,8,16,128]{3,2,1,0:T(8,128)(2,1)S(1)}, u32[]{:S(2)}, u32[]{:S(2)}) collective-permute-start(bf16[4,8,16,128]{3,2,1,0:T(8,128)(2,1)S(1)} %get-tuple-element.67), channel_id=1, source_target_pairs={{0,22},{2,20},{4,18},{6,16},{8,30},{10,28},{12,26},{14,24},{16,6},... | collective-permute-start | bytes 393224 | tf_op jit(solution)/shard_map/ppermute | solution.py:228
  117.7 19.9 %collective-permute-start.18 = (bf16[4,8,16,128]{3,2,1,0:T(8,128)(2,1)S(1)}, bf16[4,8,16,128]{3,2,1,0:T(8,128)(2,1)S(1)}, u32[]{:S(2)}, u32[]{:S(2)}) collective-permute-start(bf16[4,8,16,128]{3,2,1,0:T(8,128)(2,1)S(1)} %get-tuple-element.68), channel_id=1, source_target_pairs={{0,20},{2,22},{4,16},{6,18},{8,28},{10,30},{12,24},{14,26},{16,4},... | collective-permute-start | bytes 393224 | tf_op jit(solution)/shard_map/ppermute | solution.py:228

commit v3 on v2

--- a/solution.py
+++ b/solution.py
@@ -12,7 +12,8 @@
 LOC_FAR = 0.5
 DIRECT_MAX = 16
 
-LATE = 2
+LATE = 4
+LEAD = 2
 MIB = 1 << 20
 
 
@@ -120,7 +121,7 @@
 
 
 def combine(t, mix, rest, field, mean, sent, first):
-    _, depth, rows, points = sent[0].shape
+    depth, rows, points = sent[0][0].shape[1:]
     count = len(sent) * rows
     result = jnp.dot(
         mix[t, first:first + count, :], field, preferred_element_type=jnp.float32
@@ -129,46 +130,82 @@
         part = result[:, level * points:(level + 1) * points]
         part = part + rest[t, first:first + count, :] * mean[level:level + 1, :]
         part = part.astype(jnp.bfloat16)
-        for v, out in enumerate(sent):
-            out[t, level] = part[v * rows:(v + 1) * rows, :]
-
-
-def first_kernel(late, first, mix, rest, fields, total, *refs):
+        for v, (out, start) in enumerate(sent):
+            out[t - start, level] = part[v * rows:(v + 1) * rows, :]
+
+
+def cut_kernel(blocks, spot, fields, *refs):
+    sems = refs[-1]
+    copies = []
+    for q, (s, start, stop) in enumerate(blocks):
+        copy = pltpu.make_async_copy(
+            fields.at[:, spot[0] ^ s, pl.ds(start, stop - start)], refs[q], sems.at[q]
+        )
+        copy.start()
+        copies.append(copy)
+    for copy in copies:
+        copy.wait()
+
+
+def turn_late(t, pieces, starts, total, members, bufs, late_fields, mean_out, slot):
+    acc = total[t]
+    rows = pieces[0].shape[0]
+    for q, (piece, start) in enumerate(zip(pieces, starts)):
+        part, add = turn_in(piece, t - start, bufs.at[t * len(pieces) + q])
+        late_fields[slot, q * rows:(q + 1) * rows, :] = part
+        acc += add
+    mean_out[slot] = acc / members
+
+
+def lead_kernel(late, first, cut, mix, rest, fields, total, *refs):
     pieces, sent = refs[:late], refs[late:-3]
-    late_fields, mean_out, bufs = refs[-3:]
-    tiles, members, _ = mix.shape
-    rows = pieces[0].shape[0]
-    for t in range(tiles):
-        acc = total[t]
-        turned = [fields[t]]
-        for q, piece in enumerate(pieces):
-            part, add = turn_in(piece, t, bufs.at[t * late + q])
-            late_fields[t, q * rows:(q + 1) * rows, :] = part
-            turned.append(part)
-            acc += add
-        mean = acc / members
-        mean_out[t] = mean
-        combine(t, mix, rest, jnp.concatenate(turned, axis=0), mean, sent, first)
+    late_fields, mean, bufs = refs[-3:]
+    for t in range(cut):
+        turn_late(t, pieces, [0] * late, total, mix.shape[1], bufs, late_fields, mean, t)
+        field = jnp.concatenate([fields[t], late_fields[t]], axis=0)
+        combine(t, mix, rest, field, mean[t], [(out, 0) for out in sent], first)
+
+
+def main_kernel(late, first, lead, cut, mix, rest, fields, total, lead_fields, lead_mean, *refs):
+    pieces, sent = refs[:late], refs[late:-3]
+    late_fields, mean, bufs = refs[-3:]
+    rows = sent[0].shape[2]
+    starts = [0] * (late - 1) + [cut]
+    for t in range(mix.shape[0]):
+        if t < cut:
+            late_fields[t] = lead_fields[t]
+            mean[t] = lead_mean[t]
+            outs, skip = [(out, 0) for out in sent[lead:]], lead * rows
+        else:
+            turn_late(t, pieces, starts, total, mix.shape[1], bufs, late_fields, mean, t)
+            outs = [(out, cut if v < lead else 0) for v, out in enumerate(sent)]
+            skip = 0
+        field = jnp.concatenate([fields[t], late_fields[t]], axis=0)
+        combine(t, mix, rest, field, mean[t], outs, first + skip)
 
 
 def second_kernel(mix, rest, fields, late_fields, mean, *sent):
     for t in range(mix.shape[0]):
         field = jnp.concatenate([fields[t], late_fields[t]], axis=0)
-        combine(t, mix, rest, field, mean[t], sent, 0)
-
-
-def place_kernel(order, aliased, spot, *refs):
-    pieces = refs[:len(order)]
-    result, turned, buf, sems = refs[len(order) + aliased:]
-    tiles, depth, rows, points = pieces[0].shape
+        combine(t, mix, rest, field, mean[t], [(out, 0) for out in sent], 0)
+
+
+def place_kernel(targets, aliased, spot, *refs):
+    pieces = refs[:len(targets)]
+    result, turned, buf, sems = refs[len(targets) + aliased:]
     copies = []
-    for q, (u, piece) in enumerate(zip(order, pieces)):
+    for q, ((s, start), piece) in enumerate(zip(targets, pieces)):
+        tiles, depth, rows, points = piece.shape
         for t in range(tiles):
             view = buf.at[(q * tiles + t) % buf.shape[0]]
             for level in range(depth):
                 view[pl.ds(level, rows, stride=depth), :] = piece[t, level].astype(jnp.float32)
             turned[q, :, t] = view[...].reshape(rows, depth, points).astype(jnp.bfloat16)
-        copy = pltpu.make_async_copy(turned.at[q], result.at[:, spot[0] ^ u], sems.at[q])
+        copy = pltpu.make_async_copy(
+            turned.at[q, :, pl.ds(0, tiles)],
+            result.at[:, spot[0] ^ s, pl.ds(start, tiles)],
+            sems.at[q],
+        )
         copy.start()
         copies.append(copy)
     for copy in copies:
@@ -227,21 +264,38 @@
     def swap(x, s):
         return lax.ppermute(x, "wide", [(i, i ^ s) for i in range(wide)])
 
+    hbm = pl.BlockSpec(memory_space=pl.ANY)
     if direct:
         far, near_by = send_order(wide)
+        late = far[-LATE:]
+        early = [0] + near_by + far[:-LATE]
+        order = early + late
+        cut = 1 if tiles > 1 else 0
+
+        def slices(blocks, *after):
+            return call(
+                functools.partial(cut_kernel, blocks),
+                [
+                    jax.ShapeDtypeStruct((mine, stop - start, depth, points), jnp.bfloat16)
+                    for _, start, stop in blocks
+                ],
+                [smem, hbm],
+                [pltpu.SemaphoreType.DMA((len(blocks),))],
+                8,
+            )(me.reshape(1), fields)
+
+        last = far[-1]
         arrived = {}
-        left = fields
-        for group in (far[:2], far[2:], near_by + [0]):
-            parts = [lax.dynamic_index_in_dim(left, me ^ s, 1, keepdims=False) for s in group]
-            left, *parts = lax.optimization_barrier((left, *parts))
-            for s, part in zip(group, parts):
-                if s == 0:
-                    arrived[0] = part
-                    continue
-                arrived[s] = swap(part, s)
-        late = far[-1:-2 * LATE:-2]
-        early = [0] + near_by + [s for s in far if s not in late]
-        order = early + late
+        parts = dict(zip(far[:LEAD], slices([(s, 0, tiles) for s in far[:LEAD]])))
+        others = far[LEAD:-1] + near_by + [0]
+        wanted = [(s, 0, tiles) for s in others]
+        wanted += [(last, 0, cut)] * (cut > 0) + [(last, cut, tiles)]
+        *found, tail = slices(wanted)
+        parts.update(zip(others + [last], found))
+        arrived[0] = parts.pop(0)
+        for s, part in parts.items():
+            arrived[s] = swap(part, s)
+        arrived_tail = swap(tail, last)
     else:
         order = [0]
 
@@ -312,33 +366,57 @@
         [pltpu.VMEM((8, mine * depth, points), jnp.float32)],
         12,
     )(*[arrived[s] for s in early])
-    piece = jax.ShapeDtypeStruct((tiles, depth, mine, points), jnp.bfloat16)
     close = len(near_by) + 1
-    *sent_far, late_fields, mean = call(
-        functools.partial(first_kernel, len(late), close * mine),
-        [piece] * (len(order) - close)
-        + [
-            jax.ShapeDtypeStruct((tiles, len(late) * mine, width), jnp.bfloat16),
-            jax.ShapeDtypeStruct((tiles, depth, points), jnp.float32),
-        ],
-        [vmem] * (4 + len(late)),
-        [pltpu.VMEM((tiles * len(late), mine * depth, points), jnp.float32)],
+
+    def block(count):
+        return jax.ShapeDtypeStruct((count, depth, mine, points), jnp.bfloat16)
+
+    def late_shapes(count):
+        return [
+            jax.ShapeDtypeStruct((count, LATE * mine, width), jnp.bfloat16),
+            jax.ShapeDtypeStruct((count, depth, points), jnp.float32),
+        ]
+
+    turn_bufs = [pltpu.VMEM((tiles * LATE, mine * depth, points), jnp.float32)]
+    sent, sent_lead = {}, {}
+    if cut:
+        *outs, lead_fields, lead_mean = call(
+            functools.partial(lead_kernel, LATE, close * mine, cut),
+            [block(cut)] * LEAD + late_shapes(cut),
+            [vmem] * (4 + LATE),
+            turn_bufs,
+            12,
+        )(mix, rest, gathered, total, *[arrived[s] for s in late])
+        sent_lead = dict(zip(far[:LEAD], outs))
+    else:
+        lead_fields, lead_mean = [jnp.zeros(x.shape, x.dtype) for x in late_shapes(1)]
+    *outs, late_fields, mean = call(
+        functools.partial(main_kernel, LATE, close * mine, LEAD, cut),
+        [block(tiles - cut)] * LEAD + [block(tiles)] * (len(far) - LEAD) + late_shapes(tiles),
+        [vmem] * (6 + LATE),
+        turn_bufs,
         12,
-    )(mix, rest, gathered, total, *[arrived[s] for s in late])
-    sent_near = call(
-        second_kernel, [piece] * close, [vmem] * 5, [], 12
+    )(
+        mix, rest, gathered, total, lead_fields, lead_mean,
+        *[arrived[s] for s in late[:-1]], arrived_tail,
+    )
+    sent = dict(zip(far, outs))
+    outs = call(
+        second_kernel, [block(tiles)] * close, [vmem] * 5, [], 12
     )(mix, rest, gathered, late_fields, mean)
-    sent = dict(zip(order, list(sent_near) + sent_far))
-    back = {0: sent[0]}
+    sent.update(zip([0] + near_by, outs))
+    back = []
+    for s, part in sent_lead.items():
+        back.append((s, 0, swap(part, s)))
     for s in far + near_by:
-        back[s] = swap(sent[s], s)
+        back.append((s, cut if s in sent_lead else 0, swap(sent[s], s)))
+    back.append((0, 0, sent[0]))
 
     result = jax.ShapeDtypeStruct((mine, wide, tiles, depth, points), jnp.bfloat16)
-    hbm = pl.BlockSpec(memory_space=pl.ANY)
 
     def place(group, *rest):
         return call(
-            functools.partial(place_kernel, group, len(rest)),
+            functools.partial(place_kernel, [(s, start) for s, start, _ in group], len(rest)),
             result,
             [smem] + [vmem] * len(group) + [hbm] * len(rest),
             [
@@ -349,10 +427,11 @@
             12,
             out_specs=hbm,
             input_output_aliases={1 + len(group): 0} if rest else {},
-        )(me.reshape(1), *[back[s] for s in group], *rest)
-
-    most = place(early)
-    return place(late, most).reshape(prior_states.shape)
+        )(me.reshape(1), *[part for _, _, part in group], *rest)
+
+    most = place([x for x in back if x[0] not in late])
+    final = place([x for x in back if x[0] in late], most)
+    return final.reshape(prior_states.shape)
 
 
 def solution(mesh):

time: 139 us -> 127 us (0.914)
  starting transfers between devices: 65.7 us -> 61.9 us
  waiting for transfers between devices: 50.4 us -> 47 us
  local copies, waits for them, and re-layouts: 4.73 us -> 1.75 us
  other arithmetic: 2.35 us -> 0.16 us
    squeeze x3 -> x0, local copies, waits for them, and re-layouts: 4.64 us -> none  [on_device(): lax.dynamic_index_in_dim(left, me ^ s, 1, keepdims=False)]
    ppermute x30 -> x33, waiting for transfers between devices: 50.4 us -> 47 us  [swap(): return lax.ppermute(x, 'wide', [(i, i ^ s) for i in range(wide)])]
    ppermute x30 -> x33, starting transfers between devices: 65.2 us -> 61.9 us  [swap(): return lax.ppermute(x, 'wide', [(i, i ^ s) for i in range(wide)])]
    unnamed x6 -> x16, local copies, waits for them, and re-layouts: 0.01 us -> 1.67 us
    pallas_call x4 -> x7, Pallas kernels: 3.37 us -> 4.38 us  [the longest x2 2.43 us: place(): call(functools.partial(place_kernel, [(s, start) for s, start, _ in group...]
  transfers between devices with their start and end apart: 32 -> 35, of which waited for: 8 -> 10; matrix products, arithmetic and copies ran while one was open for 3% -> 0% of each run, Pallas kernels for 10% -> 12%
where the time goes in v3:
time: 127 us
  starting transfers between devices  61.9 us (49%)
  waiting for transfers between devices  47 us (37%)
  Pallas kernels  16 us (13%)
  local copies, waits for them, and re-layouts  1.75 us (1%)
    ppermute x33, starting transfers between devices, swap(): return lax.ppermute(x, 'wide', [(i, i ^ s) for i in range(wide)])  61.9 us
    ppermute x33, waiting for transfers between devices, swap(): return lax.ppermute(x, 'wide', [(i, i ^ s) for i in range(wide)])  47 us
    pallas_call x1, Pallas kernels, on_device(): call(functools.partial(mix_kernel, order), [jax.ShapeDtypeStruct((tiles,...  11 us
  transfers between devices with their start and end apart: 35, of which 10 were waited for; matrix products, arithmetic and copies ran while one was open for 0% of the time, Pallas kernels for 12%

profile of v3, /device:TPU:0, one launch (start us, length us, event | category | flops | bytes accessed | tf_op | source)
XLA Modules:
  0.0 127.0 jit_solution(5826939396737639059)
XLA Ops:
  0.0 1.6 %copy-done = bf16[16,1,64,8,128]{4,3,2,1,0:T(8,128)(2,1)S(1)} copy-done((bf16[16,1,64,8,128]{4,3,2,1,0:T(8,128)(2,1)S(1)}, bf16[16,1,64,8,128]{4,3,2,1,0:T(8,128)(2,1)}, u32[]{:S(2)}) %copy-start) | copy-done | bytes 2097176
  1.7 0.5 shard_map.74
  2.1 0.0 copy-start.2
  2.2 0.0 copy-start.3
  2.2 3.0 %collective-permute-start.2 = (bf16[16,4,8,128]{3,2,1,0:T(8,128)(2,1)S(1)}, bf16[16,4,8,128]{3,2,1,0:T(8,128)(2,1)S(1)}, u32[]{:S(2)}, u32[]{:S(2)}) collective-permute-start(bf16[16,4,8,128]{3,2,1,0:T(8,128)(2,1)S(1)} %get-tuple-element.51), channel_id=1, source_target_pairs={{0,2},{2,0},{4,6},{6,4},{8,10},{10,8},{12,14},{14,12},{16,18},{18,... | collective-permute-start | bytes 393224 | tf_op jit(solution)/shard_map/ppermute | solution.py:265
  5.2 1.5 %collective-permute-start.3 = (bf16[16,4,8,128]{3,2,1,0:T(8,128)(2,1)S(1)}, bf16[16,4,8,128]{3,2,1,0:T(8,128)(2,1)S(1)}, u32[]{:S(2)}, u32[]{:S(2)}) collective-permute-start(bf16[16,4,8,128]{3,2,1,0:T(8,128)(2,1)S(1)} %get-tuple-element.52), channel_id=1, source_target_pairs={{0,4},{2,6},{4,0},{6,2},{8,12},{10,14},{12,8},{14,10},{16,20},{18,... | collective-permute-start | bytes 393224 | tf_op jit(solution)/shard_map/ppermute | solution.py:265
  6.7 0.0 collective-permute-start.4
  6.8 0.1 convert_multiply_fusion
  6.9 0.1 pad.2.clone
  6.9 0.1 maximum_maximum_fusion.own_aux
  7.0 0.0 collective-permute-start.1
  7.0 2.1 %collective-permute-start.5 = (bf16[16,4,8,128]{3,2,1,0:T(8,128)(2,1)S(1)}, bf16[16,4,8,128]{3,2,1,0:T(8,128)(2,1)S(1)}, u32[]{:S(2)}, u32[]{:S(2)}) collective-permute-start(bf16[16,4,8,128]{3,2,1,0:T(8,128)(2,1)S(1)} %get-tuple-element.54), channel_id=1, source_target_pairs={{0,8},{2,10},{4,12},{6,14},{8,0},{10,2},{12,4},{14,6},{16,24},{18,... | collective-permute-start | bytes 393224 | tf_op jit(solution)/shard_map/ppermute | solution.py:265
  9.1 0.0 collective-permute-done.1
  9.1 2.0 %collective-permute-start.6 = (bf16[16,4,8,128]{3,2,1,0:T(8,128)(2,1)S(1)}, bf16[16,4,8,128]{3,2,1,0:T(8,128)(2,1)S(1)}, u32[]{:S(2)}, u32[]{:S(2)}) collective-permute-start(bf16[16,4,8,128]{3,2,1,0:T(8,128)(2,1)S(1)} %get-tuple-element.55), channel_id=1, source_target_pairs={{0,10},{2,8},{4,14},{6,12},{8,2},{10,0},{12,6},{14,4},{16,26},{18,... | collective-permute-start | bytes 393224 | tf_op jit(solution)/shard_map/ppermute | solution.py:265
  11.2 0.0 collective-permute-done.2.refs_1_
  11.2 1.9 %collective-permute-start.7 = (bf16[16,4,8,128]{3,2,1,0:T(8,128)(2,1)S(1)}, bf16[16,4,8,128]{3,2,1,0:T(8,128)(2,1)S(1)}, u32[]{:S(2)}, u32[]{:S(2)}) collective-permute-start(bf16[16,4,8,128]{3,2,1,0:T(8,128)(2,1)S(1)} %get-tuple-element.56), channel_id=1, source_target_pairs={{0,12},{2,14},{4,8},{6,10},{8,4},{10,6},{12,0},{14,2},{16,28},{18,... | collective-permute-start | bytes 393224 | tf_op jit(solution)/shard_map/ppermute | solution.py:265
  13.0 0.0 collective-permute-done.3.refs_2_
  13.0 2.4 %collective-permute-start.8 = (bf16[16,4,8,128]{3,2,1,0:T(8,128)(2,1)S(1)}, bf16[16,4,8,128]{3,2,1,0:T(8,128)(2,1)S(1)}, u32[]{:S(2)}, u32[]{:S(2)}) collective-permute-start(bf16[16,4,8,128]{3,2,1,0:T(8,128)(2,1)S(1)} %get-tuple-element.57), channel_id=1, source_target_pairs={{0,14},{2,12},{4,10},{6,8},{8,6},{10,4},{12,2},{14,0},{16,30},{18,... | collective-permute-start | bytes 393224 | tf_op jit(solution)/shard_map/ppermute | solution.py:265
  15.5 0.0 collective-permute-done.4.refs_3_
  15.5 0.0 collective-permute-start
  15.5 0.1 shard_map.75
  15.6 0.0 collective-permute-done.5.refs_4_
  15.6 2.5 %collective-permute-start.9 = (bf16[16,4,8,128]{3,2,1,0:T(8,128)(2,1)S(1)}, bf16[16,4,8,128]{3,2,1,0:T(8,128)(2,1)S(1)}, u32[]{:S(2)}, u32[]{:S(2)}) collective-permute-start(bf16[16,4,8,128]{3,2,1,0:T(8,128)(2,1)S(1)} %get-tuple-element.58), channel_id=1, source_target_pairs={{0,24},{2,26},{4,28},{6,30},{8,16},{10,18},{12,20},{14,22},{16,8},... | collective-permute-start | bytes 393224 | tf_op jit(solution)/shard_map/ppermute | solution.py:265
  18.1 0.0 collective-permute-done.6.refs_5_
  18.1 2.1 %collective-permute-start.10 = (bf16[16,4,8,128]{3,2,1,0:T(8,128)(2,1)S(1)}, bf16[16,4,8,128]{3,2,1,0:T(8,128)(2,1)S(1)}, u32[]{:S(2)}, u32[]{:S(2)}) collective-permute-start(bf16[16,4,8,128]{3,2,1,0:T(8,128)(2,1)S(1)} %get-tuple-element.59), channel_id=1, source_target_pairs={{0,16},{2,18},{4,20},{6,22},{8,24},{10,26},{12,28},{14,30},{16,0},... | collective-permute-start | bytes 393224 | tf_op jit(solution)/shard_map/ppermute | solution.py:265
  20.2 0.2 collective-permute-done.7.refs_6_
  20.5 4.6 %collective-permute-start.11 = (bf16[16,4,8,128]{3,2,1,0:T(8,128)(2,1)S(1)}, bf16[16,4,8,128]{3,2,1,0:T(8,128)(2,1)S(1)}, u32[]{:S(2)}, u32[]{:S(2)}) collective-permute-start(bf16[16,4,8,128]{3,2,1,0:T(8,128)(2,1)S(1)} %get-tuple-element.60), channel_id=1, source_target_pairs={{0,26},{2,24},{4,30},{6,28},{8,18},{10,16},{12,22},{14,20},{16,10}... | collective-permute-start | bytes 393224 | tf_op jit(solution)/shard_map/ppermute | solution.py:265
  25.0 3.5 %collective-permute-done.8.refs_7_ = bf16[16,4,8,128]{3,2,1,0:T(8,128)(2,1)S(1)} collective-permute-done((bf16[16,4,8,128]{3,2,1,0:T(8,128)(2,1)S(1)}, bf16[16,4,8,128]{3,2,1,0:T(8,128)(2,1)S(1)}, u32[]{:S(2)}, u32[]{:S(2)}) %collective-permute-start.8) | collective-permute-done | bytes 131104 | tf_op jit(solution)/shard_map/ppermute | solution.py:265
  28.5 0.0 collective-permute-start.12
  28.5 0.0 collective-permute-done.9.refs_8_
  28.5 1.8 %collective-permute-start.13 = (bf16[16,4,8,128]{3,2,1,0:T(8,128)(2,1)S(1)}, bf16[16,4,8,128]{3,2,1,0:T(8,128)(2,1)S(1)}, u32[]{:S(2)}, u32[]{:S(2)}) collective-permute-start(bf16[16,4,8,128]{3,2,1,0:T(8,128)(2,1)S(1)} %get-tuple-element.64), channel_id=1, source_target_pairs={{0,28},{2,30},{4,24},{6,26},{8,20},{10,22},{12,16},{14,18},{16,12}... | collective-permute-start | bytes 393224 | tf_op jit(solution)/shard_map/ppermute | solution.py:265
  30.4 9.1 %collective-permute-done.10.refs_9_ = bf16[16,4,8,128]{3,2,1,0:T(8,128)(2,1)S(1)} collective-permute-done((bf16[16,4,8,128]{3,2,1,0:T(8,128)(2,1)S(1)}, bf16[16,4,8,128]{3,2,1,0:T(8,128)(2,1)S(1)}, u32[]{:S(2)}, u32[]{:S(2)}) %collective-permute-start.10) | collective-permute-done | bytes 131104 | tf_op jit(solution)/shard_map/ppermute | solution.py:265
  39.4 0.1 collective-permute-start.14
  39.6 4.2 %collective-permute-start.15 = (bf16[16,4,8,128]{3,2,1,0:T(8,128)(2,1)S(1)}, bf16[16,4,8,128]{3,2,1,0:T(8,128)(2,1)S(1)}, u32[]{:S(2)}, u32[]{:S(2)}) collective-permute-start(bf16[16,4,8,128]{3,2,1,0:T(8,128)(2,1)S(1)} %get-tuple-element.66), channel_id=1, source_target_pairs={{0,30},{2,28},{4,26},{6,24},{8,22},{10,20},{12,18},{14,16},{16,14}... | collective-permute-start | bytes 393224 | tf_op jit(solution)/shard_map/ppermute | solution.py:265
  43.7 7.9 %collective-permute-done.12.refs_11_ = bf16[16,4,8,128]{3,2,1,0:T(8,128)(2,1)S(1)} collective-permute-done((bf16[16,4,8,128]{3,2,1,0:T(8,128)(2,1)S(1)}, bf16[16,4,8,128]{3,2,1,0:T(8,128)(2,1)S(1)}, u32[]{:S(2)}, u32[]{:S(2)}) %collective-permute-start.12) | collective-permute-done | bytes 131104 | tf_op jit(solution)/shard_map/ppermute | solution.py:265
  51.6 4.7 %collective-permute-start.17 = (bf16[16,3,8,128]{3,2,1,0:T(8,128)(2,1)S(1)}, bf16[16,3,8,128]{3,2,1,0:T(8,128)(2,1)S(1)}, u32[]{:S(2)}, u32[]{:S(2)}) collective-permute-start(bf16[16,3,8,128]{3,2,1,0:T(8,128)(2,1)S(1)} %get-tuple-element.70), channel_id=1, source_target_pairs={{0,22},{2,20},{4,18},{6,16},{8,30},{10,28},{12,26},{14,24},{16,6},... | collective-permute-start | bytes 294920 | tf_op jit(solution)/shard_map/ppermute | solution.py:265
  56.3 0.7 shard_map.76
  57.0 11.0 %shard_map.73 = (bf16[4,256,256]{2,1,0:T(8,128)(2,1)S(1)}, f32[4,256,128]{2,1,0:T(8,128)S(1)}) custom-call(s32[4,4]{1,0:T(4,128)S(1)} %bitcast.17, s32[1]{0:T(128)} %bitcast.spot, bf16[4,256,128]{2,1,0:T(8,128)(2,1)S(1)} %bitcast.16, bf16[4,256,128]{2,1,0:T(8,128)(2,1)S(1)} %collective-permute-done.below.above, ...), custom_call_target="tpu_custom_call" | custom-call | tf_op jit(solution)/shard_map/pallas_call | solution.py:322
  68.1 0.2 shard_map.77
  68.3 3.0 %collective-permute-start.22 = (bf16[1,8,16,128]{3,2,1,0:T(8,128)(2,1)S(1)}, bf16[1,8,16,128]{3,2,1,0:T(8,128)(2,1)S(1)}, u32[]{:S(2)}, u32[]{:S(2)}) collective-permute-start(bf16[1,8,16,128]{3,2,1,0:T(8,128)(2,1)S(1)} %get-tuple-element.75), channel_id=1, source_target_pairs={{0,24},{2,26},{4,28},{6,30},{8,16},{10,18},{12,20},{14,22},{16,8},... | collective-permute-start | bytes 98312 | tf_op jit(solution)/shard_map/ppermute | solution.py:265
  71.3 0.7 shard_map.78
  72.0 0.9 collective-permute-start.26
  72.9 3.0 %collective-permute-start.27 = (bf16[4,8,16,128]{3,2,1,0:T(8,128)(2,1)S(1)}, bf16[4,8,16,128]{3,2,1,0:T(8,128)(2,1)S(1)}, u32[]{:S(2)}, u32[]{:S(2)}) collective-permute-start(bf16[4,8,16,128]{3,2,1,0:T(8,128)(2,1)S(1)} %get-tuple-element.80), channel_id=1, source_target_pairs={{0,18},{2,16},{4,22},{6,20},{8,26},{10,24},{12,30},{14,28},{16,2},... | collective-permute-start | bytes 393224 | tf_op jit(solution)/shard_map/ppermute | solution.py:265
  75.9 0.5 shard_map.79
  76.4 0.7 collective-permute-start.28
  77.1 2.8 %collective-permute-start.24 = (bf16[3,8,16,128]{3,2,1,0:T(8,128)(2,1)S(1)}, bf16[3,8,16,128]{3,2,1,0:T(8,128)(2,1)S(1)}, u32[]{:S(2)}, u32[]{:S(2)}) collective-permute-start(bf16[3,8,16,128]{3,2,1,0:T(8,128)(2,1)S(1)} %get-tuple-element.77), channel_id=1, source_target_pairs={{0,24},{2,26},{4,28},{6,30},{8,16},{10,18},{12,20},{14,22},{16,8},... | collective-permute-start | bytes 294920 | tf_op jit(solution)/shard_map/ppermute | solution.py:265
  79.9 4.7 %collective-permute-done.24.refs_2_ = bf16[3,8,16,128]{3,2,1,0:T(8,128)(2,1)S(1)} collective-permute-done((bf16[3,8,16,128]{3,2,1,0:T(8,128)(2,1)S(1)}, bf16[3,8,16,128]{3,2,1,0:T(8,128)(2,1)S(1)}, u32[]{:S(2)}, u32[]{:S(2)}) %collective-permute-start.24) | collective-permute-done | bytes 98336 | tf_op jit(solution)/shard_map/ppermute | solution.py:265
  84.6 0.4 collective-permute-start.29
  85.0 9.5 %collective-permute-done.25.refs_3_ = bf16[3,8,16,128]{3,2,1,0:T(8,128)(2,1)S(1)} collective-permute-done((bf16[3,8,16,128]{3,2,1,0:T(8,128)(2,1)S(1)}, bf16[3,8,16,128]{3,2,1,0:T(8,128)(2,1)S(1)}, u32[]{:S(2)}, u32[]{:S(2)}) %collective-permute-start.25) | collective-permute-done | bytes 98336 | tf_op jit(solution)/shard_map/ppermute | solution.py:265
  94.4 1.1 collective-permute-start.30
  95.5 1.0 collective-permute-start.31
  96.5 1.3 %collective-permute-start.32 = (bf16[4,8,16,128]{3,2,1,0:T(8,128)(2,1)S(1)}, bf16[4,8,16,128]{3,2,1,0:T(8,128)(2,1)S(1)}, u32[]{:S(2)}, u32[]{:S(2)}) collective-permute-start(bf16[4,8,16,128]{3,2,1,0:T(8,128)(2,1)S(1)} %get-tuple-element.87), channel_id=1, source_target_pairs={{0,10},{2,8},{4,14},{6,12},{8,2},{10,0},{12,6},{14,4},{16,26},{18,... | collective-permute-start | bytes 393224 | tf_op jit(solution)/shard_map/ppermute | solution.py:265
  97.9 1.0 collective-permute-start.33
  98.9 2.7 %collective-permute-start.18 = (bf16[4,8,16,128]{3,2,1,0:T(8,128)(2,1)S(1)}, bf16[4,8,16,128]{3,2,1,0:T(8,128)(2,1)S(1)}, u32[]{:S(2)}, u32[]{:S(2)}) collective-permute-start(bf16[4,8,16,128]{3,2,1,0:T(8,128)(2,1)S(1)} %get-tuple-element.71), channel_id=1, source_target_pairs={{0,28},{2,30},{4,24},{6,26},{8,20},{10,22},{12,16},{14,18},{16,12}... | collective-permute-start | bytes 393224 | tf_op jit(solution)/shard_map/ppermute | solution.py:265
  101.6 2.1 %collective-permute-start.19 = (bf16[4,8,16,128]{3,2,1,0:T(8,128)(2,1)S(1)}, bf16[4,8,16,128]{3,2,1,0:T(8,128)(2,1)S(1)}, u32[]{:S(2)}, u32[]{:S(2)}) collective-permute-start(bf16[4,8,16,128]{3,2,1,0:T(8,128)(2,1)S(1)} %get-tuple-element.72), channel_id=1, source_target_pairs={{0,20},{2,22},{4,16},{6,18},{8,28},{10,30},{12,24},{14,26},{16,4},... | collective-permute-start | bytes 393224 | tf_op jit(solution)/shard_map/ppermute | solution.py:265
  103.7 2.0 %collective-permute-start.34 = (bf16[4,8,16,128]{3,2,1,0:T(8,128)(2,1)S(1)}, bf16[4,8,16,128]{3,2,1,0:T(8,128)(2,1)S(1)}, u32[]{:S(2)}, u32[]{:S(2)}) collective-permute-start(bf16[4,8,16,128]{3,2,1,0:T(8,128)(2,1)S(1)} %get-tuple-element.89), channel_id=1, source_target_pairs={{0,14},{2,12},{4,10},{6,8},{8,6},{10,4},{12,2},{14,0},{16,30},{18,... | collective-permute-start | bytes 393224 | tf_op jit(solution)/shard_map/ppermute | solution.py:265
  105.7 6.1 %collective-permute-start.20 = (bf16[4,8,16,128]{3,2,1,0:T(8,128)(2,1)S(1)}, bf16[4,8,16,128]{3,2,1,0:T(8,128)(2,1)S(1)}, u32[]{:S(2)}, u32[]{:S(2)}) collective-permute-start(bf16[4,8,16,128]{3,2,1,0:T(8,128)(2,1)S(1)} %get-tuple-element.73), channel_id=1, source_target_pairs={{0,30},{2,28},{4,26},{6,24},{8,22},{10,20},{12,18},{14,16},{16,14}... | collective-permute-start | bytes 393224 | tf_op jit(solution)/shard_map/ppermute | solution.py:265
  111.8 1.0 collective-permute-done.33.refs_11_
  112.7 0.7 collective-permute-start.21
  113.5 1.0 collective-permute-done.34.refs_12_
  114.5 1.5 %shard_map.80.refs_4_ = bf16[16,16,4,8,128]{4,3,2,1,0:T(8,128)(2,1)} custom-call(s32[1]{0:T(128)} %bitcast.spot, bf16[1,8,16,128]{3,2,1,0:T(8,128)(2,1)S(1)} %collective-permute-done.22.refs_0_, bf16[1,8,16,128]{3,2,1,0:T(8,128)(2,1)S(1)} %collective-permute-done.23.refs_1_, bf16[3,8,16,128]{3,2,1,0:T(8,128)(2,1)S(1)} %collective-permute-done.24.refs_2_, ...), custom_call_target="tpu_custom_call" | custom-call | tf_op jit(solution)/shard_map/pallas_call | solution.py:418
  116.0 4.6 %collective-permute-done.20.refs_2_ = bf16[4,8,16,128]{3,2,1,0:T(8,128)(2,1)S(1)} collective-permute-done((bf16[4,8,16,128]{3,2,1,0:T(8,128)(2,1)S(1)}, bf16[4,8,16,128]{3,2,1,0:T(8,128)(2,1)S(1)}, u32[]{:S(2)}, u32[]{:S(2)}) %collective-permute-start.20) | collective-permute-done | bytes 131104 | tf_op jit(solution)/shard_map/ppermute | solution.py:265
  120.6 5.5 %collective-permute-done.21.refs_3_ = bf16[4,8,16,128]{3,2,1,0:T(8,128)(2,1)S(1)} collective-permute-done((bf16[4,8,16,128]{3,2,1,0:T(8,128)(2,1)S(1)}, bf16[4,8,16,128]{3,2,1,0:T(8,128)(2,1)S(1)}, u32[]{:S(2)}, u32[]{:S(2)}) %collective-permute-start.21) | collective-permute-done | bytes 131104 | tf_op jit(solution)/shard_map/ppermute | solution.py:265
  126.1 0.9 shard_map.81
  (38 shorter events, 0.1 us)
Async XLA Ops:
  0.0 6.7 %copy-start.5 = (bf16[1,4,128]{2,1,0:T(4,128)(2,1)S(1)}, bf16[1,4,128]{2,1,0:T(4,128)(2,1)}, u32[]{:S(2)}) copy-start(bf16[1,4,128]{2,1,0:T(4,128)(2,1)} %param.9) | copy-start | bytes 3076
  0.0 6.8 %copy-start.6 = (bf16[1,4,128]{2,1,0:T(4,128)(2,1)S(1)}, bf16[1,4,128]{2,1,0:T(4,128)(2,1)}, u32[]{:S(2)}) copy-start(bf16[1,4,128]{2,1,0:T(4,128)(2,1)} %param.10) | copy-start | bytes 3076
  0.0 6.8 %copy-start.7 = (s32[1,4]{1,0:T(1,128)S(1)}, s32[1,4]{1,0:T(1,128)}, u32[]{:S(2)}) copy-start(s32[1,4]{1,0:T(1,128)} %param.11) | copy-start | bytes 52
  0.0 6.8 %copy-start.4 = (s32[1,4,128]{2,1,0:T(4,128)S(1)}, s32[1,4,128]{2,1,0:T(4,128)}, u32[]{:S(2)}) copy-start(s32[1,4,128]{2,1,0:T(4,128)} %param.12) | copy-start | bytes 6148
  0.0 1.6 %copy-start = (bf16[16,1,64,8,128]{4,3,2,1,0:T(8,128)(2,1)S(1)}, bf16[16,1,64,8,128]{4,3,2,1,0:T(8,128)(2,1)}, u32[]{:S(2)}) copy-start(bf16[16,1,64,8,128]{4,3,2,1,0:T(8,128)(2,1)} %param.7) | copy-start | bytes 6291460
  1.7 13.8 %copy-start.1 = (bf16[16,1,64,8,128]{4,3,2,1,0:T(8,128)(2,1)S(1)}, bf16[16,1,64,8,128]{4,3,2,1,0:T(8,128)(2,1)}, u32[]{:S(2)}) copy-start(bf16[16,1,64,8,128]{4,3,2,1,0:T(8,128)(2,1)} %param.7) | copy-start | bytes 6291460
  2.1 54.9 %copy-start.2 = (bf16[1,4,256,128]{3,2,1,0:T(8,128)(2,1)S(1)}, bf16[1,4,256,128]{3,2,1,0:T(8,128)(2,1)}, u32[]{:S(2)}) copy-start(bf16[1,4,256,128]{3,2,1,0:T(8,128)(2,1)} %param.8) | copy-start | bytes 786436
  2.2 54.9 %copy-start.3 = (s32[1,4,4]{2,1,0:T(4,128)S(1)}, s32[1,4,4]{2,1,0:T(4,128)}, u32[]{:S(2)}) copy-start(s32[1,4,4]{2,1,0:T(4,128)} %param.13) | copy-start | bytes 196
  2.2 9.0 %collective-permute-start.2 = (bf16[16,4,8,128]{3,2,1,0:T(8,128)(2,1)S(1)}, bf16[16,4,8,128]{3,2,1,0:T(8,128)(2,1)S(1)}, u32[]{:S(2)}, u32[]{:S(2)}) collective-permute-start(bf16[16,4,8,128]{3,2,1,0:T(8,128)(2,1)S(1)} %get-tuple-element.51), channel_id=1, source_target_pairs={{0,2},{2,0},{4,6},{6,4},{8,10},{10,8},{12,14},{14,12},{16,18},{18,... | collective-permute-start | bytes 393224 | tf_op jit(solution)/shard_map/ppermute | solution.py:265
  5.2 7.8 %collective-permute-start.3 = (bf16[16,4,8,128]{3,2,1,0:T(8,128)(2,1)S(1)}, bf16[16,4,8,128]{3,2,1,0:T(8,128)(2,1)S(1)}, u32[]{:S(2)}, u32[]{:S(2)}) collective-permute-start(bf16[16,4,8,128]{3,2,1,0:T(8,128)(2,1)S(1)} %get-tuple-element.52), channel_id=1, source_target_pairs={{0,4},{2,6},{4,0},{6,2},{8,12},{10,14},{12,8},{14,10},{16,20},{18,... | collective-permute-start | bytes 393224 | tf_op jit(solution)/shard_map/ppermute | solution.py:265
  6.7 8.8 %collective-permute-start.4 = (bf16[16,4,8,128]{3,2,1,0:T(8,128)(2,1)S(1)}, bf16[16,4,8,128]{3,2,1,0:T(8,128)(2,1)S(1)}, u32[]{:S(2)}, u32[]{:S(2)}) collective-permute-start(bf16[16,4,8,128]{3,2,1,0:T(8,128)(2,1)S(1)} %get-tuple-element.53), channel_id=1, source_target_pairs={{0,6},{2,4},{4,2},{6,0},{8,14},{10,12},{12,10},{14,8},{16,22},{18,... | collective-permute-start | bytes 393224 | tf_op jit(solution)/shard_map/ppermute | solution.py:265
  7.0 2.1 %collective-permute-start.1 = (f32[4,8,128]{2,1,0:T(8,128)S(1)}, f32[4,8,128]{2,1,0:T(8,128)S(1)}, u32[]{:S(2)}, u32[]{:S(2)}) collective-permute-start(f32[4,8,128]{2,1,0:T(8,128)S(1)} %maximum_maximum_fusion.own_aux), channel_id=1, source_target_pairs={{0,1},{1,0},{2,3},{3,2},{4,5},{5,4},{6,7},{7,6},{8,9},{9,8},{10,11... | collective-permute-start | bytes 49160 | tf_op jit(solution)/shard_map/ppermute | solution.py:220
  7.0 8.5 %collective-permute-start.5 = (bf16[16,4,8,128]{3,2,1,0:T(8,128)(2,1)S(1)}, bf16[16,4,8,128]{3,2,1,0:T(8,128)(2,1)S(1)}, u32[]{:S(2)}, u32[]{:S(2)}) collective-permute-start(bf16[16,4,8,128]{3,2,1,0:T(8,128)(2,1)S(1)} %get-tuple-element.54), channel_id=1, source_target_pairs={{0,8},{2,10},{4,12},{6,14},{8,0},{10,2},{12,4},{14,6},{16,24},{18,... | collective-permute-start | bytes 393224 | tf_op jit(solution)/shard_map/ppermute | solution.py:265
  9.1 9.0 %collective-permute-start.6 = (bf16[16,4,8,128]{3,2,1,0:T(8,128)(2,1)S(1)}, bf16[16,4,8,128]{3,2,1,0:T(8,128)(2,1)S(1)}, u32[]{:S(2)}, u32[]{:S(2)}) collective-permute-start(bf16[16,4,8,128]{3,2,1,0:T(8,128)(2,1)S(1)} %get-tuple-element.55), channel_id=1, source_target_pairs={{0,10},{2,8},{4,14},{6,12},{8,2},{10,0},{12,6},{14,4},{16,26},{18,... | collective-permute-start | bytes 393224 | tf_op jit(solution)/shard_map/ppermute | solution.py:265
  11.2 9.3 %collective-permute-start.7 = (bf16[16,4,8,128]{3,2,1,0:T(8,128)(2,1)S(1)}, bf16[16,4,8,128]{3,2,1,0:T(8,128)(2,1)S(1)}, u32[]{:S(2)}, u32[]{:S(2)}) collective-permute-start(bf16[16,4,8,128]{3,2,1,0:T(8,128)(2,1)S(1)} %get-tuple-element.56), channel_id=1, source_target_pairs={{0,12},{2,14},{4,8},{6,10},{8,4},{10,6},{12,0},{14,2},{16,28},{18,... | collective-permute-start | bytes 393224 | tf_op jit(solution)/shard_map/ppermute | solution.py:265
  13.0 15.5 %collective-permute-start.8 = (bf16[16,4,8,128]{3,2,1,0:T(8,128)(2,1)S(1)}, bf16[16,4,8,128]{3,2,1,0:T(8,128)(2,1)S(1)}, u32[]{:S(2)}, u32[]{:S(2)}) collective-permute-start(bf16[16,4,8,128]{3,2,1,0:T(8,128)(2,1)S(1)} %get-tuple-element.57), channel_id=1, source_target_pairs={{0,14},{2,12},{4,10},{6,8},{8,6},{10,4},{12,2},{14,0},{16,30},{18,... | collective-permute-start | bytes 393224 | tf_op jit(solution)/shard_map/ppermute | solution.py:265
  15.5 36.1 %collective-permute-start = (bf16[4,256,128]{2,1,0:T(8,128)(2,1)}, bf16[4,256,128]{2,1,0:T(8,128)(2,1)S(1)}, u32[]{:S(2)}, u32[]{:S(2)}) collective-permute-start(bf16[4,256,128]{2,1,0:T(8,128)(2,1)} %bitcast.15), channel_id=1, source_target_pairs={{0,1},{1,0},{2,3},{3,2},{4,5},{5,4},{6,7},{7,6},{8,9},{9,8},{10,11... | collective-permute-start | bytes 786440 | tf_op jit(solution)/shard_map/ppermute | solution.py:220
  15.6 13.0 %collective-permute-start.9 = (bf16[16,4,8,128]{3,2,1,0:T(8,128)(2,1)S(1)}, bf16[16,4,8,128]{3,2,1,0:T(8,128)(2,1)S(1)}, u32[]{:S(2)}, u32[]{:S(2)}) collective-permute-start(bf16[16,4,8,128]{3,2,1,0:T(8,128)(2,1)S(1)} %get-tuple-element.58), channel_id=1, source_target_pairs={{0,24},{2,26},{4,28},{6,30},{8,16},{10,18},{12,20},{14,22},{16,8},... | collective-permute-start | bytes 393224 | tf_op jit(solution)/shard_map/ppermute | solution.py:265
  18.1 21.3 %collective-permute-start.10 = (bf16[16,4,8,128]{3,2,1,0:T(8,128)(2,1)S(1)}, bf16[16,4,8,128]{3,2,1,0:T(8,128)(2,1)S(1)}, u32[]{:S(2)}, u32[]{:S(2)}) collective-permute-start(bf16[16,4,8,128]{3,2,1,0:T(8,128)(2,1)S(1)} %get-tuple-element.59), channel_id=1, source_target_pairs={{0,16},{2,18},{4,20},{6,22},{8,24},{10,26},{12,28},{14,30},{16,0},... | collective-permute-start | bytes 393224 | tf_op jit(solution)/shard_map/ppermute | solution.py:265
  20.5 19.1 %collective-permute-start.11 = (bf16[16,4,8,128]{3,2,1,0:T(8,128)(2,1)S(1)}, bf16[16,4,8,128]{3,2,1,0:T(8,128)(2,1)S(1)}, u32[]{:S(2)}, u32[]{:S(2)}) collective-permute-start(bf16[16,4,8,128]{3,2,1,0:T(8,128)(2,1)S(1)} %get-tuple-element.60), channel_id=1, source_target_pairs={{0,26},{2,24},{4,30},{6,28},{8,18},{10,16},{12,22},{14,20},{16,10}... | collective-permute-start | bytes 393224 | tf_op jit(solution)/shard_map/ppermute | solution.py:265
  28.5 23.1 %collective-permute-start.12 = (bf16[16,4,8,128]{3,2,1,0:T(8,128)(2,1)S(1)}, bf16[16,4,8,128]{3,2,1,0:T(8,128)(2,1)S(1)}, u32[]{:S(2)}, u32[]{:S(2)}) collective-permute-start(bf16[16,4,8,128]{3,2,1,0:T(8,128)(2,1)S(1)} %get-tuple-element.61), channel_id=1, source_target_pairs={{0,18},{2,16},{4,22},{6,20},{8,26},{10,24},{12,30},{14,28},{16,2},... | collective-permute-start | bytes 393224 | tf_op jit(solution)/shard_map/ppermute | solution.py:265
  28.5 39.5 %collective-permute-start.13 = (bf16[16,4,8,128]{3,2,1,0:T(8,128)(2,1)S(1)}, bf16[16,4,8,128]{3,2,1,0:T(8,128)(2,1)S(1)}, u32[]{:S(2)}, u32[]{:S(2)}) collective-permute-start(bf16[16,4,8,128]{3,2,1,0:T(8,128)(2,1)S(1)} %get-tuple-element.64), channel_id=1, source_target_pairs={{0,28},{2,30},{4,24},{6,26},{8,20},{10,22},{12,16},{14,18},{16,12}... | collective-permute-start | bytes 393224 | tf_op jit(solution)/shard_map/ppermute | solution.py:265
  39.4 28.6 %collective-permute-start.14 = (bf16[16,4,8,128]{3,2,1,0:T(8,128)(2,1)S(1)}, bf16[16,4,8,128]{3,2,1,0:T(8,128)(2,1)S(1)}, u32[]{:S(2)}, u32[]{:S(2)}) collective-permute-start(bf16[16,4,8,128]{3,2,1,0:T(8,128)(2,1)S(1)} %get-tuple-element.65), channel_id=1, source_target_pairs={{0,20},{2,22},{4,16},{6,18},{8,28},{10,30},{12,24},{14,26},{16,4},... | collective-permute-start | bytes 393224 | tf_op jit(solution)/shard_map/ppermute | solution.py:265
  39.6 28.5 %collective-permute-start.15 = (bf16[16,4,8,128]{3,2,1,0:T(8,128)(2,1)S(1)}, bf16[16,4,8,128]{3,2,1,0:T(8,128)(2,1)S(1)}, u32[]{:S(2)}, u32[]{:S(2)}) collective-permute-start(bf16[16,4,8,128]{3,2,1,0:T(8,128)(2,1)S(1)} %get-tuple-element.66), channel_id=1, source_target_pairs={{0,30},{2,28},{4,26},{6,24},{8,22},{10,20},{12,18},{14,16},{16,14}... | collective-permute-start | bytes 393224 | tf_op jit(solution)/shard_map/ppermute | solution.py:265
  51.6 16.4 %collective-permute-start.16 = (bf16[16,1,8,128]{3,2,1,0:T(8,128)(2,1)S(1)}, bf16[16,1,8,128]{3,2,1,0:T(8,128)(2,1)S(1)}, u32[]{:S(2)}, u32[]{:S(2)}) collective-permute-start(bf16[16,1,8,128]{3,2,1,0:T(8,128)(2,1)S(1)} %get-tuple-element.67), channel_id=1, source_target_pairs={{0,22},{2,20},{4,18},{6,16},{8,30},{10,28},{12,26},{14,24},{16,6},... | collective-permute-start | bytes 98312 | tf_op jit(solution)/shard_map/ppermute | solution.py:265
  51.6 19.7 %collective-permute-start.17 = (bf16[16,3,8,128]{3,2,1,0:T(8,128)(2,1)S(1)}, bf16[16,3,8,128]{3,2,1,0:T(8,128)(2,1)S(1)}, u32[]{:S(2)}, u32[]{:S(2)}) collective-permute-start(bf16[16,3,8,128]{3,2,1,0:T(8,128)(2,1)S(1)} %get-tuple-element.70), channel_id=1, source_target_pairs={{0,22},{2,20},{4,18},{6,16},{8,30},{10,28},{12,26},{14,24},{16,6},... | collective-permute-start | bytes 294920 | tf_op jit(solution)/shard_map/ppermute | solution.py:265
  68.3 8.8 %collective-permute-start.22 = (bf16[1,8,16,128]{3,2,1,0:T(8,128)(2,1)S(1)}, bf16[1,8,16,128]{3,2,1,0:T(8,128)(2,1)S(1)}, u32[]{:S(2)}, u32[]{:S(2)}) collective-permute-start(bf16[1,8,16,128]{3,2,1,0:T(8,128)(2,1)S(1)} %get-tuple-element.75), channel_id=1, source_target_pairs={{0,24},{2,26},{4,28},{6,30},{8,16},{10,18},{12,20},{14,22},{16,8},... | collective-permute-start | bytes 98312 | tf_op jit(solution)/shard_map/ppermute | solution.py:265
  71.3 8.6 %collective-permute-start.23 = (bf16[1,8,16,128]{3,2,1,0:T(8,128)(2,1)S(1)}, bf16[1,8,16,128]{3,2,1,0:T(8,128)(2,1)S(1)}, u32[]{:S(2)}, u32[]{:S(2)}) collective-permute-start(bf16[1,8,16,128]{3,2,1,0:T(8,128)(2,1)S(1)} %get-tuple-element.76), channel_id=1, source_target_pairs={{0,16},{2,18},{4,20},{6,22},{8,24},{10,26},{12,28},{14,30},{16,0},... | collective-permute-start | bytes 98312 | tf_op jit(solution)/shard_map/ppermute | solution.py:265
  72.0 23.6 %collective-permute-start.26 = (bf16[4,8,16,128]{3,2,1,0:T(8,128)(2,1)S(1)}, bf16[4,8,16,128]{3,2,1,0:T(8,128)(2,1)S(1)}, u32[]{:S(2)}, u32[]{:S(2)}) collective-permute-start(bf16[4,8,16,128]{3,2,1,0:T(8,128)(2,1)S(1)} %get-tuple-element.79), channel_id=1, source_target_pairs={{0,26},{2,24},{4,30},{6,28},{8,18},{10,16},{12,22},{14,20},{16,10}... | collective-permute-start | bytes 393224 | tf_op jit(solution)/shard_map/ppermute | solution.py:265
  72.9 23.6 %collective-permute-start.27 = (bf16[4,8,16,128]{3,2,1,0:T(8,128)(2,1)S(1)}, bf16[4,8,16,128]{3,2,1,0:T(8,128)(2,1)S(1)}, u32[]{:S(2)}, u32[]{:S(2)}) collective-permute-start(bf16[4,8,16,128]{3,2,1,0:T(8,128)(2,1)S(1)} %get-tuple-element.80), channel_id=1, source_target_pairs={{0,18},{2,16},{4,22},{6,20},{8,26},{10,24},{12,30},{14,28},{16,2},... | collective-permute-start | bytes 393224 | tf_op jit(solution)/shard_map/ppermute | solution.py:265
  76.4 21.5 %collective-permute-start.28 = (bf16[4,8,16,128]{3,2,1,0:T(8,128)(2,1)S(1)}, bf16[4,8,16,128]{3,2,1,0:T(8,128)(2,1)S(1)}, u32[]{:S(2)}, u32[]{:S(2)}) collective-permute-start(bf16[4,8,16,128]{3,2,1,0:T(8,128)(2,1)S(1)} %get-tuple-element.83), channel_id=1, source_target_pairs={{0,2},{2,0},{4,6},{6,4},{8,10},{10,8},{12,14},{14,12},{16,18},{18,... | collective-permute-start | bytes 393224 | tf_op jit(solution)/shard_map/ppermute | solution.py:265
  77.1 7.5 %collective-permute-start.24 = (bf16[3,8,16,128]{3,2,1,0:T(8,128)(2,1)S(1)}, bf16[3,8,16,128]{3,2,1,0:T(8,128)(2,1)S(1)}, u32[]{:S(2)}, u32[]{:S(2)}) collective-permute-start(bf16[3,8,16,128]{3,2,1,0:T(8,128)(2,1)S(1)} %get-tuple-element.77), channel_id=1, source_target_pairs={{0,24},{2,26},{4,28},{6,30},{8,16},{10,18},{12,20},{14,22},{16,8},... | collective-permute-start | bytes 294920 | tf_op jit(solution)/shard_map/ppermute | solution.py:265
  79.9 14.5 %collective-permute-start.25 = (bf16[3,8,16,128]{3,2,1,0:T(8,128)(2,1)S(1)}, bf16[3,8,16,128]{3,2,1,0:T(8,128)(2,1)S(1)}, u32[]{:S(2)}, u32[]{:S(2)}) collective-permute-start(bf16[3,8,16,128]{3,2,1,0:T(8,128)(2,1)S(1)} %get-tuple-element.78), channel_id=1, source_target_pairs={{0,16},{2,18},{4,20},{6,22},{8,24},{10,26},{12,28},{14,30},{16,0},... | collective-permute-start | bytes 294920 | tf_op jit(solution)/shard_map/ppermute | solution.py:265
  84.6 14.3 %collective-permute-start.29 = (bf16[4,8,16,128]{3,2,1,0:T(8,128)(2,1)S(1)}, bf16[4,8,16,128]{3,2,1,0:T(8,128)(2,1)S(1)}, u32[]{:S(2)}, u32[]{:S(2)}) collective-permute-start(bf16[4,8,16,128]{3,2,1,0:T(8,128)(2,1)S(1)} %get-tuple-element.84), channel_id=1, source_target_pairs={{0,4},{2,6},{4,0},{6,2},{8,12},{10,14},{12,8},{14,10},{16,20},{18,... | collective-permute-start | bytes 393224 | tf_op jit(solution)/shard_map/ppermute | solution.py:265
  94.4 7.2 %collective-permute-start.30 = (bf16[4,8,16,128]{3,2,1,0:T(8,128)(2,1)S(1)}, bf16[4,8,16,128]{3,2,1,0:T(8,128)(2,1)S(1)}, u32[]{:S(2)}, u32[]{:S(2)}) collective-permute-start(bf16[4,8,16,128]{3,2,1,0:T(8,128)(2,1)S(1)} %get-tuple-element.85), channel_id=1, source_target_pairs={{0,6},{2,4},{4,2},{6,0},{8,14},{10,12},{12,10},{14,8},{16,22},{18,... | collective-permute-start | bytes 393224 | tf_op jit(solution)/shard_map/ppermute | solution.py:265
  95.5 8.1 %collective-permute-start.31 = (bf16[4,8,16,128]{3,2,1,0:T(8,128)(2,1)S(1)}, bf16[4,8,16,128]{3,2,1,0:T(8,128)(2,1)S(1)}, u32[]{:S(2)}, u32[]{:S(2)}) collective-permute-start(bf16[4,8,16,128]{3,2,1,0:T(8,128)(2,1)S(1)} %get-tuple-element.86), channel_id=1, source_target_pairs={{0,8},{2,10},{4,12},{6,14},{8,0},{10,2},{12,4},{14,6},{16,24},{18,... | collective-permute-start | bytes 393224 | tf_op jit(solution)/shard_map/ppermute | solution.py:265
  96.5 9.1 %collective-permute-start.32 = (bf16[4,8,16,128]{3,2,1,0:T(8,128)(2,1)S(1)}, bf16[4,8,16,128]{3,2,1,0:T(8,128)(2,1)S(1)}, u32[]{:S(2)}, u32[]{:S(2)}) collective-permute-start(bf16[4,8,16,128]{3,2,1,0:T(8,128)(2,1)S(1)} %get-tuple-element.87), channel_id=1, source_target_pairs={{0,10},{2,8},{4,14},{6,12},{8,2},{10,0},{12,6},{14,4},{16,26},{18,... | collective-permute-start | bytes 393224 | tf_op jit(solution)/shard_map/ppermute | solution.py:265
  97.9 14.9 %collective-permute-start.33 = (bf16[4,8,16,128]{3,2,1,0:T(8,128)(2,1)S(1)}, bf16[4,8,16,128]{3,2,1,0:T(8,128)(2,1)S(1)}, u32[]{:S(2)}, u32[]{:S(2)}) collective-permute-start(bf16[4,8,16,128]{3,2,1,0:T(8,128)(2,1)S(1)} %get-tuple-element.88), channel_id=1, source_target_pairs={{0,12},{2,14},{4,8},{6,10},{8,4},{10,6},{12,0},{14,2},{16,28},{18,... | collective-permute-start | bytes 393224 | tf_op jit(solution)/shard_map/ppermute | solution.py:265
  98.9 17.1 %collective-permute-start.18 = (bf16[4,8,16,128]{3,2,1,0:T(8,128)(2,1)S(1)}, bf16[4,8,16,128]{3,2,1,0:T(8,128)(2,1)S(1)}, u32[]{:S(2)}, u32[]{:S(2)}) collective-permute-start(bf16[4,8,16,128]{3,2,1,0:T(8,128)(2,1)S(1)} %get-tuple-element.71), channel_id=1, source_target_pairs={{0,28},{2,30},{4,24},{6,26},{8,20},{10,22},{12,16},{14,18},{16,12}... | collective-permute-start | bytes 393224 | tf_op jit(solution)/shard_map/ppermute | solution.py:265
  101.6 14.4 %collective-permute-start.19 = (bf16[4,8,16,128]{3,2,1,0:T(8,128)(2,1)S(1)}, bf16[4,8,16,128]{3,2,1,0:T(8,128)(2,1)S(1)}, u32[]{:S(2)}, u32[]{:S(2)}) collective-permute-start(bf16[4,8,16,128]{3,2,1,0:T(8,128)(2,1)S(1)} %get-tuple-element.72), channel_id=1, source_target_pairs={{0,20},{2,22},{4,16},{6,18},{8,28},{10,30},{12,24},{14,26},{16,4},... | collective-permute-start | bytes 393224 | tf_op jit(solution)/shard_map/ppermute | solution.py:265
  103.7 10.8 %collective-permute-start.34 = (bf16[4,8,16,128]{3,2,1,0:T(8,128)(2,1)S(1)}, bf16[4,8,16,128]{3,2,1,0:T(8,128)(2,1)S(1)}, u32[]{:S(2)}, u32[]{:S(2)}) collective-permute-start(bf16[4,8,16,128]{3,2,1,0:T(8,128)(2,1)S(1)} %get-tuple-element.89), channel_id=1, source_target_pairs={{0,14},{2,12},{4,10},{6,8},{8,6},{10,4},{12,2},{14,0},{16,30},{18,... | collective-permute-start | bytes 393224 | tf_op jit(solution)/shard_map/ppermute | solution.py:265
  105.7 14.9 %collective-permute-start.20 = (bf16[4,8,16,128]{3,2,1,0:T(8,128)(2,1)S(1)}, bf16[4,8,16,128]{3,2,1,0:T(8,128)(2,1)S(1)}, u32[]{:S(2)}, u32[]{:S(2)}) collective-permute-start(bf16[4,8,16,128]{3,2,1,0:T(8,128)(2,1)S(1)} %get-tuple-element.73), channel_id=1, source_target_pairs={{0,30},{2,28},{4,26},{6,24},{8,22},{10,20},{12,18},{14,16},{16,14}... | collective-permute-start | bytes 393224 | tf_op jit(solution)/shard_map/ppermute | solution.py:265
  112.7 13.4 %collective-permute-start.21 = (bf16[4,8,16,128]{3,2,1,0:T(8,128)(2,1)S(1)}, bf16[4,8,16,128]{3,2,1,0:T(8,128)(2,1)S(1)}, u32[]{:S(2)}, u32[]{:S(2)}) collective-permute-start(bf16[4,8,16,128]{3,2,1,0:T(8,128)(2,1)S(1)} %get-tuple-element.74), channel_id=1, source_target_pairs={{0,22},{2,20},{4,18},{6,16},{8,30},{10,28},{12,26},{14,24},{16,6},... | collective-permute-start | bytes 393224 | tf_op jit(solution)/shard_map/ppermute | solution.py:265

commit v4 on v3

--- a/solution.py
+++ b/solution.py
@@ -14,6 +14,7 @@
 
 LATE = 4
 LEAD = 2
+PLACE = (9, 14)
 MIB = 1 << 20
 
 
@@ -224,9 +225,15 @@
 
 
 def send_order(wide):
-    far = list(range(wide // 2, wide))
-    half = len(far) // 2
-    return [s for pair in zip(far[half:], far[:half]) for s in pair], list(range(1, wide // 2))
+    near = list(range(1, wide // 2))
+    return list(range(wide // 2, wide)), near[wide // 4 - 1:] + near[:wide // 4 - 1]
+
+
+def interleave(a, b):
+    mixed = []
+    for k, s in enumerate(a):
+        mixed += [s] + b[k:k + 1]
+    return mixed + b[len(a):]
 
 
 def on_device(
@@ -279,7 +286,7 @@
                     jax.ShapeDtypeStruct((mine, stop - start, depth, points), jnp.bfloat16)
                     for _, start, stop in blocks
                 ],
-                [smem, hbm],
+                [smem, pl.BlockSpec(memory_space=pltpu.HBM)],
                 [pltpu.SemaphoreType.DMA((len(blocks),))],
                 8,
             )(me.reshape(1), fields)
@@ -429,9 +436,12 @@
             input_output_aliases={1 + len(group): 0} if rest else {},
         )(me.reshape(1), *[part for _, _, part in group], *rest)
 
-    most = place([x for x in back if x[0] not in late])
-    final = place([x for x in back if x[0] in late], most)
-    return final.reshape(prior_states.shape)
+    turn = {s: k for k, s in enumerate([0] + far[:LEAD] + interleave(far[LEAD:], near_by))}
+    back.sort(key=lambda x: turn[x[0]])
+    final = []
+    for start, stop in zip((0,) + PLACE, PLACE + (len(back),)):
+        final = [place(back[start:stop], *final)]
+    return final[0].reshape(prior_states.shape)
 
 
 def solution(mesh):

time: 127 us -> 124 us (0.976)
  waiting for transfers between devices: 47 us -> 40.3 us
  starting transfers between devices: 61.9 us -> 65 us
    ppermute x33, waiting for transfers between devices: 47 us -> 39.4 us  [swap(): return lax.ppermute(x, 'wide', [(i, i ^ s) for i in range(wide)])]
    ppermute x33, starting transfers between devices: 61.9 us -> 65 us  [swap(): return lax.ppermute(x, 'wide', [(i, i ^ s) for i in range(wide)])]
    pallas_call x2 -> x3, Pallas kernels: 2.43 us -> 3.08 us  [place(): call(functools.partial(place_kernel, [(s, start) for s, start, _ in group...]
  transfers between devices with their start and end apart: 35 -> 35, of which waited for: 10 -> 14; matrix products, arithmetic and copies ran while one was open for 0% -> 0% of each run, Pallas kernels for 12% -> 13%
where the time goes in v4:
time: 124 us
  starting transfers between devices  65 us (52%)
  waiting for transfers between devices  40.3 us (32%)
  Pallas kernels  16.7 us (13%)
  local copies, waits for them, and re-layouts  1.69 us (1%)
    ppermute x33, starting transfers between devices, swap(): return lax.ppermute(x, 'wide', [(i, i ^ s) for i in range(wide)])  65 us
    ppermute x33, waiting for transfers between devices, swap(): return lax.ppermute(x, 'wide', [(i, i ^ s) for i in range(wide)])  39.4 us
    pallas_call x1, Pallas kernels, on_device(): call(functools.partial(mix_kernel, order), [jax.ShapeDtypeStruct((tiles,...  11 us
    pallas_call x3, Pallas kernels, place(): call(functools.partial(place_kernel, [(s, start) for s, start, _ in group...  3.08 us
  transfers between devices with their start and end apart: 35, of which 14 were waited for; matrix products, arithmetic and copies ran while one was open for 0% of the time, Pallas kernels for 13%

profile of v4, /device:TPU:0, one launch (start us, length us, event | category | flops | bytes accessed | tf_op | source)
XLA Modules:
  0.0 124.1 jit_solution(8208685798323695810)
XLA Ops:
  0.0 1.6 %copy-done = bf16[16,1,64,8,128]{4,3,2,1,0:T(8,128)(2,1)S(1)} copy-done((bf16[16,1,64,8,128]{4,3,2,1,0:T(8,128)(2,1)S(1)}, bf16[16,1,64,8,128]{4,3,2,1,0:T(8,128)(2,1)}, u32[]{:S(2)}) %copy-start) | copy-done | bytes 2097176
  1.6 0.1 shard_map.75
  1.7 0.0 copy-start.2
  1.7 4.1 %collective-permute-start.9 = (bf16[16,4,8,128]{3,2,1,0:T(8,128)(2,1)S(1)}, bf16[16,4,8,128]{3,2,1,0:T(8,128)(2,1)S(1)}, u32[]{:S(2)}, u32[]{:S(2)}) collective-permute-start(bf16[16,4,8,128]{3,2,1,0:T(8,128)(2,1)S(1)} %get-tuple-element.58), channel_id=1, source_target_pairs={{0,16},{2,18},{4,20},{6,22},{8,24},{10,26},{12,28},{14,30},{16,0},... | collective-permute-start | bytes 393224 | tf_op jit(solution)/shard_map/ppermute | solution.py:272
  5.8 1.3 %collective-permute-start.10 = (bf16[16,4,8,128]{3,2,1,0:T(8,128)(2,1)S(1)}, bf16[16,4,8,128]{3,2,1,0:T(8,128)(2,1)S(1)}, u32[]{:S(2)}, u32[]{:S(2)}) collective-permute-start(bf16[16,4,8,128]{3,2,1,0:T(8,128)(2,1)S(1)} %get-tuple-element.59), channel_id=1, source_target_pairs={{0,18},{2,16},{4,22},{6,20},{8,26},{10,24},{12,30},{14,28},{16,2},... | collective-permute-start | bytes 393224 | tf_op jit(solution)/shard_map/ppermute | solution.py:272
  7.1 0.5 shard_map.74
  7.6 1.6 %collective-permute-start.2 = (bf16[16,4,8,128]{3,2,1,0:T(8,128)(2,1)S(1)}, bf16[16,4,8,128]{3,2,1,0:T(8,128)(2,1)S(1)}, u32[]{:S(2)}, u32[]{:S(2)}) collective-permute-start(bf16[16,4,8,128]{3,2,1,0:T(8,128)(2,1)S(1)} %get-tuple-element.51), channel_id=1, source_target_pairs={{0,8},{2,10},{4,12},{6,14},{8,0},{10,2},{12,4},{14,6},{16,24},{18,... | collective-permute-start | bytes 393224 | tf_op jit(solution)/shard_map/ppermute | solution.py:272
  9.2 0.1 pad.2.clone
  9.3 0.1 convert_multiply_fusion
  9.4 0.1 maximum_maximum_fusion.own_aux
  9.5 0.0 collective-permute-start.1
  9.5 0.2 collective-permute-start.3
  9.7 0.9 collective-permute-done.1
  10.7 1.9 %collective-permute-start.4 = (bf16[16,4,8,128]{3,2,1,0:T(8,128)(2,1)S(1)}, bf16[16,4,8,128]{3,2,1,0:T(8,128)(2,1)S(1)}, u32[]{:S(2)}, u32[]{:S(2)}) collective-permute-start(bf16[16,4,8,128]{3,2,1,0:T(8,128)(2,1)S(1)} %get-tuple-element.53), channel_id=1, source_target_pairs={{0,12},{2,14},{4,8},{6,10},{8,4},{10,6},{12,0},{14,2},{16,28},{18,... | collective-permute-start | bytes 393224 | tf_op jit(solution)/shard_map/ppermute | solution.py:272
  12.5 3.3 %collective-permute-done.9.refs_8_ = bf16[16,4,8,128]{3,2,1,0:T(8,128)(2,1)S(1)} collective-permute-done((bf16[16,4,8,128]{3,2,1,0:T(8,128)(2,1)S(1)}, bf16[16,4,8,128]{3,2,1,0:T(8,128)(2,1)S(1)}, u32[]{:S(2)}, u32[]{:S(2)}) %collective-permute-start.9) | collective-permute-done | bytes 131104 | tf_op jit(solution)/shard_map/ppermute | solution.py:272
  15.8 1.9 %collective-permute-start.5 = (bf16[16,4,8,128]{3,2,1,0:T(8,128)(2,1)S(1)}, bf16[16,4,8,128]{3,2,1,0:T(8,128)(2,1)S(1)}, u32[]{:S(2)}, u32[]{:S(2)}) collective-permute-start(bf16[16,4,8,128]{3,2,1,0:T(8,128)(2,1)S(1)} %get-tuple-element.54), channel_id=1, source_target_pairs={{0,14},{2,12},{4,10},{6,8},{8,6},{10,4},{12,2},{14,0},{16,30},{18,... | collective-permute-start | bytes 393224 | tf_op jit(solution)/shard_map/ppermute | solution.py:272
  17.7 1.1 collective-permute-done.10.refs_9_
  18.8 0.4 collective-permute-start.6
  19.2 0.0 collective-permute-done.2.refs_1_
  19.2 1.8 %collective-permute-done.3.refs_2_ = bf16[16,4,8,128]{3,2,1,0:T(8,128)(2,1)S(1)} collective-permute-done((bf16[16,4,8,128]{3,2,1,0:T(8,128)(2,1)S(1)}, bf16[16,4,8,128]{3,2,1,0:T(8,128)(2,1)S(1)}, u32[]{:S(2)}, u32[]{:S(2)}) %collective-permute-start.3) | collective-permute-done | bytes 131104 | tf_op jit(solution)/shard_map/ppermute | solution.py:272
  21.0 1.5 %collective-permute-start.7 = (bf16[16,4,8,128]{3,2,1,0:T(8,128)(2,1)S(1)}, bf16[16,4,8,128]{3,2,1,0:T(8,128)(2,1)S(1)}, u32[]{:S(2)}, u32[]{:S(2)}) collective-permute-start(bf16[16,4,8,128]{3,2,1,0:T(8,128)(2,1)S(1)} %get-tuple-element.56), channel_id=1, source_target_pairs={{0,4},{2,6},{4,0},{6,2},{8,12},{10,14},{12,8},{14,10},{16,20},{18,... | collective-permute-start | bytes 393224 | tf_op jit(solution)/shard_map/ppermute | solution.py:272
  22.6 1.2 collective-permute-done.4.refs_3_
  23.7 1.9 %collective-permute-start.8 = (bf16[16,4,8,128]{3,2,1,0:T(8,128)(2,1)S(1)}, bf16[16,4,8,128]{3,2,1,0:T(8,128)(2,1)S(1)}, u32[]{:S(2)}, u32[]{:S(2)}) collective-permute-start(bf16[16,4,8,128]{3,2,1,0:T(8,128)(2,1)S(1)} %get-tuple-element.57), channel_id=1, source_target_pairs={{0,6},{2,4},{4,2},{6,0},{8,14},{10,12},{12,10},{14,8},{16,22},{18,... | collective-permute-start | bytes 393224 | tf_op jit(solution)/shard_map/ppermute | solution.py:272
  25.6 1.9 %collective-permute-done.5.refs_4_ = bf16[16,4,8,128]{3,2,1,0:T(8,128)(2,1)S(1)} collective-permute-done((bf16[16,4,8,128]{3,2,1,0:T(8,128)(2,1)S(1)}, bf16[16,4,8,128]{3,2,1,0:T(8,128)(2,1)S(1)}, u32[]{:S(2)}, u32[]{:S(2)}) %collective-permute-start.5) | collective-permute-done | bytes 131104 | tf_op jit(solution)/shard_map/ppermute | solution.py:272
  27.5 1.7 %collective-permute-start.11 = (bf16[16,4,8,128]{3,2,1,0:T(8,128)(2,1)S(1)}, bf16[16,4,8,128]{3,2,1,0:T(8,128)(2,1)S(1)}, u32[]{:S(2)}, u32[]{:S(2)}) collective-permute-start(bf16[16,4,8,128]{3,2,1,0:T(8,128)(2,1)S(1)} %get-tuple-element.60), channel_id=1, source_target_pairs={{0,20},{2,22},{4,16},{6,18},{8,28},{10,30},{12,24},{14,26},{16,4},... | collective-permute-start | bytes 393224 | tf_op jit(solution)/shard_map/ppermute | solution.py:272
  29.2 0.0 collective-permute-done.6.refs_5_
  29.2 2.1 %collective-permute-start.12 = (bf16[16,4,8,128]{3,2,1,0:T(8,128)(2,1)S(1)}, bf16[16,4,8,128]{3,2,1,0:T(8,128)(2,1)S(1)}, u32[]{:S(2)}, u32[]{:S(2)}) collective-permute-start(bf16[16,4,8,128]{3,2,1,0:T(8,128)(2,1)S(1)} %get-tuple-element.61), channel_id=1, source_target_pairs={{0,22},{2,20},{4,18},{6,16},{8,30},{10,28},{12,26},{14,24},{16,6},... | collective-permute-start | bytes 393224 | tf_op jit(solution)/shard_map/ppermute | solution.py:272
  31.3 0.9 collective-permute-done.7.refs_6_
  32.2 4.6 %collective-permute-start.16 = (bf16[16,1,8,128]{3,2,1,0:T(8,128)(2,1)S(1)}, bf16[16,1,8,128]{3,2,1,0:T(8,128)(2,1)S(1)}, u32[]{:S(2)}, u32[]{:S(2)}) collective-permute-start(bf16[16,1,8,128]{3,2,1,0:T(8,128)(2,1)S(1)} %get-tuple-element.67), channel_id=1, source_target_pairs={{0,30},{2,28},{4,26},{6,24},{8,22},{10,20},{12,18},{14,16},{16,14}... | collective-permute-start | bytes 98312 | tf_op jit(solution)/shard_map/ppermute | solution.py:272
  36.8 1.1 collective-permute-start.17
  37.8 3.4 %collective-permute-done.11.refs_10_ = bf16[16,4,8,128]{3,2,1,0:T(8,128)(2,1)S(1)} collective-permute-done((bf16[16,4,8,128]{3,2,1,0:T(8,128)(2,1)S(1)}, bf16[16,4,8,128]{3,2,1,0:T(8,128)(2,1)S(1)}, u32[]{:S(2)}, u32[]{:S(2)}) %collective-permute-start.11) | collective-permute-done | bytes 131104 | tf_op jit(solution)/shard_map/ppermute | solution.py:272
  41.2 1.2 collective-permute-start.13
  42.4 4.7 %collective-permute-done.12.refs_11_ = bf16[16,4,8,128]{3,2,1,0:T(8,128)(2,1)S(1)} collective-permute-done((bf16[16,4,8,128]{3,2,1,0:T(8,128)(2,1)S(1)}, bf16[16,4,8,128]{3,2,1,0:T(8,128)(2,1)S(1)}, u32[]{:S(2)}, u32[]{:S(2)}) %collective-permute-start.12) | collective-permute-done | bytes 131104 | tf_op jit(solution)/shard_map/ppermute | solution.py:272
  47.1 1.2 collective-permute-start.14
  48.3 6.0 %collective-permute-start.15 = (bf16[16,4,8,128]{3,2,1,0:T(8,128)(2,1)S(1)}, bf16[16,4,8,128]{3,2,1,0:T(8,128)(2,1)S(1)}, u32[]{:S(2)}, u32[]{:S(2)}) collective-permute-start(bf16[16,4,8,128]{3,2,1,0:T(8,128)(2,1)S(1)} %get-tuple-element.66), channel_id=1, source_target_pairs={{0,28},{2,30},{4,24},{6,26},{8,20},{10,22},{12,16},{14,18},{16,12}... | collective-permute-start | bytes 393224 | tf_op jit(solution)/shard_map/ppermute | solution.py:272
  54.3 0.7 shard_map.76
  55.0 11.0 %shard_map.73 = (bf16[4,256,256]{2,1,0:T(8,128)(2,1)S(1)}, f32[4,256,128]{2,1,0:T(8,128)S(1)}) custom-call(s32[4,4]{1,0:T(4,128)S(1)} %bitcast.17, s32[1]{0:T(128)} %bitcast.spot, bf16[4,256,128]{2,1,0:T(8,128)(2,1)S(1)} %bitcast.16, bf16[4,256,128]{2,1,0:T(8,128)(2,1)S(1)} %collective-permute-done.below.above, ...), custom_call_target="tpu_custom_call" | custom-call | tf_op jit(solution)/shard_map/pallas_call | solution.py:329
  66.0 0.0 collective-permute-done.13.refs_0_
  66.1 0.2 shard_map.77
  66.3 0.1 collective-permute-start.27
  66.4 2.8 %collective-permute-start.29 = (bf16[1,8,16,128]{3,2,1,0:T(8,128)(2,1)S(1)}, bf16[1,8,16,128]{3,2,1,0:T(8,128)(2,1)S(1)}, u32[]{:S(2)}, u32[]{:S(2)}) collective-permute-start(bf16[1,8,16,128]{3,2,1,0:T(8,128)(2,1)S(1)} %get-tuple-element.85), channel_id=1, source_target_pairs={{0,18},{2,16},{4,22},{6,20},{8,26},{10,24},{12,30},{14,28},{16,2},... | collective-permute-start | bytes 98312 | tf_op jit(solution)/shard_map/ppermute | solution.py:272
  69.1 0.7 shard_map.78
  69.8 0.5 shard_map.79
  70.3 0.1 collective-permute-start.23
  70.4 3.9 %collective-permute-start.25 = (bf16[4,8,16,128]{3,2,1,0:T(8,128)(2,1)S(1)}, bf16[4,8,16,128]{3,2,1,0:T(8,128)(2,1)S(1)}, u32[]{:S(2)}, u32[]{:S(2)}) collective-permute-start(bf16[4,8,16,128]{3,2,1,0:T(8,128)(2,1)S(1)} %get-tuple-element.80), channel_id=1, source_target_pairs={{0,14},{2,12},{4,10},{6,8},{8,6},{10,4},{12,2},{14,0},{16,30},{18,... | collective-permute-start | bytes 393224 | tf_op jit(solution)/shard_map/ppermute | solution.py:272
  74.4 2.0 %collective-permute-start.28 = (bf16[3,8,16,128]{3,2,1,0:T(8,128)(2,1)S(1)}, bf16[3,8,16,128]{3,2,1,0:T(8,128)(2,1)S(1)}, u32[]{:S(2)}, u32[]{:S(2)}) collective-permute-start(bf16[3,8,16,128]{3,2,1,0:T(8,128)(2,1)S(1)} %get-tuple-element.84), channel_id=1, source_target_pairs={{0,16},{2,18},{4,20},{6,22},{8,24},{10,26},{12,28},{14,30},{16,0},... | collective-permute-start | bytes 294920 | tf_op jit(solution)/shard_map/ppermute | solution.py:272
  76.4 0.8 collective-permute-start.30
  77.2 4.1 %collective-permute-done.28.refs_2_ = bf16[3,8,16,128]{3,2,1,0:T(8,128)(2,1)S(1)} collective-permute-done((bf16[3,8,16,128]{3,2,1,0:T(8,128)(2,1)S(1)}, bf16[3,8,16,128]{3,2,1,0:T(8,128)(2,1)S(1)}, u32[]{:S(2)}, u32[]{:S(2)}) %collective-permute-start.28) | collective-permute-done | bytes 98336 | tf_op jit(solution)/shard_map/ppermute | solution.py:272
  81.3 4.9 %collective-permute-start.34 = (bf16[4,8,16,128]{3,2,1,0:T(8,128)(2,1)S(1)}, bf16[4,8,16,128]{3,2,1,0:T(8,128)(2,1)S(1)}, u32[]{:S(2)}, u32[]{:S(2)}) collective-permute-start(bf16[4,8,16,128]{3,2,1,0:T(8,128)(2,1)S(1)} %get-tuple-element.90), channel_id=1, source_target_pairs={{0,10},{2,8},{4,14},{6,12},{8,2},{10,0},{12,6},{14,4},{16,26},{18,... | collective-permute-start | bytes 393224 | tf_op jit(solution)/shard_map/ppermute | solution.py:272
  86.1 1.5 %collective-permute-start.22 = (bf16[4,8,16,128]{3,2,1,0:T(8,128)(2,1)S(1)}, bf16[4,8,16,128]{3,2,1,0:T(8,128)(2,1)S(1)}, u32[]{:S(2)}, u32[]{:S(2)}) collective-permute-start(bf16[4,8,16,128]{3,2,1,0:T(8,128)(2,1)S(1)} %get-tuple-element.77), channel_id=1, source_target_pairs={{0,24},{2,26},{4,28},{6,30},{8,16},{10,18},{12,20},{14,22},{16,8},... | collective-permute-start | bytes 393224 | tf_op jit(solution)/shard_map/ppermute | solution.py:272
  87.7 3.0 %collective-permute-start.24 = (bf16[4,8,16,128]{3,2,1,0:T(8,128)(2,1)S(1)}, bf16[4,8,16,128]{3,2,1,0:T(8,128)(2,1)S(1)}, u32[]{:S(2)}, u32[]{:S(2)}) collective-permute-start(bf16[4,8,16,128]{3,2,1,0:T(8,128)(2,1)S(1)} %get-tuple-element.79), channel_id=1, source_target_pairs={{0,26},{2,24},{4,30},{6,28},{8,18},{10,16},{12,22},{14,20},{16,10}... | collective-permute-start | bytes 393224 | tf_op jit(solution)/shard_map/ppermute | solution.py:272
  90.7 4.0 %collective-permute-start.33 = (bf16[4,8,16,128]{3,2,1,0:T(8,128)(2,1)S(1)}, bf16[4,8,16,128]{3,2,1,0:T(8,128)(2,1)S(1)}, u32[]{:S(2)}, u32[]{:S(2)}) collective-permute-start(bf16[4,8,16,128]{3,2,1,0:T(8,128)(2,1)S(1)} %get-tuple-element.89), channel_id=1, source_target_pairs={{0,22},{2,20},{4,18},{6,16},{8,30},{10,28},{12,26},{14,24},{16,6},... | collective-permute-start | bytes 393224 | tf_op jit(solution)/shard_map/ppermute | solution.py:272
  94.7 1.3 %collective-permute-start.18 = (bf16[4,8,16,128]{3,2,1,0:T(8,128)(2,1)S(1)}, bf16[4,8,16,128]{3,2,1,0:T(8,128)(2,1)S(1)}, u32[]{:S(2)}, u32[]{:S(2)}) collective-permute-start(bf16[4,8,16,128]{3,2,1,0:T(8,128)(2,1)S(1)} %get-tuple-element.73), channel_id=1, source_target_pairs={{0,2},{2,0},{4,6},{6,4},{8,10},{10,8},{12,14},{14,12},{16,18},{18,... | collective-permute-start | bytes 393224 | tf_op jit(solution)/shard_map/ppermute | solution.py:272
  96.0 0.4 collective-permute-start.20
  96.4 1.4 %collective-permute-done.24.refs_2_ = bf16[4,8,16,128]{3,2,1,0:T(8,128)(2,1)S(1)} collective-permute-done((bf16[4,8,16,128]{3,2,1,0:T(8,128)(2,1)S(1)}, bf16[4,8,16,128]{3,2,1,0:T(8,128)(2,1)S(1)}, u32[]{:S(2)}, u32[]{:S(2)}) %collective-permute-start.24) | collective-permute-done | bytes 131104 | tf_op jit(solution)/shard_map/ppermute | solution.py:272
  97.8 2.4 %collective-permute-start.26 = (bf16[4,8,16,128]{3,2,1,0:T(8,128)(2,1)S(1)}, bf16[4,8,16,128]{3,2,1,0:T(8,128)(2,1)S(1)}, u32[]{:S(2)}, u32[]{:S(2)}) collective-permute-start(bf16[4,8,16,128]{3,2,1,0:T(8,128)(2,1)S(1)} %get-tuple-element.81), channel_id=1, source_target_pairs={{0,28},{2,30},{4,24},{6,26},{8,20},{10,22},{12,16},{14,18},{16,12}... | collective-permute-start | bytes 393224 | tf_op jit(solution)/shard_map/ppermute | solution.py:272
  100.3 10.7 %collective-permute-done.31.refs_5_ = bf16[4,8,16,128]{3,2,1,0:T(8,128)(2,1)S(1)} collective-permute-done((bf16[4,8,16,128]{3,2,1,0:T(8,128)(2,1)S(1)}, bf16[4,8,16,128]{3,2,1,0:T(8,128)(2,1)S(1)}, u32[]{:S(2)}, u32[]{:S(2)}) %collective-permute-start.31) | collective-permute-done | bytes 131104 | tf_op jit(solution)/shard_map/ppermute | solution.py:272
  111.0 2.1 %collective-permute-start.21 = (bf16[4,8,16,128]{3,2,1,0:T(8,128)(2,1)S(1)}, bf16[4,8,16,128]{3,2,1,0:T(8,128)(2,1)S(1)}, u32[]{:S(2)}, u32[]{:S(2)}) collective-permute-start(bf16[4,8,16,128]{3,2,1,0:T(8,128)(2,1)S(1)} %get-tuple-element.76), channel_id=1, source_target_pairs={{0,6},{2,4},{4,2},{6,0},{8,14},{10,12},{12,10},{14,8},{16,22},{18,... | collective-permute-start | bytes 393224 | tf_op jit(solution)/shard_map/ppermute | solution.py:272
  113.2 1.4 %collective-permute-done.33.refs_7_ = bf16[4,8,16,128]{3,2,1,0:T(8,128)(2,1)S(1)} collective-permute-done((bf16[4,8,16,128]{3,2,1,0:T(8,128)(2,1)S(1)}, bf16[4,8,16,128]{3,2,1,0:T(8,128)(2,1)S(1)}, u32[]{:S(2)}, u32[]{:S(2)}) %collective-permute-start.33) | collective-permute-done | bytes 131104 | tf_op jit(solution)/shard_map/ppermute | solution.py:272
  114.6 2.9 %collective-permute-start.19 = (bf16[4,8,16,128]{3,2,1,0:T(8,128)(2,1)S(1)}, bf16[4,8,16,128]{3,2,1,0:T(8,128)(2,1)S(1)}, u32[]{:S(2)}, u32[]{:S(2)}) collective-permute-start(bf16[4,8,16,128]{3,2,1,0:T(8,128)(2,1)S(1)} %get-tuple-element.74), channel_id=1, source_target_pairs={{0,30},{2,28},{4,26},{6,24},{8,22},{10,20},{12,18},{14,16},{16,14}... | collective-permute-start | bytes 393224 | tf_op jit(solution)/shard_map/ppermute | solution.py:272
  117.5 1.2 shard_map.80.refs_5_
  118.7 1.0 shard_map.81.refs_4_
  119.7 3.4 %collective-permute-done.19.refs_1_ = bf16[4,8,16,128]{3,2,1,0:T(8,128)(2,1)S(1)} collective-permute-done((bf16[4,8,16,128]{3,2,1,0:T(8,128)(2,1)S(1)}, bf16[4,8,16,128]{3,2,1,0:T(8,128)(2,1)S(1)}, u32[]{:S(2)}, u32[]{:S(2)}) %collective-permute-start.19) | collective-permute-done | bytes 131104 | tf_op jit(solution)/shard_map/ppermute | solution.py:272
  123.1 0.9 shard_map.82
  (37 shorter events, 0.1 us)
Async XLA Ops:
  0.0 1.6 %copy-start = (bf16[16,1,64,8,128]{4,3,2,1,0:T(8,128)(2,1)S(1)}, bf16[16,1,64,8,128]{4,3,2,1,0:T(8,128)(2,1)}, u32[]{:S(2)}) copy-start(bf16[16,1,64,8,128]{4,3,2,1,0:T(8,128)(2,1)} %param.7) | copy-start | bytes 6291460
  1.6 7.6 %copy-start.4 = (bf16[1,4,128]{2,1,0:T(4,128)(2,1)S(1)}, bf16[1,4,128]{2,1,0:T(4,128)(2,1)}, u32[]{:S(2)}) copy-start(bf16[1,4,128]{2,1,0:T(4,128)(2,1)} %param.9) | copy-start | bytes 3076
  1.6 7.7 %copy-start.5 = (bf16[1,4,128]{2,1,0:T(4,128)(2,1)S(1)}, bf16[1,4,128]{2,1,0:T(4,128)(2,1)}, u32[]{:S(2)}) copy-start(bf16[1,4,128]{2,1,0:T(4,128)(2,1)} %param.10) | copy-start | bytes 3076
  1.6 7.7 %copy-start.6 = (s32[1,4]{1,0:T(1,128)S(1)}, s32[1,4]{1,0:T(1,128)}, u32[]{:S(2)}) copy-start(s32[1,4]{1,0:T(1,128)} %param.11) | copy-start | bytes 52
  1.6 7.8 %copy-start.3 = (s32[1,4,128]{2,1,0:T(4,128)S(1)}, s32[1,4,128]{2,1,0:T(4,128)}, u32[]{:S(2)}) copy-start(s32[1,4,128]{2,1,0:T(4,128)} %param.12) | copy-start | bytes 6148
  1.6 17.6 %copy-start.1 = (bf16[1,4,256,128]{3,2,1,0:T(8,128)(2,1)S(1)}, bf16[1,4,256,128]{3,2,1,0:T(8,128)(2,1)}, u32[]{:S(2)}) copy-start(bf16[1,4,256,128]{3,2,1,0:T(8,128)(2,1)} %param.8) | copy-start | bytes 786436
  1.7 53.3 %copy-start.2 = (s32[1,4,4]{2,1,0:T(4,128)S(1)}, s32[1,4,4]{2,1,0:T(4,128)}, u32[]{:S(2)}) copy-start(s32[1,4,4]{2,1,0:T(4,128)} %param.13) | copy-start | bytes 196
  1.7 14.1 %collective-permute-start.9 = (bf16[16,4,8,128]{3,2,1,0:T(8,128)(2,1)S(1)}, bf16[16,4,8,128]{3,2,1,0:T(8,128)(2,1)S(1)}, u32[]{:S(2)}, u32[]{:S(2)}) collective-permute-start(bf16[16,4,8,128]{3,2,1,0:T(8,128)(2,1)S(1)} %get-tuple-element.58), channel_id=1, source_target_pairs={{0,16},{2,18},{4,20},{6,22},{8,24},{10,26},{12,28},{14,30},{16,0},... | collective-permute-start | bytes 393224 | tf_op jit(solution)/shard_map/ppermute | solution.py:272
  5.8 13.0 %collective-permute-start.10 = (bf16[16,4,8,128]{3,2,1,0:T(8,128)(2,1)S(1)}, bf16[16,4,8,128]{3,2,1,0:T(8,128)(2,1)S(1)}, u32[]{:S(2)}, u32[]{:S(2)}) collective-permute-start(bf16[16,4,8,128]{3,2,1,0:T(8,128)(2,1)S(1)} %get-tuple-element.59), channel_id=1, source_target_pairs={{0,18},{2,16},{4,22},{6,20},{8,26},{10,24},{12,30},{14,28},{16,2},... | collective-permute-start | bytes 393224 | tf_op jit(solution)/shard_map/ppermute | solution.py:272
  7.6 11.6 %collective-permute-start.2 = (bf16[16,4,8,128]{3,2,1,0:T(8,128)(2,1)S(1)}, bf16[16,4,8,128]{3,2,1,0:T(8,128)(2,1)S(1)}, u32[]{:S(2)}, u32[]{:S(2)}) collective-permute-start(bf16[16,4,8,128]{3,2,1,0:T(8,128)(2,1)S(1)} %get-tuple-element.51), channel_id=1, source_target_pairs={{0,8},{2,10},{4,12},{6,14},{8,0},{10,2},{12,4},{14,6},{16,24},{18,... | collective-permute-start | bytes 393224 | tf_op jit(solution)/shard_map/ppermute | solution.py:272
  9.5 1.2 collective-permute-start.1
  9.5 11.5 %collective-permute-start.3 = (bf16[16,4,8,128]{3,2,1,0:T(8,128)(2,1)S(1)}, bf16[16,4,8,128]{3,2,1,0:T(8,128)(2,1)S(1)}, u32[]{:S(2)}, u32[]{:S(2)}) collective-permute-start(bf16[16,4,8,128]{3,2,1,0:T(8,128)(2,1)S(1)} %get-tuple-element.52), channel_id=1, source_target_pairs={{0,10},{2,8},{4,14},{6,12},{8,2},{10,0},{12,6},{14,4},{16,26},{18,... | collective-permute-start | bytes 393224 | tf_op jit(solution)/shard_map/ppermute | solution.py:272
  10.7 13.0 %collective-permute-start.4 = (bf16[16,4,8,128]{3,2,1,0:T(8,128)(2,1)S(1)}, bf16[16,4,8,128]{3,2,1,0:T(8,128)(2,1)S(1)}, u32[]{:S(2)}, u32[]{:S(2)}) collective-permute-start(bf16[16,4,8,128]{3,2,1,0:T(8,128)(2,1)S(1)} %get-tuple-element.53), channel_id=1, source_target_pairs={{0,12},{2,14},{4,8},{6,10},{8,4},{10,6},{12,0},{14,2},{16,28},{18,... | collective-permute-start | bytes 393224 | tf_op jit(solution)/shard_map/ppermute | solution.py:272
  15.8 11.7 %collective-permute-start.5 = (bf16[16,4,8,128]{3,2,1,0:T(8,128)(2,1)S(1)}, bf16[16,4,8,128]{3,2,1,0:T(8,128)(2,1)S(1)}, u32[]{:S(2)}, u32[]{:S(2)}) collective-permute-start(bf16[16,4,8,128]{3,2,1,0:T(8,128)(2,1)S(1)} %get-tuple-element.54), channel_id=1, source_target_pairs={{0,14},{2,12},{4,10},{6,8},{8,6},{10,4},{12,2},{14,0},{16,30},{18,... | collective-permute-start | bytes 393224 | tf_op jit(solution)/shard_map/ppermute | solution.py:272
  18.8 10.4 %collective-permute-start.6 = (bf16[16,4,8,128]{3,2,1,0:T(8,128)(2,1)S(1)}, bf16[16,4,8,128]{3,2,1,0:T(8,128)(2,1)S(1)}, u32[]{:S(2)}, u32[]{:S(2)}) collective-permute-start(bf16[16,4,8,128]{3,2,1,0:T(8,128)(2,1)S(1)} %get-tuple-element.55), channel_id=1, source_target_pairs={{0,2},{2,0},{4,6},{6,4},{8,10},{10,8},{12,14},{14,12},{16,18},{18,... | collective-permute-start | bytes 393224 | tf_op jit(solution)/shard_map/ppermute | solution.py:272
  19.2 29.1 %collective-permute-start = (bf16[4,256,128]{2,1,0:T(8,128)(2,1)S(1)}, bf16[4,256,128]{2,1,0:T(8,128)(2,1)S(1)}, u32[]{:S(2)}, u32[]{:S(2)}) collective-permute-start(bf16[4,256,128]{2,1,0:T(8,128)(2,1)S(1)} %bitcast.15), channel_id=1, source_target_pairs={{0,1},{1,0},{2,3},{3,2},{4,5},{5,4},{6,7},{7,6},{8,9},{9,8},{10,11... | collective-permute-start | bytes 786440 | tf_op jit(solution)/shard_map/ppermute | solution.py:221
  21.0 11.2 %collective-permute-start.7 = (bf16[16,4,8,128]{3,2,1,0:T(8,128)(2,1)S(1)}, bf16[16,4,8,128]{3,2,1,0:T(8,128)(2,1)S(1)}, u32[]{:S(2)}, u32[]{:S(2)}) collective-permute-start(bf16[16,4,8,128]{3,2,1,0:T(8,128)(2,1)S(1)} %get-tuple-element.56), channel_id=1, source_target_pairs={{0,4},{2,6},{4,0},{6,2},{8,12},{10,14},{12,8},{14,10},{16,20},{18,... | collective-permute-start | bytes 393224 | tf_op jit(solution)/shard_map/ppermute | solution.py:272
  23.7 13.0 %collective-permute-start.8 = (bf16[16,4,8,128]{3,2,1,0:T(8,128)(2,1)S(1)}, bf16[16,4,8,128]{3,2,1,0:T(8,128)(2,1)S(1)}, u32[]{:S(2)}, u32[]{:S(2)}) collective-permute-start(bf16[16,4,8,128]{3,2,1,0:T(8,128)(2,1)S(1)} %get-tuple-element.57), channel_id=1, source_target_pairs={{0,6},{2,4},{4,2},{6,0},{8,14},{10,12},{12,10},{14,8},{16,22},{18,... | collective-permute-start | bytes 393224 | tf_op jit(solution)/shard_map/ppermute | solution.py:272
  27.5 13.7 %collective-permute-start.11 = (bf16[16,4,8,128]{3,2,1,0:T(8,128)(2,1)S(1)}, bf16[16,4,8,128]{3,2,1,0:T(8,128)(2,1)S(1)}, u32[]{:S(2)}, u32[]{:S(2)}) collective-permute-start(bf16[16,4,8,128]{3,2,1,0:T(8,128)(2,1)S(1)} %get-tuple-element.60), channel_id=1, source_target_pairs={{0,20},{2,22},{4,16},{6,18},{8,28},{10,30},{12,24},{14,26},{16,4},... | collective-permute-start | bytes 393224 | tf_op jit(solution)/shard_map/ppermute | solution.py:272
  29.2 17.9 %collective-permute-start.12 = (bf16[16,4,8,128]{3,2,1,0:T(8,128)(2,1)S(1)}, bf16[16,4,8,128]{3,2,1,0:T(8,128)(2,1)S(1)}, u32[]{:S(2)}, u32[]{:S(2)}) collective-permute-start(bf16[16,4,8,128]{3,2,1,0:T(8,128)(2,1)S(1)} %get-tuple-element.61), channel_id=1, source_target_pairs={{0,22},{2,20},{4,18},{6,16},{8,30},{10,28},{12,26},{14,24},{16,6},... | collective-permute-start | bytes 393224 | tf_op jit(solution)/shard_map/ppermute | solution.py:272
  32.2 33.8 %collective-permute-start.16 = (bf16[16,1,8,128]{3,2,1,0:T(8,128)(2,1)S(1)}, bf16[16,1,8,128]{3,2,1,0:T(8,128)(2,1)S(1)}, u32[]{:S(2)}, u32[]{:S(2)}) collective-permute-start(bf16[16,1,8,128]{3,2,1,0:T(8,128)(2,1)S(1)} %get-tuple-element.67), channel_id=1, source_target_pairs={{0,30},{2,28},{4,26},{6,24},{8,22},{10,20},{12,18},{14,16},{16,14}... | collective-permute-start | bytes 98312 | tf_op jit(solution)/shard_map/ppermute | solution.py:272
  36.8 32.4 %collective-permute-start.17 = (bf16[16,3,8,128]{3,2,1,0:T(8,128)(2,1)S(1)}, bf16[16,3,8,128]{3,2,1,0:T(8,128)(2,1)S(1)}, u32[]{:S(2)}, u32[]{:S(2)}) collective-permute-start(bf16[16,3,8,128]{3,2,1,0:T(8,128)(2,1)S(1)} %get-tuple-element.70), channel_id=1, source_target_pairs={{0,30},{2,28},{4,26},{6,24},{8,22},{10,20},{12,18},{14,16},{16,14}... | collective-permute-start | bytes 294920 | tf_op jit(solution)/shard_map/ppermute | solution.py:272
  41.2 24.8 %collective-permute-start.13 = (bf16[16,4,8,128]{3,2,1,0:T(8,128)(2,1)S(1)}, bf16[16,4,8,128]{3,2,1,0:T(8,128)(2,1)S(1)}, u32[]{:S(2)}, u32[]{:S(2)}) collective-permute-start(bf16[16,4,8,128]{3,2,1,0:T(8,128)(2,1)S(1)} %get-tuple-element.64), channel_id=1, source_target_pairs={{0,24},{2,26},{4,28},{6,30},{8,16},{10,18},{12,20},{14,22},{16,8},... | collective-permute-start | bytes 393224 | tf_op jit(solution)/shard_map/ppermute | solution.py:272
  47.1 18.9 %collective-permute-start.14 = (bf16[16,4,8,128]{3,2,1,0:T(8,128)(2,1)S(1)}, bf16[16,4,8,128]{3,2,1,0:T(8,128)(2,1)S(1)}, u32[]{:S(2)}, u32[]{:S(2)}) collective-permute-start(bf16[16,4,8,128]{3,2,1,0:T(8,128)(2,1)S(1)} %get-tuple-element.65), channel_id=1, source_target_pairs={{0,26},{2,24},{4,30},{6,28},{8,18},{10,16},{12,22},{14,20},{16,10}... | collective-permute-start | bytes 393224 | tf_op jit(solution)/shard_map/ppermute | solution.py:272
  48.3 17.8 %collective-permute-start.15 = (bf16[16,4,8,128]{3,2,1,0:T(8,128)(2,1)S(1)}, bf16[16,4,8,128]{3,2,1,0:T(8,128)(2,1)S(1)}, u32[]{:S(2)}, u32[]{:S(2)}) collective-permute-start(bf16[16,4,8,128]{3,2,1,0:T(8,128)(2,1)S(1)} %get-tuple-element.66), channel_id=1, source_target_pairs={{0,28},{2,30},{4,24},{6,26},{8,20},{10,22},{12,16},{14,18},{16,12}... | collective-permute-start | bytes 393224 | tf_op jit(solution)/shard_map/ppermute | solution.py:272
  66.3 8.1 %collective-permute-start.27 = (bf16[1,8,16,128]{3,2,1,0:T(8,128)(2,1)S(1)}, bf16[1,8,16,128]{3,2,1,0:T(8,128)(2,1)S(1)}, u32[]{:S(2)}, u32[]{:S(2)}) collective-permute-start(bf16[1,8,16,128]{3,2,1,0:T(8,128)(2,1)S(1)} %get-tuple-element.83), channel_id=1, source_target_pairs={{0,16},{2,18},{4,20},{6,22},{8,24},{10,26},{12,28},{14,30},{16,0},... | collective-permute-start | bytes 98312 | tf_op jit(solution)/shard_map/ppermute | solution.py:272
  66.4 10.0 %collective-permute-start.29 = (bf16[1,8,16,128]{3,2,1,0:T(8,128)(2,1)S(1)}, bf16[1,8,16,128]{3,2,1,0:T(8,128)(2,1)S(1)}, u32[]{:S(2)}, u32[]{:S(2)}) collective-permute-start(bf16[1,8,16,128]{3,2,1,0:T(8,128)(2,1)S(1)} %get-tuple-element.85), channel_id=1, source_target_pairs={{0,18},{2,16},{4,22},{6,20},{8,26},{10,24},{12,30},{14,28},{16,2},... | collective-permute-start | bytes 98312 | tf_op jit(solution)/shard_map/ppermute | solution.py:272
  70.3 17.3 %collective-permute-start.23 = (bf16[4,8,16,128]{3,2,1,0:T(8,128)(2,1)S(1)}, bf16[4,8,16,128]{3,2,1,0:T(8,128)(2,1)S(1)}, u32[]{:S(2)}, u32[]{:S(2)}) collective-permute-start(bf16[4,8,16,128]{3,2,1,0:T(8,128)(2,1)S(1)} %get-tuple-element.78), channel_id=1, source_target_pairs={{0,12},{2,14},{4,8},{6,10},{8,4},{10,6},{12,0},{14,2},{16,28},{18,... | collective-permute-start | bytes 393224 | tf_op jit(solution)/shard_map/ppermute | solution.py:272
  70.4 20.3 %collective-permute-start.25 = (bf16[4,8,16,128]{3,2,1,0:T(8,128)(2,1)S(1)}, bf16[4,8,16,128]{3,2,1,0:T(8,128)(2,1)S(1)}, u32[]{:S(2)}, u32[]{:S(2)}) collective-permute-start(bf16[4,8,16,128]{3,2,1,0:T(8,128)(2,1)S(1)} %get-tuple-element.80), channel_id=1, source_target_pairs={{0,14},{2,12},{4,10},{6,8},{8,6},{10,4},{12,2},{14,0},{16,30},{18,... | collective-permute-start | bytes 393224 | tf_op jit(solution)/shard_map/ppermute | solution.py:272
  74.4 16.3 %collective-permute-start.32 = (bf16[4,8,16,128]{3,2,1,0:T(8,128)(2,1)S(1)}, bf16[4,8,16,128]{3,2,1,0:T(8,128)(2,1)S(1)}, u32[]{:S(2)}, u32[]{:S(2)}) collective-permute-start(bf16[4,8,16,128]{3,2,1,0:T(8,128)(2,1)S(1)} %get-tuple-element.88), channel_id=1, source_target_pairs={{0,8},{2,10},{4,12},{6,14},{8,0},{10,2},{12,4},{14,6},{16,24},{18,... | collective-permute-start | bytes 393224 | tf_op jit(solution)/shard_map/ppermute | solution.py:272
  74.4 6.9 %collective-permute-start.28 = (bf16[3,8,16,128]{3,2,1,0:T(8,128)(2,1)S(1)}, bf16[3,8,16,128]{3,2,1,0:T(8,128)(2,1)S(1)}, u32[]{:S(2)}, u32[]{:S(2)}) collective-permute-start(bf16[3,8,16,128]{3,2,1,0:T(8,128)(2,1)S(1)} %get-tuple-element.84), channel_id=1, source_target_pairs={{0,16},{2,18},{4,20},{6,22},{8,24},{10,26},{12,28},{14,30},{16,0},... | collective-permute-start | bytes 294920 | tf_op jit(solution)/shard_map/ppermute | solution.py:272
  76.4 9.8 %collective-permute-start.30 = (bf16[3,8,16,128]{3,2,1,0:T(8,128)(2,1)S(1)}, bf16[3,8,16,128]{3,2,1,0:T(8,128)(2,1)S(1)}, u32[]{:S(2)}, u32[]{:S(2)}) collective-permute-start(bf16[3,8,16,128]{3,2,1,0:T(8,128)(2,1)S(1)} %get-tuple-element.86), channel_id=1, source_target_pairs={{0,18},{2,16},{4,22},{6,20},{8,26},{10,24},{12,30},{14,28},{16,2},... | collective-permute-start | bytes 294920 | tf_op jit(solution)/shard_map/ppermute | solution.py:272
  81.3 13.4 %collective-permute-start.34 = (bf16[4,8,16,128]{3,2,1,0:T(8,128)(2,1)S(1)}, bf16[4,8,16,128]{3,2,1,0:T(8,128)(2,1)S(1)}, u32[]{:S(2)}, u32[]{:S(2)}) collective-permute-start(bf16[4,8,16,128]{3,2,1,0:T(8,128)(2,1)S(1)} %get-tuple-element.90), channel_id=1, source_target_pairs={{0,10},{2,8},{4,14},{6,12},{8,2},{10,0},{12,6},{14,4},{16,26},{18,... | collective-permute-start | bytes 393224 | tf_op jit(solution)/shard_map/ppermute | solution.py:272
  86.1 9.8 %collective-permute-start.22 = (bf16[4,8,16,128]{3,2,1,0:T(8,128)(2,1)S(1)}, bf16[4,8,16,128]{3,2,1,0:T(8,128)(2,1)S(1)}, u32[]{:S(2)}, u32[]{:S(2)}) collective-permute-start(bf16[4,8,16,128]{3,2,1,0:T(8,128)(2,1)S(1)} %get-tuple-element.77), channel_id=1, source_target_pairs={{0,24},{2,26},{4,28},{6,30},{8,16},{10,18},{12,20},{14,22},{16,8},... | collective-permute-start | bytes 393224 | tf_op jit(solution)/shard_map/ppermute | solution.py:272
  87.7 10.2 %collective-permute-start.24 = (bf16[4,8,16,128]{3,2,1,0:T(8,128)(2,1)S(1)}, bf16[4,8,16,128]{3,2,1,0:T(8,128)(2,1)S(1)}, u32[]{:S(2)}, u32[]{:S(2)}) collective-permute-start(bf16[4,8,16,128]{3,2,1,0:T(8,128)(2,1)S(1)} %get-tuple-element.79), channel_id=1, source_target_pairs={{0,26},{2,24},{4,30},{6,28},{8,18},{10,16},{12,22},{14,20},{16,10}... | collective-permute-start | bytes 393224 | tf_op jit(solution)/shard_map/ppermute | solution.py:272
  90.7 20.3 %collective-permute-start.31 = (bf16[4,8,16,128]{3,2,1,0:T(8,128)(2,1)S(1)}, bf16[4,8,16,128]{3,2,1,0:T(8,128)(2,1)S(1)}, u32[]{:S(2)}, u32[]{:S(2)}) collective-permute-start(bf16[4,8,16,128]{3,2,1,0:T(8,128)(2,1)S(1)} %get-tuple-element.87), channel_id=1, source_target_pairs={{0,20},{2,22},{4,16},{6,18},{8,28},{10,30},{12,24},{14,26},{16,4},... | collective-permute-start | bytes 393224 | tf_op jit(solution)/shard_map/ppermute | solution.py:272
  90.7 23.9 %collective-permute-start.33 = (bf16[4,8,16,128]{3,2,1,0:T(8,128)(2,1)S(1)}, bf16[4,8,16,128]{3,2,1,0:T(8,128)(2,1)S(1)}, u32[]{:S(2)}, u32[]{:S(2)}) collective-permute-start(bf16[4,8,16,128]{3,2,1,0:T(8,128)(2,1)S(1)} %get-tuple-element.89), channel_id=1, source_target_pairs={{0,22},{2,20},{4,18},{6,16},{8,30},{10,28},{12,26},{14,24},{16,6},... | collective-permute-start | bytes 393224 | tf_op jit(solution)/shard_map/ppermute | solution.py:272
  94.7 25.0 %collective-permute-start.18 = (bf16[4,8,16,128]{3,2,1,0:T(8,128)(2,1)S(1)}, bf16[4,8,16,128]{3,2,1,0:T(8,128)(2,1)S(1)}, u32[]{:S(2)}, u32[]{:S(2)}) collective-permute-start(bf16[4,8,16,128]{3,2,1,0:T(8,128)(2,1)S(1)} %get-tuple-element.73), channel_id=1, source_target_pairs={{0,2},{2,0},{4,6},{6,4},{8,10},{10,8},{12,14},{14,12},{16,18},{18,... | collective-permute-start | bytes 393224 | tf_op jit(solution)/shard_map/ppermute | solution.py:272
  96.0 23.7 %collective-permute-start.20 = (bf16[4,8,16,128]{3,2,1,0:T(8,128)(2,1)S(1)}, bf16[4,8,16,128]{3,2,1,0:T(8,128)(2,1)S(1)}, u32[]{:S(2)}, u32[]{:S(2)}) collective-permute-start(bf16[4,8,16,128]{3,2,1,0:T(8,128)(2,1)S(1)} %get-tuple-element.75), channel_id=1, source_target_pairs={{0,4},{2,6},{4,0},{6,2},{8,12},{10,14},{12,8},{14,10},{16,20},{18,... | collective-permute-start | bytes 393224 | tf_op jit(solution)/shard_map/ppermute | solution.py:272
  97.8 20.8 %collective-permute-start.26 = (bf16[4,8,16,128]{3,2,1,0:T(8,128)(2,1)S(1)}, bf16[4,8,16,128]{3,2,1,0:T(8,128)(2,1)S(1)}, u32[]{:S(2)}, u32[]{:S(2)}) collective-permute-start(bf16[4,8,16,128]{3,2,1,0:T(8,128)(2,1)S(1)} %get-tuple-element.81), channel_id=1, source_target_pairs={{0,28},{2,30},{4,24},{6,26},{8,20},{10,22},{12,16},{14,18},{16,12}... | collective-permute-start | bytes 393224 | tf_op jit(solution)/shard_map/ppermute | solution.py:272
  111.0 8.7 %collective-permute-start.21 = (bf16[4,8,16,128]{3,2,1,0:T(8,128)(2,1)S(1)}, bf16[4,8,16,128]{3,2,1,0:T(8,128)(2,1)S(1)}, u32[]{:S(2)}, u32[]{:S(2)}) collective-permute-start(bf16[4,8,16,128]{3,2,1,0:T(8,128)(2,1)S(1)} %get-tuple-element.76), channel_id=1, source_target_pairs={{0,6},{2,4},{4,2},{6,0},{8,14},{10,12},{12,10},{14,8},{16,22},{18,... | collective-permute-start | bytes 393224 | tf_op jit(solution)/shard_map/ppermute | solution.py:272
  114.6 8.6 %collective-permute-start.19 = (bf16[4,8,16,128]{3,2,1,0:T(8,128)(2,1)S(1)}, bf16[4,8,16,128]{3,2,1,0:T(8,128)(2,1)S(1)}, u32[]{:S(2)}, u32[]{:S(2)}) collective-permute-start(bf16[4,8,16,128]{3,2,1,0:T(8,128)(2,1)S(1)} %get-tuple-element.74), channel_id=1, source_target_pairs={{0,30},{2,28},{4,26},{6,24},{8,22},{10,20},{12,18},{14,16},{16,14}... | collective-permute-start | bytes 393224 | tf_op jit(solution)/shard_map/ppermute | solution.py:272

commit v5 on v4

--- a/solution.py
+++ b/solution.py
@@ -277,13 +277,13 @@
         late = far[-LATE:]
         early = [0] + near_by + far[:-LATE]
         order = early + late
-        cut = 1 if tiles > 1 else 0
+        cut = tiles // 2
 
         def slices(blocks, *after):
             return call(
                 functools.partial(cut_kernel, blocks),
                 [
-                    jax.ShapeDtypeStruct((mine, stop - start, depth, points), jnp.bfloat16)
+                    pltpu.VMEM((mine, stop - start, depth, points), jnp.bfloat16)
                     for _, start, stop in blocks
                 ],
                 [smem, pl.BlockSpec(memory_space=pltpu.HBM)],
@@ -293,8 +293,8 @@
 
         last = far[-1]
         arrived = {}
-        parts = dict(zip(far[:LEAD], slices([(s, 0, tiles) for s in far[:LEAD]])))
-        others = far[LEAD:-1] + near_by + [0]
+        parts = {far[0]: lax.dynamic_index_in_dim(fields, me ^ far[0], 1, keepdims=False)}
+        others = far[1:-1] + near_by + [0]
         wanted = [(s, 0, tiles) for s in others]
         wanted += [(last, 0, cut)] * (cut > 0) + [(last, cut, tiles)]
         *found, tail = slices(wanted)

time: 124 us -> 123 us (level)
  starting transfers between devices: 65 us -> 62.5 us
    ppermute x33, starting transfers between devices: 65 us -> 62.5 us  [swap(): return lax.ppermute(x, 'wide', [(i, i ^ s) for i in range(wide)])]
  transfers between devices with their start and end apart: 35 -> 35, of which waited for: 14 -> 12; matrix products, arithmetic and copies ran while one was open for 0% -> 0% of each run, Pallas kernels for 13% -> 13%
where the time goes in v5:
time: 123 us
  starting transfers between devices  62.5 us (51%)
  waiting for transfers between devices  40.4 us (33%)
  Pallas kernels  16.7 us (14%)
  local copies, waits for them, and re-layouts  2.69 us (2%)
    ppermute x33, starting transfers between devices, swap(): return lax.ppermute(x, 'wide', [(i, i ^ s) for i in range(wide)])  62.5 us
    ppermute x33, waiting for transfers between devices, swap(): return lax.ppermute(x, 'wide', [(i, i ^ s) for i in range(wide)])  40.4 us
    pallas_call x1, Pallas kernels, on_device(): call(functools.partial(mix_kernel, order), [jax.ShapeDtypeStruct((tiles,...  11 us
    pallas_call x3, Pallas kernels, place(): call(functools.partial(place_kernel, [(s, start) for s, start, _ in group...  3.08 us
  transfers between devices with their start and end apart: 35, of which 12 were waited for; matrix products, arithmetic and copies ran while one was open for 0% of the time, Pallas kernels for 13%

profile of v5, /device:TPU:0, one launch (start us, length us, event | category | flops | bytes accessed | tf_op | source)
XLA Modules:
  0.0 122.6 jit_solution(7044668452816964911)
XLA Ops:
  0.0 1.0 dynamic-slice_bitcast_fusion
  1.0 4.1 %collective-permute-start.9 = (bf16[16,4,8,128]{3,2,1,0:T(8,128)(2,1)S(1)}, bf16[16,4,8,128]{3,2,1,0:T(8,128)(2,1)S(1)}, u32[]{:S(2)}, u32[]{:S(2)}) collective-permute-start(bf16[16,4,8,128]{3,2,1,0:T(8,128)(2,1)S(1)} %dynamic-slice_bitcast_fusion), channel_id=1, source_target_pairs={{0,16},{2,18},{4,20},{6,22},{8,24},{10,26},{12,28},{14,30},{16,0},... | collective-permute-start | bytes 393224 | tf_op jit(solution)/shard_map/ppermute | solution.py:272
  5.2 1.6 %copy-done = bf16[16,1,64,8,128]{4,3,2,1,0:T(8,128)(2,1)S(1)} copy-done((bf16[16,1,64,8,128]{4,3,2,1,0:T(8,128)(2,1)S(1)}, bf16[16,1,64,8,128]{4,3,2,1,0:T(8,128)(2,1)}, u32[]{:S(2)}) %copy-start) | copy-done | bytes 2097176
  6.8 0.5 shard_map.74
  7.3 1.6 %collective-permute-start.2 = (bf16[16,4,8,128]{3,2,1,0:T(8,128)(2,1)S(1)}, bf16[16,4,8,128]{3,2,1,0:T(8,128)(2,1)S(1)}, u32[]{:S(2)}, u32[]{:S(2)}) collective-permute-start(bf16[16,4,8,128]{3,2,1,0:T(8,128)(2,1)S(1)} %get-tuple-element.50), channel_id=1, source_target_pairs={{0,8},{2,10},{4,12},{6,14},{8,0},{10,2},{12,4},{14,6},{16,24},{18,... | collective-permute-start | bytes 393224 | tf_op jit(solution)/shard_map/ppermute | solution.py:272
  8.9 1.4 %collective-permute-start.3 = (bf16[16,4,8,128]{3,2,1,0:T(8,128)(2,1)S(1)}, bf16[16,4,8,128]{3,2,1,0:T(8,128)(2,1)S(1)}, u32[]{:S(2)}, u32[]{:S(2)}) collective-permute-start(bf16[16,4,8,128]{3,2,1,0:T(8,128)(2,1)S(1)} %get-tuple-element.51), channel_id=1, source_target_pairs={{0,10},{2,8},{4,14},{6,12},{8,2},{10,0},{12,6},{14,4},{16,26},{18,... | collective-permute-start | bytes 393224 | tf_op jit(solution)/shard_map/ppermute | solution.py:272
  10.3 0.1 pad.2.clone
  10.4 0.1 convert_multiply_fusion
  10.5 0.1 maximum_maximum_fusion.own_aux
  10.5 0.0 collective-permute-start.1
  10.6 2.6 %collective-permute-start.4 = (bf16[16,4,8,128]{3,2,1,0:T(8,128)(2,1)S(1)}, bf16[16,4,8,128]{3,2,1,0:T(8,128)(2,1)S(1)}, u32[]{:S(2)}, u32[]{:S(2)}) collective-permute-start(bf16[16,4,8,128]{3,2,1,0:T(8,128)(2,1)S(1)} %get-tuple-element.52), channel_id=1, source_target_pairs={{0,12},{2,14},{4,8},{6,10},{8,4},{10,6},{12,0},{14,2},{16,28},{18,... | collective-permute-start | bytes 393224 | tf_op jit(solution)/shard_map/ppermute | solution.py:272
  13.2 1.1 collective-permute-start.5
  14.2 0.0 collective-permute-done.9.refs_8_
  14.2 1.5 %collective-permute-start.6 = (bf16[16,4,8,128]{3,2,1,0:T(8,128)(2,1)S(1)}, bf16[16,4,8,128]{3,2,1,0:T(8,128)(2,1)S(1)}, u32[]{:S(2)}, u32[]{:S(2)}) collective-permute-start(bf16[16,4,8,128]{3,2,1,0:T(8,128)(2,1)S(1)} %get-tuple-element.54), channel_id=1, source_target_pairs={{0,2},{2,0},{4,6},{6,4},{8,10},{10,8},{12,14},{14,12},{16,18},{18,... | collective-permute-start | bytes 393224 | tf_op jit(solution)/shard_map/ppermute | solution.py:272
  15.7 0.0 collective-permute-done.2.refs_1_
  15.7 0.8 collective-permute-start.7
  16.6 1.6 %collective-permute-done.3.refs_2_ = bf16[16,4,8,128]{3,2,1,0:T(8,128)(2,1)S(1)} collective-permute-done((bf16[16,4,8,128]{3,2,1,0:T(8,128)(2,1)S(1)}, bf16[16,4,8,128]{3,2,1,0:T(8,128)(2,1)S(1)}, u32[]{:S(2)}, u32[]{:S(2)}) %collective-permute-start.3) | collective-permute-done | bytes 131104 | tf_op jit(solution)/shard_map/ppermute | solution.py:272
  18.2 2.9 %collective-permute-done.4.refs_3_ = bf16[16,4,8,128]{3,2,1,0:T(8,128)(2,1)S(1)} collective-permute-done((bf16[16,4,8,128]{3,2,1,0:T(8,128)(2,1)S(1)}, bf16[16,4,8,128]{3,2,1,0:T(8,128)(2,1)S(1)}, u32[]{:S(2)}, u32[]{:S(2)}) %collective-permute-start.4) | collective-permute-done | bytes 131104 | tf_op jit(solution)/shard_map/ppermute | solution.py:272
  21.1 1.6 %collective-permute-start.8 = (bf16[16,4,8,128]{3,2,1,0:T(8,128)(2,1)S(1)}, bf16[16,4,8,128]{3,2,1,0:T(8,128)(2,1)S(1)}, u32[]{:S(2)}, u32[]{:S(2)}) collective-permute-start(bf16[16,4,8,128]{3,2,1,0:T(8,128)(2,1)S(1)} %get-tuple-element.56), channel_id=1, source_target_pairs={{0,6},{2,4},{4,2},{6,0},{8,14},{10,12},{12,10},{14,8},{16,22},{18,... | collective-permute-start | bytes 393224 | tf_op jit(solution)/shard_map/ppermute | solution.py:272
  22.6 1.8 %collective-permute-done.5.refs_4_ = bf16[16,4,8,128]{3,2,1,0:T(8,128)(2,1)S(1)} collective-permute-done((bf16[16,4,8,128]{3,2,1,0:T(8,128)(2,1)S(1)}, bf16[16,4,8,128]{3,2,1,0:T(8,128)(2,1)S(1)}, u32[]{:S(2)}, u32[]{:S(2)}) %collective-permute-start.5) | collective-permute-done | bytes 131104 | tf_op jit(solution)/shard_map/ppermute | solution.py:272
  24.4 0.0 collective-permute-start.10
  24.4 0.0 collective-permute-done.6.refs_5_
  24.4 2.9 %collective-permute-start.11 = (bf16[16,4,8,128]{3,2,1,0:T(8,128)(2,1)S(1)}, bf16[16,4,8,128]{3,2,1,0:T(8,128)(2,1)S(1)}, u32[]{:S(2)}, u32[]{:S(2)}) collective-permute-start(bf16[16,4,8,128]{3,2,1,0:T(8,128)(2,1)S(1)} %get-tuple-element.58), channel_id=1, source_target_pairs={{0,20},{2,22},{4,16},{6,18},{8,28},{10,30},{12,24},{14,26},{16,4},... | collective-permute-start | bytes 393224 | tf_op jit(solution)/shard_map/ppermute | solution.py:272
  27.2 1.6 %collective-permute-done.7.refs_6_ = bf16[16,4,8,128]{3,2,1,0:T(8,128)(2,1)S(1)} collective-permute-done((bf16[16,4,8,128]{3,2,1,0:T(8,128)(2,1)S(1)}, bf16[16,4,8,128]{3,2,1,0:T(8,128)(2,1)S(1)}, u32[]{:S(2)}, u32[]{:S(2)}) %collective-permute-start.7) | collective-permute-done | bytes 131104 | tf_op jit(solution)/shard_map/ppermute | solution.py:272
  28.8 3.3 %collective-permute-start.16 = (bf16[16,2,8,128]{3,2,1,0:T(8,128)(2,1)S(1)}, bf16[16,2,8,128]{3,2,1,0:T(8,128)(2,1)S(1)}, u32[]{:S(2)}, u32[]{:S(2)}) collective-permute-start(bf16[16,2,8,128]{3,2,1,0:T(8,128)(2,1)S(1)} %get-tuple-element.65), channel_id=1, source_target_pairs={{0,30},{2,28},{4,26},{6,24},{8,22},{10,20},{12,18},{14,16},{16,14}... | collective-permute-start | bytes 196616 | tf_op jit(solution)/shard_map/ppermute | solution.py:272
  32.1 8.2 %collective-permute-done.10.refs_9_ = bf16[16,4,8,128]{3,2,1,0:T(8,128)(2,1)S(1)} collective-permute-done((bf16[16,4,8,128]{3,2,1,0:T(8,128)(2,1)S(1)}, bf16[16,4,8,128]{3,2,1,0:T(8,128)(2,1)S(1)}, u32[]{:S(2)}, u32[]{:S(2)}) %collective-permute-start.10) | collective-permute-done | bytes 131104 | tf_op jit(solution)/shard_map/ppermute | solution.py:272
  40.3 1.9 %collective-permute-start.17 = (bf16[16,2,8,128]{3,2,1,0:T(8,128)(2,1)S(1)}, bf16[16,2,8,128]{3,2,1,0:T(8,128)(2,1)S(1)}, u32[]{:S(2)}, u32[]{:S(2)}) collective-permute-start(bf16[16,2,8,128]{3,2,1,0:T(8,128)(2,1)S(1)} %get-tuple-element.68), channel_id=1, source_target_pairs={{0,30},{2,28},{4,26},{6,24},{8,22},{10,20},{12,18},{14,16},{16,14}... | collective-permute-start | bytes 196616 | tf_op jit(solution)/shard_map/ppermute | solution.py:272
  42.2 0.8 collective-permute-done.11.refs_10_
  43.0 1.6 %collective-permute-start.13 = (bf16[16,4,8,128]{3,2,1,0:T(8,128)(2,1)S(1)}, bf16[16,4,8,128]{3,2,1,0:T(8,128)(2,1)S(1)}, u32[]{:S(2)}, u32[]{:S(2)}) collective-permute-start(bf16[16,4,8,128]{3,2,1,0:T(8,128)(2,1)S(1)} %get-tuple-element.62), channel_id=1, source_target_pairs={{0,24},{2,26},{4,28},{6,30},{8,16},{10,18},{12,20},{14,22},{16,8},... | collective-permute-start | bytes 393224 | tf_op jit(solution)/shard_map/ppermute | solution.py:272
  44.6 2.2 %collective-permute-done.12.refs_11_ = bf16[16,4,8,128]{3,2,1,0:T(8,128)(2,1)S(1)} collective-permute-done((bf16[16,4,8,128]{3,2,1,0:T(8,128)(2,1)S(1)}, bf16[16,4,8,128]{3,2,1,0:T(8,128)(2,1)S(1)}, u32[]{:S(2)}, u32[]{:S(2)}) %collective-permute-start.12) | collective-permute-done | bytes 131104 | tf_op jit(solution)/shard_map/ppermute | solution.py:272
  46.8 1.1 collective-permute-start.14
  47.9 0.0 collective-permute-done.below.above
  47.9 3.6 %collective-permute-start.15 = (bf16[16,4,8,128]{3,2,1,0:T(8,128)(2,1)S(1)}, bf16[16,4,8,128]{3,2,1,0:T(8,128)(2,1)S(1)}, u32[]{:S(2)}, u32[]{:S(2)}) collective-permute-start(bf16[16,4,8,128]{3,2,1,0:T(8,128)(2,1)S(1)} %get-tuple-element.64), channel_id=1, source_target_pairs={{0,28},{2,30},{4,24},{6,26},{8,20},{10,22},{12,16},{14,18},{16,12}... | collective-permute-start | bytes 393224 | tf_op jit(solution)/shard_map/ppermute | solution.py:272
  51.5 0.7 shard_map.75
  52.2 11.0 %shard_map.73 = (bf16[4,256,256]{2,1,0:T(8,128)(2,1)S(1)}, f32[4,256,128]{2,1,0:T(8,128)S(1)}) custom-call(s32[4,4]{1,0:T(4,128)S(1)} %bitcast.19, s32[1]{0:T(128)} %bitcast.spot, bf16[4,256,128]{2,1,0:T(8,128)(2,1)S(1)} %bitcast.18, bf16[4,256,128]{2,1,0:T(8,128)(2,1)S(1)} %collective-permute-done.below.above, ...), custom_call_target="tpu_custom_call" | custom-call | tf_op jit(solution)/shard_map/pallas_call | solution.py:329
  63.2 0.0 collective-permute-done.16.refs_3_
  63.2 0.0 collective-permute-done.13.refs_0_
  63.2 0.3 shard_map.76
  63.6 3.8 %collective-permute-start.27 = (bf16[2,8,16,128]{3,2,1,0:T(8,128)(2,1)S(1)}, bf16[2,8,16,128]{3,2,1,0:T(8,128)(2,1)S(1)}, u32[]{:S(2)}, u32[]{:S(2)}) collective-permute-start(bf16[2,8,16,128]{3,2,1,0:T(8,128)(2,1)S(1)} %get-tuple-element.81), channel_id=1, source_target_pairs={{0,16},{2,18},{4,20},{6,22},{8,24},{10,26},{12,28},{14,30},{16,0},... | collective-permute-start | bytes 196616 | tf_op jit(solution)/shard_map/ppermute | solution.py:272
  67.4 2.1 %collective-permute-start.29 = (bf16[2,8,16,128]{3,2,1,0:T(8,128)(2,1)S(1)}, bf16[2,8,16,128]{3,2,1,0:T(8,128)(2,1)S(1)}, u32[]{:S(2)}, u32[]{:S(2)}) collective-permute-start(bf16[2,8,16,128]{3,2,1,0:T(8,128)(2,1)S(1)} %get-tuple-element.83), channel_id=1, source_target_pairs={{0,18},{2,16},{4,22},{6,20},{8,26},{10,24},{12,30},{14,28},{16,2},... | collective-permute-start | bytes 196616 | tf_op jit(solution)/shard_map/ppermute | solution.py:272
  69.4 0.6 shard_map.77
  70.1 0.5 shard_map.78
  70.5 1.6 %collective-permute-start.23 = (bf16[4,8,16,128]{3,2,1,0:T(8,128)(2,1)S(1)}, bf16[4,8,16,128]{3,2,1,0:T(8,128)(2,1)S(1)}, u32[]{:S(2)}, u32[]{:S(2)}) collective-permute-start(bf16[4,8,16,128]{3,2,1,0:T(8,128)(2,1)S(1)} %get-tuple-element.76), channel_id=1, source_target_pairs={{0,12},{2,14},{4,8},{6,10},{8,4},{10,6},{12,0},{14,2},{16,28},{18,... | collective-permute-start | bytes 393224 | tf_op jit(solution)/shard_map/ppermute | solution.py:272
  72.2 0.2 collective-permute-start.25
  72.4 2.7 %collective-permute-start.32 = (bf16[4,8,16,128]{3,2,1,0:T(8,128)(2,1)S(1)}, bf16[4,8,16,128]{3,2,1,0:T(8,128)(2,1)S(1)}, u32[]{:S(2)}, u32[]{:S(2)}) collective-permute-start(bf16[4,8,16,128]{3,2,1,0:T(8,128)(2,1)S(1)} %get-tuple-element.86), channel_id=1, source_target_pairs={{0,8},{2,10},{4,12},{6,14},{8,0},{10,2},{12,4},{14,6},{16,24},{18,... | collective-permute-start | bytes 393224 | tf_op jit(solution)/shard_map/ppermute | solution.py:272
  75.1 0.3 collective-permute-start.28
  75.4 2.6 %collective-permute-start.30 = (bf16[2,8,16,128]{3,2,1,0:T(8,128)(2,1)S(1)}, bf16[2,8,16,128]{3,2,1,0:T(8,128)(2,1)S(1)}, u32[]{:S(2)}, u32[]{:S(2)}) collective-permute-start(bf16[2,8,16,128]{3,2,1,0:T(8,128)(2,1)S(1)} %get-tuple-element.84), channel_id=1, source_target_pairs={{0,18},{2,16},{4,22},{6,20},{8,26},{10,24},{12,30},{14,28},{16,2},... | collective-permute-start | bytes 196616 | tf_op jit(solution)/shard_map/ppermute | solution.py:272
  78.0 3.8 %collective-permute-done.28.refs_2_ = bf16[2,8,16,128]{3,2,1,0:T(8,128)(2,1)S(1)} collective-permute-done((bf16[2,8,16,128]{3,2,1,0:T(8,128)(2,1)S(1)}, bf16[2,8,16,128]{3,2,1,0:T(8,128)(2,1)S(1)}, u32[]{:S(2)}, u32[]{:S(2)}) %collective-permute-start.28) | collective-permute-done | bytes 65568 | tf_op jit(solution)/shard_map/ppermute | solution.py:272
  81.8 4.1 %collective-permute-start.34 = (bf16[4,8,16,128]{3,2,1,0:T(8,128)(2,1)S(1)}, bf16[4,8,16,128]{3,2,1,0:T(8,128)(2,1)S(1)}, u32[]{:S(2)}, u32[]{:S(2)}) collective-permute-start(bf16[4,8,16,128]{3,2,1,0:T(8,128)(2,1)S(1)} %get-tuple-element.88), channel_id=1, source_target_pairs={{0,10},{2,8},{4,14},{6,12},{8,2},{10,0},{12,6},{14,4},{16,26},{18,... | collective-permute-start | bytes 393224 | tf_op jit(solution)/shard_map/ppermute | solution.py:272
  85.9 0.4 collective-permute-start.22
  86.3 3.3 %collective-permute-start.24 = (bf16[4,8,16,128]{3,2,1,0:T(8,128)(2,1)S(1)}, bf16[4,8,16,128]{3,2,1,0:T(8,128)(2,1)S(1)}, u32[]{:S(2)}, u32[]{:S(2)}) collective-permute-start(bf16[4,8,16,128]{3,2,1,0:T(8,128)(2,1)S(1)} %get-tuple-element.77), channel_id=1, source_target_pairs={{0,26},{2,24},{4,30},{6,28},{8,18},{10,16},{12,22},{14,20},{16,10}... | collective-permute-start | bytes 393224 | tf_op jit(solution)/shard_map/ppermute | solution.py:272
  89.6 4.9 %collective-permute-start.33 = (bf16[4,8,16,128]{3,2,1,0:T(8,128)(2,1)S(1)}, bf16[4,8,16,128]{3,2,1,0:T(8,128)(2,1)S(1)}, u32[]{:S(2)}, u32[]{:S(2)}) collective-permute-start(bf16[4,8,16,128]{3,2,1,0:T(8,128)(2,1)S(1)} %get-tuple-element.87), channel_id=1, source_target_pairs={{0,22},{2,20},{4,18},{6,16},{8,30},{10,28},{12,26},{14,24},{16,6},... | collective-permute-start | bytes 393224 | tf_op jit(solution)/shard_map/ppermute | solution.py:272
  94.4 0.4 collective-permute-start.18
  94.8 0.8 collective-permute-start.20
  95.6 1.7 %collective-permute-done.24.refs_2_ = bf16[4,8,16,128]{3,2,1,0:T(8,128)(2,1)S(1)} collective-permute-done((bf16[4,8,16,128]{3,2,1,0:T(8,128)(2,1)S(1)}, bf16[4,8,16,128]{3,2,1,0:T(8,128)(2,1)S(1)}, u32[]{:S(2)}, u32[]{:S(2)}) %collective-permute-start.24) | collective-permute-done | bytes 131104 | tf_op jit(solution)/shard_map/ppermute | solution.py:272
  97.3 1.5 %collective-permute-start.26 = (bf16[4,8,16,128]{3,2,1,0:T(8,128)(2,1)S(1)}, bf16[4,8,16,128]{3,2,1,0:T(8,128)(2,1)S(1)}, u32[]{:S(2)}, u32[]{:S(2)}) collective-permute-start(bf16[4,8,16,128]{3,2,1,0:T(8,128)(2,1)S(1)} %get-tuple-element.79), channel_id=1, source_target_pairs={{0,28},{2,30},{4,24},{6,26},{8,20},{10,22},{12,16},{14,18},{16,12}... | collective-permute-start | bytes 393224 | tf_op jit(solution)/shard_map/ppermute | solution.py:272
  98.8 11.9 %collective-permute-done.31.refs_5_ = bf16[4,8,16,128]{3,2,1,0:T(8,128)(2,1)S(1)} collective-permute-done((bf16[4,8,16,128]{3,2,1,0:T(8,128)(2,1)S(1)}, bf16[4,8,16,128]{3,2,1,0:T(8,128)(2,1)S(1)}, u32[]{:S(2)}, u32[]{:S(2)}) %collective-permute-start.31) | collective-permute-done | bytes 131104 | tf_op jit(solution)/shard_map/ppermute | solution.py:272
  110.7 1.3 %collective-permute-start.21 = (bf16[4,8,16,128]{3,2,1,0:T(8,128)(2,1)S(1)}, bf16[4,8,16,128]{3,2,1,0:T(8,128)(2,1)S(1)}, u32[]{:S(2)}, u32[]{:S(2)}) collective-permute-start(bf16[4,8,16,128]{3,2,1,0:T(8,128)(2,1)S(1)} %get-tuple-element.74), channel_id=1, source_target_pairs={{0,6},{2,4},{4,2},{6,0},{8,14},{10,12},{12,10},{14,8},{16,22},{18,... | collective-permute-start | bytes 393224 | tf_op jit(solution)/shard_map/ppermute | solution.py:272
  112.0 1.1 collective-permute-done.33.refs_7_
  113.1 3.5 %collective-permute-start.19 = (bf16[4,8,16,128]{3,2,1,0:T(8,128)(2,1)S(1)}, bf16[4,8,16,128]{3,2,1,0:T(8,128)(2,1)S(1)}, u32[]{:S(2)}, u32[]{:S(2)}) collective-permute-start(bf16[4,8,16,128]{3,2,1,0:T(8,128)(2,1)S(1)} %get-tuple-element.72), channel_id=1, source_target_pairs={{0,30},{2,28},{4,26},{6,24},{8,22},{10,20},{12,18},{14,16},{16,14}... | collective-permute-start | bytes 393224 | tf_op jit(solution)/shard_map/ppermute | solution.py:272
  116.6 1.2 shard_map.79.refs_5_
  117.8 1.0 shard_map.80.refs_4_
  118.8 2.8 %collective-permute-done.19.refs_1_ = bf16[4,8,16,128]{3,2,1,0:T(8,128)(2,1)S(1)} collective-permute-done((bf16[4,8,16,128]{3,2,1,0:T(8,128)(2,1)S(1)}, bf16[4,8,16,128]{3,2,1,0:T(8,128)(2,1)S(1)}, u32[]{:S(2)}, u32[]{:S(2)}) %collective-permute-start.19) | collective-permute-done | bytes 131104 | tf_op jit(solution)/shard_map/ppermute | solution.py:272
  121.7 0.9 shard_map.81
  (37 shorter events, 0.1 us)
Async XLA Ops:
  0.0 10.3 %copy-start.4 = (bf16[1,4,128]{2,1,0:T(4,128)(2,1)S(1)}, bf16[1,4,128]{2,1,0:T(4,128)(2,1)}, u32[]{:S(2)}) copy-start(bf16[1,4,128]{2,1,0:T(4,128)(2,1)} %param.9) | copy-start | bytes 3076
  0.0 10.4 %copy-start.6 = (s32[1,4]{1,0:T(1,128)S(1)}, s32[1,4]{1,0:T(1,128)}, u32[]{:S(2)}) copy-start(s32[1,4]{1,0:T(1,128)} %param.11) | copy-start | bytes 52
  0.0 10.4 %copy-start.5 = (bf16[1,4,128]{2,1,0:T(4,128)(2,1)S(1)}, bf16[1,4,128]{2,1,0:T(4,128)(2,1)}, u32[]{:S(2)}) copy-start(bf16[1,4,128]{2,1,0:T(4,128)(2,1)} %param.10) | copy-start | bytes 3076
  0.0 10.5 %copy-start.3 = (s32[1,4,128]{2,1,0:T(4,128)S(1)}, s32[1,4,128]{2,1,0:T(4,128)}, u32[]{:S(2)}) copy-start(s32[1,4,128]{2,1,0:T(4,128)} %param.12) | copy-start | bytes 6148
  0.0 18.2 %copy-start.1 = (bf16[1,4,256,128]{3,2,1,0:T(8,128)(2,1)S(1)}, bf16[1,4,256,128]{3,2,1,0:T(8,128)(2,1)}, u32[]{:S(2)}) copy-start(bf16[1,4,256,128]{3,2,1,0:T(8,128)(2,1)} %param.8) | copy-start | bytes 786436
  0.0 52.2 %copy-start.2 = (s32[1,4,4]{2,1,0:T(4,128)S(1)}, s32[1,4,4]{2,1,0:T(4,128)}, u32[]{:S(2)}) copy-start(s32[1,4,4]{2,1,0:T(4,128)} %param.13) | copy-start | bytes 196
  1.0 13.2 %collective-permute-start.9 = (bf16[16,4,8,128]{3,2,1,0:T(8,128)(2,1)S(1)}, bf16[16,4,8,128]{3,2,1,0:T(8,128)(2,1)S(1)}, u32[]{:S(2)}, u32[]{:S(2)}) collective-permute-start(bf16[16,4,8,128]{3,2,1,0:T(8,128)(2,1)S(1)} %dynamic-slice_bitcast_fusion), channel_id=1, source_target_pairs={{0,16},{2,18},{4,20},{6,22},{8,24},{10,26},{12,28},{14,30},{16,0},... | collective-permute-start | bytes 393224 | tf_op jit(solution)/shard_map/ppermute | solution.py:272
  5.2 1.6 %copy-start = (bf16[16,1,64,8,128]{4,3,2,1,0:T(8,128)(2,1)S(1)}, bf16[16,1,64,8,128]{4,3,2,1,0:T(8,128)(2,1)}, u32[]{:S(2)}) copy-start(bf16[16,1,64,8,128]{4,3,2,1,0:T(8,128)(2,1)} %param.7) | copy-start | bytes 6291460
  7.3 8.5 %collective-permute-start.2 = (bf16[16,4,8,128]{3,2,1,0:T(8,128)(2,1)S(1)}, bf16[16,4,8,128]{3,2,1,0:T(8,128)(2,1)S(1)}, u32[]{:S(2)}, u32[]{:S(2)}) collective-permute-start(bf16[16,4,8,128]{3,2,1,0:T(8,128)(2,1)S(1)} %get-tuple-element.50), channel_id=1, source_target_pairs={{0,8},{2,10},{4,12},{6,14},{8,0},{10,2},{12,4},{14,6},{16,24},{18,... | collective-permute-start | bytes 393224 | tf_op jit(solution)/shard_map/ppermute | solution.py:272
  8.9 9.2 %collective-permute-start.3 = (bf16[16,4,8,128]{3,2,1,0:T(8,128)(2,1)S(1)}, bf16[16,4,8,128]{3,2,1,0:T(8,128)(2,1)S(1)}, u32[]{:S(2)}, u32[]{:S(2)}) collective-permute-start(bf16[16,4,8,128]{3,2,1,0:T(8,128)(2,1)S(1)} %get-tuple-element.51), channel_id=1, source_target_pairs={{0,10},{2,8},{4,14},{6,12},{8,2},{10,0},{12,6},{14,4},{16,26},{18,... | collective-permute-start | bytes 393224 | tf_op jit(solution)/shard_map/ppermute | solution.py:272
  10.5 2.6 %collective-permute-start.1 = (f32[4,8,128]{2,1,0:T(8,128)S(1)}, f32[4,8,128]{2,1,0:T(8,128)S(1)}, u32[]{:S(2)}, u32[]{:S(2)}) collective-permute-start(f32[4,8,128]{2,1,0:T(8,128)S(1)} %maximum_maximum_fusion.own_aux), channel_id=1, source_target_pairs={{0,1},{1,0},{2,3},{3,2},{4,5},{5,4},{6,7},{7,6},{8,9},{9,8},{10,11... | collective-permute-start | bytes 49160 | tf_op jit(solution)/shard_map/ppermute | solution.py:221
  10.6 10.5 %collective-permute-start.4 = (bf16[16,4,8,128]{3,2,1,0:T(8,128)(2,1)S(1)}, bf16[16,4,8,128]{3,2,1,0:T(8,128)(2,1)S(1)}, u32[]{:S(2)}, u32[]{:S(2)}) collective-permute-start(bf16[16,4,8,128]{3,2,1,0:T(8,128)(2,1)S(1)} %get-tuple-element.52), channel_id=1, source_target_pairs={{0,12},{2,14},{4,8},{6,10},{8,4},{10,6},{12,0},{14,2},{16,28},{18,... | collective-permute-start | bytes 393224 | tf_op jit(solution)/shard_map/ppermute | solution.py:272
  13.2 11.2 %collective-permute-start.5 = (bf16[16,4,8,128]{3,2,1,0:T(8,128)(2,1)S(1)}, bf16[16,4,8,128]{3,2,1,0:T(8,128)(2,1)S(1)}, u32[]{:S(2)}, u32[]{:S(2)}) collective-permute-start(bf16[16,4,8,128]{3,2,1,0:T(8,128)(2,1)S(1)} %get-tuple-element.53), channel_id=1, source_target_pairs={{0,14},{2,12},{4,10},{6,8},{8,6},{10,4},{12,2},{14,0},{16,30},{18,... | collective-permute-start | bytes 393224 | tf_op jit(solution)/shard_map/ppermute | solution.py:272
  14.2 10.1 %collective-permute-start.6 = (bf16[16,4,8,128]{3,2,1,0:T(8,128)(2,1)S(1)}, bf16[16,4,8,128]{3,2,1,0:T(8,128)(2,1)S(1)}, u32[]{:S(2)}, u32[]{:S(2)}) collective-permute-start(bf16[16,4,8,128]{3,2,1,0:T(8,128)(2,1)S(1)} %get-tuple-element.54), channel_id=1, source_target_pairs={{0,2},{2,0},{4,6},{6,4},{8,10},{10,8},{12,14},{14,12},{16,18},{18,... | collective-permute-start | bytes 393224 | tf_op jit(solution)/shard_map/ppermute | solution.py:272
  15.7 13.1 %collective-permute-start.7 = (bf16[16,4,8,128]{3,2,1,0:T(8,128)(2,1)S(1)}, bf16[16,4,8,128]{3,2,1,0:T(8,128)(2,1)S(1)}, u32[]{:S(2)}, u32[]{:S(2)}) collective-permute-start(bf16[16,4,8,128]{3,2,1,0:T(8,128)(2,1)S(1)} %get-tuple-element.55), channel_id=1, source_target_pairs={{0,4},{2,6},{4,0},{6,2},{8,12},{10,14},{12,8},{14,10},{16,20},{18,... | collective-permute-start | bytes 393224 | tf_op jit(solution)/shard_map/ppermute | solution.py:272
  18.2 29.7 %collective-permute-start = (bf16[4,256,128]{2,1,0:T(8,128)(2,1)S(1)}, bf16[4,256,128]{2,1,0:T(8,128)(2,1)S(1)}, u32[]{:S(2)}, u32[]{:S(2)}) collective-permute-start(bf16[4,256,128]{2,1,0:T(8,128)(2,1)S(1)} %bitcast.17), channel_id=1, source_target_pairs={{0,1},{1,0},{2,3},{3,2},{4,5},{5,4},{6,7},{7,6},{8,9},{9,8},{10,11... | collective-permute-start | bytes 786440 | tf_op jit(solution)/shard_map/ppermute | solution.py:221
  21.1 7.8 %collective-permute-start.8 = (bf16[16,4,8,128]{3,2,1,0:T(8,128)(2,1)S(1)}, bf16[16,4,8,128]{3,2,1,0:T(8,128)(2,1)S(1)}, u32[]{:S(2)}, u32[]{:S(2)}) collective-permute-start(bf16[16,4,8,128]{3,2,1,0:T(8,128)(2,1)S(1)} %get-tuple-element.56), channel_id=1, source_target_pairs={{0,6},{2,4},{4,2},{6,0},{8,14},{10,12},{12,10},{14,8},{16,22},{18,... | collective-permute-start | bytes 393224 | tf_op jit(solution)/shard_map/ppermute | solution.py:272
  24.4 16.0 %collective-permute-start.10 = (bf16[16,4,8,128]{3,2,1,0:T(8,128)(2,1)S(1)}, bf16[16,4,8,128]{3,2,1,0:T(8,128)(2,1)S(1)}, u32[]{:S(2)}, u32[]{:S(2)}) collective-permute-start(bf16[16,4,8,128]{3,2,1,0:T(8,128)(2,1)S(1)} %get-tuple-element.57), channel_id=1, source_target_pairs={{0,18},{2,16},{4,22},{6,20},{8,26},{10,24},{12,30},{14,28},{16,2},... | collective-permute-start | bytes 393224 | tf_op jit(solution)/shard_map/ppermute | solution.py:272
  24.4 18.7 %collective-permute-start.11 = (bf16[16,4,8,128]{3,2,1,0:T(8,128)(2,1)S(1)}, bf16[16,4,8,128]{3,2,1,0:T(8,128)(2,1)S(1)}, u32[]{:S(2)}, u32[]{:S(2)}) collective-permute-start(bf16[16,4,8,128]{3,2,1,0:T(8,128)(2,1)S(1)} %get-tuple-element.58), channel_id=1, source_target_pairs={{0,20},{2,22},{4,16},{6,18},{8,28},{10,30},{12,24},{14,26},{16,4},... | collective-permute-start | bytes 393224 | tf_op jit(solution)/shard_map/ppermute | solution.py:272
  28.8 18.0 %collective-permute-start.12 = (bf16[16,4,8,128]{3,2,1,0:T(8,128)(2,1)S(1)}, bf16[16,4,8,128]{3,2,1,0:T(8,128)(2,1)S(1)}, u32[]{:S(2)}, u32[]{:S(2)}) collective-permute-start(bf16[16,4,8,128]{3,2,1,0:T(8,128)(2,1)S(1)} %get-tuple-element.59), channel_id=1, source_target_pairs={{0,22},{2,20},{4,18},{6,16},{8,30},{10,28},{12,26},{14,24},{16,6},... | collective-permute-start | bytes 393224 | tf_op jit(solution)/shard_map/ppermute | solution.py:272
  28.8 34.4 %collective-permute-start.16 = (bf16[16,2,8,128]{3,2,1,0:T(8,128)(2,1)S(1)}, bf16[16,2,8,128]{3,2,1,0:T(8,128)(2,1)S(1)}, u32[]{:S(2)}, u32[]{:S(2)}) collective-permute-start(bf16[16,2,8,128]{3,2,1,0:T(8,128)(2,1)S(1)} %get-tuple-element.65), channel_id=1, source_target_pairs={{0,30},{2,28},{4,26},{6,24},{8,22},{10,20},{12,18},{14,16},{16,14}... | collective-permute-start | bytes 196616 | tf_op jit(solution)/shard_map/ppermute | solution.py:272
  40.3 29.1 %collective-permute-start.17 = (bf16[16,2,8,128]{3,2,1,0:T(8,128)(2,1)S(1)}, bf16[16,2,8,128]{3,2,1,0:T(8,128)(2,1)S(1)}, u32[]{:S(2)}, u32[]{:S(2)}) collective-permute-start(bf16[16,2,8,128]{3,2,1,0:T(8,128)(2,1)S(1)} %get-tuple-element.68), channel_id=1, source_target_pairs={{0,30},{2,28},{4,26},{6,24},{8,22},{10,20},{12,18},{14,16},{16,14}... | collective-permute-start | bytes 196616 | tf_op jit(solution)/shard_map/ppermute | solution.py:272
  43.0 20.2 %collective-permute-start.13 = (bf16[16,4,8,128]{3,2,1,0:T(8,128)(2,1)S(1)}, bf16[16,4,8,128]{3,2,1,0:T(8,128)(2,1)S(1)}, u32[]{:S(2)}, u32[]{:S(2)}) collective-permute-start(bf16[16,4,8,128]{3,2,1,0:T(8,128)(2,1)S(1)} %get-tuple-element.62), channel_id=1, source_target_pairs={{0,24},{2,26},{4,28},{6,30},{8,16},{10,18},{12,20},{14,22},{16,8},... | collective-permute-start | bytes 393224 | tf_op jit(solution)/shard_map/ppermute | solution.py:272
  46.8 16.4 %collective-permute-start.14 = (bf16[16,4,8,128]{3,2,1,0:T(8,128)(2,1)S(1)}, bf16[16,4,8,128]{3,2,1,0:T(8,128)(2,1)S(1)}, u32[]{:S(2)}, u32[]{:S(2)}) collective-permute-start(bf16[16,4,8,128]{3,2,1,0:T(8,128)(2,1)S(1)} %get-tuple-element.63), channel_id=1, source_target_pairs={{0,26},{2,24},{4,30},{6,28},{8,18},{10,16},{12,22},{14,20},{16,10}... | collective-permute-start | bytes 393224 | tf_op jit(solution)/shard_map/ppermute | solution.py:272
  47.9 15.3 %collective-permute-start.15 = (bf16[16,4,8,128]{3,2,1,0:T(8,128)(2,1)S(1)}, bf16[16,4,8,128]{3,2,1,0:T(8,128)(2,1)S(1)}, u32[]{:S(2)}, u32[]{:S(2)}) collective-permute-start(bf16[16,4,8,128]{3,2,1,0:T(8,128)(2,1)S(1)} %get-tuple-element.64), channel_id=1, source_target_pairs={{0,28},{2,30},{4,24},{6,26},{8,20},{10,22},{12,16},{14,18},{16,12}... | collective-permute-start | bytes 393224 | tf_op jit(solution)/shard_map/ppermute | solution.py:272
  63.6 11.6 %collective-permute-start.27 = (bf16[2,8,16,128]{3,2,1,0:T(8,128)(2,1)S(1)}, bf16[2,8,16,128]{3,2,1,0:T(8,128)(2,1)S(1)}, u32[]{:S(2)}, u32[]{:S(2)}) collective-permute-start(bf16[2,8,16,128]{3,2,1,0:T(8,128)(2,1)S(1)} %get-tuple-element.81), channel_id=1, source_target_pairs={{0,16},{2,18},{4,20},{6,22},{8,24},{10,26},{12,28},{14,30},{16,0},... | collective-permute-start | bytes 196616 | tf_op jit(solution)/shard_map/ppermute | solution.py:272
  67.4 8.1 %collective-permute-start.29 = (bf16[2,8,16,128]{3,2,1,0:T(8,128)(2,1)S(1)}, bf16[2,8,16,128]{3,2,1,0:T(8,128)(2,1)S(1)}, u32[]{:S(2)}, u32[]{:S(2)}) collective-permute-start(bf16[2,8,16,128]{3,2,1,0:T(8,128)(2,1)S(1)} %get-tuple-element.83), channel_id=1, source_target_pairs={{0,18},{2,16},{4,22},{6,20},{8,26},{10,24},{12,30},{14,28},{16,2},... | collective-permute-start | bytes 196616 | tf_op jit(solution)/shard_map/ppermute | solution.py:272
  70.5 15.7 %collective-permute-start.23 = (bf16[4,8,16,128]{3,2,1,0:T(8,128)(2,1)S(1)}, bf16[4,8,16,128]{3,2,1,0:T(8,128)(2,1)S(1)}, u32[]{:S(2)}, u32[]{:S(2)}) collective-permute-start(bf16[4,8,16,128]{3,2,1,0:T(8,128)(2,1)S(1)} %get-tuple-element.76), channel_id=1, source_target_pairs={{0,12},{2,14},{4,8},{6,10},{8,4},{10,6},{12,0},{14,2},{16,28},{18,... | collective-permute-start | bytes 393224 | tf_op jit(solution)/shard_map/ppermute | solution.py:272
  72.2 17.4 %collective-permute-start.25 = (bf16[4,8,16,128]{3,2,1,0:T(8,128)(2,1)S(1)}, bf16[4,8,16,128]{3,2,1,0:T(8,128)(2,1)S(1)}, u32[]{:S(2)}, u32[]{:S(2)}) collective-permute-start(bf16[4,8,16,128]{3,2,1,0:T(8,128)(2,1)S(1)} %get-tuple-element.78), channel_id=1, source_target_pairs={{0,14},{2,12},{4,10},{6,8},{8,6},{10,4},{12,2},{14,0},{16,30},{18,... | collective-permute-start | bytes 393224 | tf_op jit(solution)/shard_map/ppermute | solution.py:272
  72.4 17.1 %collective-permute-start.32 = (bf16[4,8,16,128]{3,2,1,0:T(8,128)(2,1)S(1)}, bf16[4,8,16,128]{3,2,1,0:T(8,128)(2,1)S(1)}, u32[]{:S(2)}, u32[]{:S(2)}) collective-permute-start(bf16[4,8,16,128]{3,2,1,0:T(8,128)(2,1)S(1)} %get-tuple-element.86), channel_id=1, source_target_pairs={{0,8},{2,10},{4,12},{6,14},{8,0},{10,2},{12,4},{14,6},{16,24},{18,... | collective-permute-start | bytes 393224 | tf_op jit(solution)/shard_map/ppermute | solution.py:272
  75.1 6.6 %collective-permute-start.28 = (bf16[2,8,16,128]{3,2,1,0:T(8,128)(2,1)S(1)}, bf16[2,8,16,128]{3,2,1,0:T(8,128)(2,1)S(1)}, u32[]{:S(2)}, u32[]{:S(2)}) collective-permute-start(bf16[2,8,16,128]{3,2,1,0:T(8,128)(2,1)S(1)} %get-tuple-element.82), channel_id=1, source_target_pairs={{0,16},{2,18},{4,20},{6,22},{8,24},{10,26},{12,28},{14,30},{16,0},... | collective-permute-start | bytes 196616 | tf_op jit(solution)/shard_map/ppermute | solution.py:272
  75.4 10.5 %collective-permute-start.30 = (bf16[2,8,16,128]{3,2,1,0:T(8,128)(2,1)S(1)}, bf16[2,8,16,128]{3,2,1,0:T(8,128)(2,1)S(1)}, u32[]{:S(2)}, u32[]{:S(2)}) collective-permute-start(bf16[2,8,16,128]{3,2,1,0:T(8,128)(2,1)S(1)} %get-tuple-element.84), channel_id=1, source_target_pairs={{0,18},{2,16},{4,22},{6,20},{8,26},{10,24},{12,30},{14,28},{16,2},... | collective-permute-start | bytes 196616 | tf_op jit(solution)/shard_map/ppermute | solution.py:272
  81.8 12.7 %collective-permute-start.34 = (bf16[4,8,16,128]{3,2,1,0:T(8,128)(2,1)S(1)}, bf16[4,8,16,128]{3,2,1,0:T(8,128)(2,1)S(1)}, u32[]{:S(2)}, u32[]{:S(2)}) collective-permute-start(bf16[4,8,16,128]{3,2,1,0:T(8,128)(2,1)S(1)} %get-tuple-element.88), channel_id=1, source_target_pairs={{0,10},{2,8},{4,14},{6,12},{8,2},{10,0},{12,6},{14,4},{16,26},{18,... | collective-permute-start | bytes 393224 | tf_op jit(solution)/shard_map/ppermute | solution.py:272
  85.9 9.0 %collective-permute-start.22 = (bf16[4,8,16,128]{3,2,1,0:T(8,128)(2,1)S(1)}, bf16[4,8,16,128]{3,2,1,0:T(8,128)(2,1)S(1)}, u32[]{:S(2)}, u32[]{:S(2)}) collective-permute-start(bf16[4,8,16,128]{3,2,1,0:T(8,128)(2,1)S(1)} %get-tuple-element.75), channel_id=1, source_target_pairs={{0,24},{2,26},{4,28},{6,30},{8,16},{10,18},{12,20},{14,22},{16,8},... | collective-permute-start | bytes 393224 | tf_op jit(solution)/shard_map/ppermute | solution.py:272
  86.3 11.0 %collective-permute-start.24 = (bf16[4,8,16,128]{3,2,1,0:T(8,128)(2,1)S(1)}, bf16[4,8,16,128]{3,2,1,0:T(8,128)(2,1)S(1)}, u32[]{:S(2)}, u32[]{:S(2)}) collective-permute-start(bf16[4,8,16,128]{3,2,1,0:T(8,128)(2,1)S(1)} %get-tuple-element.77), channel_id=1, source_target_pairs={{0,26},{2,24},{4,30},{6,28},{8,18},{10,16},{12,22},{14,20},{16,10}... | collective-permute-start | bytes 393224 | tf_op jit(solution)/shard_map/ppermute | solution.py:272
  89.5 21.2 %collective-permute-start.31 = (bf16[4,8,16,128]{3,2,1,0:T(8,128)(2,1)S(1)}, bf16[4,8,16,128]{3,2,1,0:T(8,128)(2,1)S(1)}, u32[]{:S(2)}, u32[]{:S(2)}) collective-permute-start(bf16[4,8,16,128]{3,2,1,0:T(8,128)(2,1)S(1)} %get-tuple-element.85), channel_id=1, source_target_pairs={{0,20},{2,22},{4,16},{6,18},{8,28},{10,30},{12,24},{14,26},{16,4},... | collective-permute-start | bytes 393224 | tf_op jit(solution)/shard_map/ppermute | solution.py:272
  89.6 23.5 %collective-permute-start.33 = (bf16[4,8,16,128]{3,2,1,0:T(8,128)(2,1)S(1)}, bf16[4,8,16,128]{3,2,1,0:T(8,128)(2,1)S(1)}, u32[]{:S(2)}, u32[]{:S(2)}) collective-permute-start(bf16[4,8,16,128]{3,2,1,0:T(8,128)(2,1)S(1)} %get-tuple-element.87), channel_id=1, source_target_pairs={{0,22},{2,20},{4,18},{6,16},{8,30},{10,28},{12,26},{14,24},{16,6},... | collective-permute-start | bytes 393224 | tf_op jit(solution)/shard_map/ppermute | solution.py:272
  94.4 24.4 %collective-permute-start.18 = (bf16[4,8,16,128]{3,2,1,0:T(8,128)(2,1)S(1)}, bf16[4,8,16,128]{3,2,1,0:T(8,128)(2,1)S(1)}, u32[]{:S(2)}, u32[]{:S(2)}) collective-permute-start(bf16[4,8,16,128]{3,2,1,0:T(8,128)(2,1)S(1)} %get-tuple-element.71), channel_id=1, source_target_pairs={{0,2},{2,0},{4,6},{6,4},{8,10},{10,8},{12,14},{14,12},{16,18},{18,... | collective-permute-start | bytes 393224 | tf_op jit(solution)/shard_map/ppermute | solution.py:272
  94.8 24.0 %collective-permute-start.20 = (bf16[4,8,16,128]{3,2,1,0:T(8,128)(2,1)S(1)}, bf16[4,8,16,128]{3,2,1,0:T(8,128)(2,1)S(1)}, u32[]{:S(2)}, u32[]{:S(2)}) collective-permute-start(bf16[4,8,16,128]{3,2,1,0:T(8,128)(2,1)S(1)} %get-tuple-element.73), channel_id=1, source_target_pairs={{0,4},{2,6},{4,0},{6,2},{8,12},{10,14},{12,8},{14,10},{16,20},{18,... | collective-permute-start | bytes 393224 | tf_op jit(solution)/shard_map/ppermute | solution.py:272
  97.3 20.5 %collective-permute-start.26 = (bf16[4,8,16,128]{3,2,1,0:T(8,128)(2,1)S(1)}, bf16[4,8,16,128]{3,2,1,0:T(8,128)(2,1)S(1)}, u32[]{:S(2)}, u32[]{:S(2)}) collective-permute-start(bf16[4,8,16,128]{3,2,1,0:T(8,128)(2,1)S(1)} %get-tuple-element.79), channel_id=1, source_target_pairs={{0,28},{2,30},{4,24},{6,26},{8,20},{10,22},{12,16},{14,18},{16,12}... | collective-permute-start | bytes 393224 | tf_op jit(solution)/shard_map/ppermute | solution.py:272
  110.7 8.1 %collective-permute-start.21 = (bf16[4,8,16,128]{3,2,1,0:T(8,128)(2,1)S(1)}, bf16[4,8,16,128]{3,2,1,0:T(8,128)(2,1)S(1)}, u32[]{:S(2)}, u32[]{:S(2)}) collective-permute-start(bf16[4,8,16,128]{3,2,1,0:T(8,128)(2,1)S(1)} %get-tuple-element.74), channel_id=1, source_target_pairs={{0,6},{2,4},{4,2},{6,0},{8,14},{10,12},{12,10},{14,8},{16,22},{18,... | collective-permute-start | bytes 393224 | tf_op jit(solution)/shard_map/ppermute | solution.py:272
  113.1 8.6 %collective-permute-start.19 = (bf16[4,8,16,128]{3,2,1,0:T(8,128)(2,1)S(1)}, bf16[4,8,16,128]{3,2,1,0:T(8,128)(2,1)S(1)}, u32[]{:S(2)}, u32[]{:S(2)}) collective-permute-start(bf16[4,8,16,128]{3,2,1,0:T(8,128)(2,1)S(1)} %get-tuple-element.72), channel_id=1, source_target_pairs={{0,30},{2,28},{4,26},{6,24},{8,22},{10,20},{12,18},{14,16},{16,14}... | collective-permute-start | bytes 393224 | tf_op jit(solution)/shard_map/ppermute | solution.py:272
